TPU v7x, 32 devices: a whole 2x2x4 slice. The times are simulated.
32 devices in a mesh: dp: 8 (over y, x, core), mp: 4 (over z).
Axes of the slice: x: 2, y: 2, z: 4, core: 2. Of those that a mesh axis runs over, the one named last changes fastest.
Arguments:
- tokens: bfloat16 [768, 32768], P('mp', 'dp'), may hold values from -6 to 6
- bucket: int32 [64], P('dp'), may hold values from 0 to 2
- w_in: bfloat16 [768, 3072], P(None, 'mp'), may hold values from -0.21875 to 0.21875
- b_in: float32 [3072], P('mp'), may hold values from -3 to 3
- w_out: bfloat16 [3072, 768], P('mp'), may hold values from -0.15625 to 0.15625
- b_out: float32 [768], P('mp'), may hold values from -3 to 3
- gain_one: float32 [768], P('mp'), may hold values from 0.1 to 1.9
- shift_one: float32 [768], P('mp'), may hold values from -3 to 3
- gain_two: float32 [768], P('mp'), may hold values from 0.1 to 1.9
- shift_two: float32 [768], P('mp'), may hold values from -4 to 4
- mask: int32 [32768], P('dp'), may hold values from 0 to 1, as said below
- labels: int32 [32768], P('dp'), may hold values from 0 to 767
- cotangent: bfloat16 [768, 32768], P('mp', 'dp'), may hold values from -6 to 6
Outputs:
- output: bfloat16 [768, 32768], P('mp', 'dp')
- d_tokens: float32 [768, 32768], P('mp', 'dp')
- d_w_in: float32 [768, 3072], P(None, 'mp')
- d_b_in: float32 [3072], P('mp')
- d_w_out: float32 [3072, 768], P('mp')
- d_b_out: float32 [768], P('mp')
- d_gain_one: float32 [768], P('mp')
- d_shift_one: float32 [768], P('mp')
- d_gain_two: float32 [768], P('mp')
- d_shift_two: float32 [768], P('mp')
- hits: float32 [], replicated
Inputs may be any that keep to these rules, and one draw needn't show every extreme that they name: `mask`: 1 marks a masked token, 0 an unmasked one. `labels`: a feature index of the model width.
All inputs are finite; a program needn't handle non-finite values.
Results may differ from a plain program's by a relative error of at most 0.0071.
Values may be sent and summed in bfloat16 or wider, within the bound.
A program may use at most 192 MiB of HBM per device.

v0:
```python
import math

import jax
import jax.numpy as jnp
from jax import lax
from jax.sharding import PartitionSpec as P

EPSILON = 1e-05


def seq_tables(bucket, slot_length):
    lengths = slot_length // 4 * jnp.left_shift(jnp.ones_like(bucket), bucket)
    lengths = lengths[:, None, None]
    places = jnp.arange(slot_length, dtype=jnp.int32)
    row_index = places[None, :, None]
    col_index = places[None, None, :]
    together = row_index // lengths == col_index // lengths
    phases = row_index % lengths * (col_index % lengths) % lengths
    length_float = lengths.astype(jnp.float32)
    angles = phases.astype(jnp.float32) * (2.0 * math.pi) / length_float
    scaling = lax.rsqrt(length_float)
    cosine = jnp.where(together, jnp.cos(angles) * scaling, 0.0)
    sine = jnp.where(together, jnp.sin(angles) * scaling, 0.0)
    return (cosine.astype(jnp.bfloat16), sine.astype(jnp.bfloat16))


def hid_tables(first_row, row_count, width):
    row_index = first_row + jnp.arange(row_count, dtype=jnp.int32)[:, None]
    col_index = jnp.arange(width, dtype=jnp.int32)[None, :]
    phases = row_index * col_index % width
    angles = phases.astype(jnp.float32) * (2.0 * math.pi) / width
    scaling = 1.0 / math.sqrt(width)
    return (
        (jnp.cos(angles) * scaling).astype(jnp.bfloat16),
        (jnp.sin(angles) * scaling).astype(jnp.bfloat16),
    )


def gelu_exact(values):
    return jax.nn.gelu(values, approximate=False)


def contract_last(left, right):
    return lax.dot_general(
        left, right, (((1,), (1,)), ((), ())), preferred_element_type=jnp.float32
    )


def contract_first(left, right):
    return lax.dot_general(
        left, right, (((0,), (0,)), ((), ())), preferred_element_type=jnp.float32
    )


def seq_transform(features, cos_seq, sin_seq, slot_count, slot_length):
    blocks = features.reshape(features.shape[0], slot_count, slot_length)
    seq_cos = jnp.einsum(
        "sjk,dsk->dsj", cos_seq, blocks, preferred_element_type=jnp.float32
    ).astype(jnp.bfloat16)
    seq_sin = jnp.einsum(
        "sjk,dsk->dsj", sin_seq, blocks, preferred_element_type=jnp.float32
    ).astype(jnp.bfloat16)
    return (seq_cos.reshape(features.shape[0], -1), seq_sin.reshape(features.shape[0], -1))


def layer_norm(residual, gain, shift):
    width = residual.shape[0] * lax.axis_size("mp")
    totals = lax.psum(jnp.sum(residual, axis=0), "mp")
    centered = residual - (totals / width)[None, :]
    spread = lax.psum(jnp.sum(centered * centered, axis=0), "mp") / width
    inverse = lax.rsqrt(spread + EPSILON)
    normed = centered * inverse[None, :]
    return (normed * gain[:, None] + shift[:, None], normed, inverse)


def norm_back(upstream, normed, inverse, gain):
    width = upstream.shape[0] * lax.axis_size("mp")
    scaled = upstream * gain[:, None]
    first_sum, second_sum = lax.psum(
        (jnp.sum(scaled, axis=0), jnp.sum(scaled * normed, axis=0)), "mp"
    )
    grad_in = inverse[None, :] * (
        scaled - (first_sum / width)[None, :] - normed * (second_sum / width)[None, :]
    )
    return (grad_in, jnp.sum(upstream * normed, axis=1), jnp.sum(upstream, axis=1))


def body(
    tokens,
    bucket,
    w_in,
    b_in,
    w_out,
    b_out,
    gain_one,
    shift_one,
    gain_two,
    shift_two,
    mask,
    labels,
    cotangent,
):
    local_width, token_count = tokens.shape
    slot_count = bucket.shape[0]
    slot_length = token_count // slot_count
    width = local_width * lax.axis_size("mp")
    first_col = lax.axis_index("mp") * local_width
    cos_seq, sin_seq = seq_tables(bucket, slot_length)
    cos_hid, sin_hid = hid_tables(first_col, local_width, width)
    seq_cos, seq_sin = seq_transform(tokens, cos_seq, sin_seq, slot_count, slot_length)
    partial_mix = contract_first(cos_hid, seq_cos) - contract_first(sin_hid, seq_sin)
    mixing = lax.psum_scatter(partial_mix, "mp", scatter_dimension=0, tiled=True)
    first_res = tokens.astype(jnp.float32) + mixing
    hidden_one, normed_one, inverse_one = layer_norm(first_res, gain_one, shift_one)
    hidden_low = hidden_one.astype(jnp.bfloat16)
    piece = lax.all_gather(hidden_low, "mp", axis=0, tiled=True)
    running = contract_first(w_in, piece)
    hidden_full = piece
    activation, gelu_pull = jax.vjp(gelu_exact, running + b_in[:, None])
    act_low = activation.astype(jnp.bfloat16)
    ffn_sum = lax.psum_scatter(
        contract_first(w_out, act_low), "mp", scatter_dimension=0, tiled=True
    )
    second_res = hidden_one + (ffn_sum + b_out[:, None])
    result, normed_two, inverse_two = layer_norm(second_res, gain_two, shift_two)
    label_local = labels - first_col
    chosen = jnp.arange(local_width, dtype=jnp.int32)[:, None] == label_local[None, :]
    chosen = jnp.logical_and(chosen, (mask == 1)[None, :])
    own_hits = jnp.sum(jnp.where(chosen, jax.nn.sigmoid(2.0 * result), 0.0))
    all_hits = lax.psum(own_hits, ("dp", "mp"))
    score = all_hits * 8.0 / (token_count * lax.axis_size("dp"))
    upstream = cotangent.astype(jnp.float32)
    grad_two, d_gain_two, d_shift_two = norm_back(upstream, normed_two, inverse_two, gain_two)
    ffn_grad = grad_two.astype(jnp.bfloat16)
    d_b_out = jnp.sum(ffn_grad.astype(jnp.float32), axis=1)
    piece = lax.all_gather(ffn_grad, "mp", axis=0, tiled=True)
    grad_act = jnp.dot(w_out, piece, preferred_element_type=jnp.float32)
    grad_wout = contract_last(act_low, piece)
    grad_act, d_w_out = (grad_act, grad_wout)
    grad_pre = gelu_pull(grad_act)[0].astype(jnp.bfloat16)
    d_b_in = jnp.sum(grad_pre.astype(jnp.float32), axis=1)
    d_w_in = contract_last(hidden_full, grad_pre)
    back_part = jnp.dot(w_in, grad_pre, preferred_element_type=jnp.float32)
    grad_hidden = grad_two + lax.psum_scatter(back_part, "mp", scatter_dimension=0, tiled=True)
    grad_one, d_gain_one, d_shift_one = norm_back(grad_hidden, normed_one, inverse_one, gain_one)
    mix_grad = grad_one.astype(jnp.bfloat16)
    empty_local = jnp.zeros((local_width, token_count), jnp.float32)
    piece = lax.all_gather(mix_grad, "mp", axis=0, tiled=True)
    grad_sine = empty_local
    grad_cosine = jnp.dot(cos_hid, piece, preferred_element_type=jnp.float32)
    grad_sine = grad_sine - jnp.dot(sin_hid, piece, preferred_element_type=jnp.float32)
    grad_cosine, grad_sine = (grad_cosine, grad_sine)
    grad_cosine = grad_cosine.astype(jnp.bfloat16).reshape(local_width, slot_count, slot_length)
    grad_sine = grad_sine.astype(jnp.bfloat16).reshape(local_width, slot_count, slot_length)
    seq_back = jnp.einsum("skj,dsk->dsj", cos_seq, grad_cosine, preferred_element_type=jnp.float32)
    seq_back = seq_back + jnp.einsum(
        "skj,dsk->dsj", sin_seq, grad_sine, preferred_element_type=jnp.float32
    )
    d_tokens = grad_one + seq_back.reshape(local_width, token_count)
    d_w_in, d_b_in, d_w_out, d_b_out, d_gain_one, d_shift_one, d_gain_two, d_shift_two = lax.psum(
        (d_w_in, d_b_in, d_w_out, d_b_out, d_gain_one, d_shift_one, d_gain_two, d_shift_two), "dp"
    )
    return (
        result.astype(jnp.bfloat16),
        d_tokens,
        d_w_in,
        d_b_in,
        d_w_out,
        d_b_out,
        d_gain_one,
        d_shift_one,
        d_gain_two,
        d_shift_two,
        score,
    )


def solution(mesh):
    in_specs = (
        P("mp", "dp"),
        P("dp"),
        P(None, "mp"),
        P("mp"),
        P("mp", None),
        P("mp"),
        P("mp"),
        P("mp"),
        P("mp"),
        P("mp"),
        P("dp"),
        P("dp"),
        P("mp", "dp"),
    )
    out_specs = (
        P("mp", "dp"),
        P("mp", "dp"),
        P(None, "mp"),
        P("mp"),
        P("mp", None),
        P("mp"),
        P("mp"),
        P("mp"),
        P("mp"),
        P("mp"),
        P(),
    )
    return jax.shard_map(body, mesh=mesh, in_specs=in_specs, out_specs=out_specs, check_vma=False)
```

profile of v0, /device:TPU:0, one launch (start us, length us, event | category | flops | bytes accessed | tf_op | source)
XLA Modules:
  0.0 1696.8 jit_solution(606150039670175843)
XLA Ops:
  7.2 0.8 broadcast_compare_fusion.1
  8.0 0.7 convert_rsqrt_fusion
  8.7 0.7 compare_select_fusion.2
  9.8 113.4 %fusion.64 = bf16[8,24,8,512]{3,2,1,0:T(8,128)(2,1)} fusion(f32[8]{0:T(128)S(1)} %convert_rsqrt_fusion, s32[8,512]{1,0:T(8,128)S(1)} %get-tuple-element.50, f32[8]{0:T(128)S(1)} %get-tuple-element.46, pred[8]{0:T(512)(128)(4,1)S(1)} %broadcast_compare_fusion.1, s32[8]{0:T(128)S(1)} %get-tuple-element.44, s32[8,512]{1,0:T(8,128)S(1)} %get-tuple-element.49, ...), kind=kOutput, calls=%fused_computation.92 | convolution fusion | flops 837550080 | bytes 3178600 | tf_op jit(solution)/shard_map/sjk,dsk->dsj/dot_general | solution.py:60
  123.2 111.1 %fusion.69 = bf16[8,24,8,512]{3,2,1,0:T(8,128)(2,1)S(1)} fusion(f32[8]{0:T(128)S(1)} %convert_rsqrt_fusion, s32[8,512]{1,0:T(8,128)S(1)} %get-tuple-element.50, f32[8]{0:T(128)S(1)} %get-tuple-element.46, pred[8]{0:T(512)(128)(4,1)S(1)} %broadcast_compare_fusion.1, s32[8]{0:T(128)S(1)} %get-tuple-element.44, s32[8,512]{1,0:T(8,128)S(1)} %get-tuple-element.49, ...), kind=kOutput, calls=%fused_computation.93 | convolution fusion | flops 837550080 | bytes 3178600 | tf_op jit(solution)/shard_map/sjk,dsk->dsj/dot_general | solution.py:57
  234.3 1.6 copy.46
  236.1 4.0 fusion.81
  240.1 7.0 convolution_subtract_fusion
  247.2 214.6 %reduce-scatter.4.cloned.1.call-done = f32[192,4096]{1,0:T(8,128)} async-done(((f32[768,4096]{1,0:T(8,128)}), f32[192,4096]{1,0:T(8,128)}) %reduce-scatter.4.cloned.1.call-update) | async-done | bytes 3145744 | tf_op jit(solution)/shard_map/reduce_scatter | solution.py:112
  461.8 4.1 fusion.126
  465.9 18.5 %psum.119 = f32[4096]{0:T(1024)S(1)} all-reduce(f32[4096]{0:T(1024)S(1)} %get-tuple-element.41), channel_id=1, replica_groups=mesh['dp'=8,'mp'=4] {'mp'}, use_global_device_ids=true, to_apply=%region_2.3 | all-reduce | flops 4096 | bytes 32768 | tf_op jit(solution)/shard_map/psum | solution.py:68
  484.3 2.2 multiply_reduce_fusion.3
  486.6 15.5 psum.120
  502.2 3.6 fusion.48
  505.9 114.2 %all-gather.4.cloned.1.call-done = bf16[768,4096]{1,0:T(8,128)(2,1)} async-done(((bf16[192,4096]{1,0:T(8,128)(2,1)}), bf16[768,4096]{1,0:T(8,128)(2,1)}) %all-gather.4.cloned.1.call-update) | async-done | bytes 6291472 | tf_op jit(solution)/shard_map/all_gather | solution.py:116
  620.0 34.9 %fusion.9 = (bf16[768,4096]{0,1:T(8,128)(2,1)S(1)}, f32[768,4096]{0,1:T(8,128)}, f32[4096,768]{1,0:T(8,128)}) fusion(f32[768]{0:T(1024)S(1)} %copy-done.27, bf16[768,4096]{1,0:T(8,128)(2,1)} %all-gather.4.cloned.1.call-done, bf16[768,768]{1,0:T(8,128)(2,1)S(1)} %copy-done), kind=kOutput, calls=%fused_computation.17 | convolution fusion | flops 5039456256 | bytes 38931456 | tf_op jit(solution)/shard_map/dot_general | solution.py:50
  654.9 2.6 copy-done.30
  657.5 7.9 convolution_bitcast_fusion.1
  665.4 0.6 copy-done.8
  666.1 209.5 %reduce-scatter.6.cloned.1.call-done = f32[192,4096]{1,0:T(8,128)} async-done(((f32[768,4096]{1,0:T(8,128)}), f32[192,4096]{1,0:T(8,128)}) %reduce-scatter.6.cloned.1.call-update) | async-done | bytes 3145744 | tf_op jit(solution)/shard_map/reduce_scatter | solution.py:121
  875.6 5.5 fusion.124
  881.1 18.5 %psum.121 = f32[4096]{0:T(1024)S(1)} all-reduce(f32[4096]{0:T(1024)S(1)} %get-tuple-element.37), channel_id=1, replica_groups=mesh['dp'=8,'mp'=4] {'mp'}, use_global_device_ids=true, to_apply=%region_7.8 | all-reduce | flops 4096 | bytes 32768 | tf_op jit(solution)/shard_map/psum | solution.py:68
  899.6 2.2 multiply_reduce_fusion.2
  901.9 15.6 psum.122
  917.5 6.0 fusion.38
  923.5 17.0 %all-reduce.3 = (f32[4096]{0:T(1024)S(1)}, f32[4096]{0:T(1024)S(1)}) all-reduce(f32[4096]{0:T(1024)S(1)} %get-tuple-element.14, f32[4096]{0:T(1024)S(1)} %get-tuple-element.18), channel_id=1, replica_groups=mesh['dp'=8,'mp'=4] {'mp'}, use_global_device_ids=true, to_apply=%region_13.14 | all-reduce | flops 8192 | bytes 65536 | tf_op jit(solution)/shard_map/psum | solution.py:79
  940.6 4.4 convert_reduce_fusion.2
  945.0 114.3 %all-gather.6.cloned.1.call-done = bf16[768,4096]{1,0:T(8,128)(2,1)} async-done(((bf16[192,4096]{1,0:T(8,128)(2,1)}), bf16[768,4096]{1,0:T(8,128)(2,1)}) %all-gather.6.cloned.1.call-update) | async-done | bytes 6291472 | tf_op jit(solution)/shard_map/all_gather | solution.py:136
  1059.3 19.6 %convert_reduce_fusion = (f32[768]{0:T(1024)S(1)}, bf16[768,4096]{0,1:T(8,128)(2,1)}) fusion(f32[768,4096]{0,1:T(8,128)} %get-tuple-element.40, f32[4096,768]{1,0:T(8,128)} %get-tuple-element.48, f32[768]{0:T(1024)S(1)} %copy-done.27, bf16[768,4096]{1,0:T(8,128)(2,1)} %all-gather.6.cloned.1.call-done, bf16[768,768]{1,0:T(8,128)(2,1)} %param.17), kind=kOutput, calls=%fused_computation.18 | convolution fusion | flops 4885314560 | bytes 38934528 | tf_op jit(solution)/shard_map/dot_general | solution.py:137
  1078.9 10.7 convolution_bitcast_fusion
  1089.7 210.2 %reduce-scatter.8.cloned.1.call-done = f32[192,4096]{1,0:T(8,128)} async-done(((f32[768,4096]{1,0:T(8,128)}), f32[192,4096]{1,0:T(8,128)}) %reduce-scatter.8.cloned.1.call-update) | async-done | bytes 3145744 | tf_op jit(solution)/shard_map/reduce_scatter | solution.py:144
  1299.9 6.2 multiply_reduce_fusion
  1306.1 18.8 %all-reduce.2 = (f32[4096]{0:T(1024)S(1)}, f32[4096]{0:T(1024)S(1)}) all-reduce(f32[4096]{0:T(1024)S(1)} %get-tuple-element.12, f32[4096]{0:T(1024)S(1)} %get-tuple-element.16), channel_id=1, replica_groups=mesh['dp'=8,'mp'=4] {'mp'}, use_global_device_ids=true, to_apply=%region_18.19 | all-reduce | flops 8192 | bytes 65536 | tf_op jit(solution)/shard_map/psum | solution.py:79
  1324.9 4.8 fusion.120
  1329.7 47.5 %psum.135 = f32[]{:T(128)} all-reduce(f32[]{:T(128)} %get-tuple-element.15), channel_id=1, replica_groups=mesh['dp'=8,'mp'=4] {'dp','mp'}, use_global_device_ids=true, to_apply=%region_34.35 | all-reduce | flops 1 | bytes 8 | tf_op jit(solution)/shard_map/psum | solution.py:130
  1377.8 10.2 fusion.128
  1388.0 10.0 fusion.127
  1398.1 14.8 all-reduce
  1412.9 31.7 %all-gather.8.cloned.1.call-done = bf16[768,4096]{1,0:T(8,128)(2,1)} async-done(((bf16[192,4096]{1,0:T(8,128)(2,1)}), bf16[768,4096]{1,0:T(8,128)(2,1)}) %all-gather.8.cloned.1.call-update) | async-done | bytes 6291472 | tf_op jit(solution)/shard_map/all_gather | solution.py:148
  1444.6 6.6 fusion.31
  1451.2 111.5 %fusion.40 = f32[8,192,512]{2,1,0:T(8,128)S(1)} fusion(f32[8]{0:T(128)S(1)} %copy-done.29, s32[8,512]{1,0:T(8,128)S(1)} %copy-done.13, f32[8]{0:T(128)S(1)} %copy-done.25, pred[8]{0:T(512)(128)(4,1)S(1)} %copy-done.23, s32[8]{0:T(128)S(1)} %copy-done.19, s32[8,512]{1,0:T(8,128)S(1)} %copy-done.11, bf16[24,8,8,512]{3,2,1,0:T(8,128)(2,1)S(1)} %bitcast.148), kind=kOutput, calls=%fused_computation.77 | convolution fusion | flops 836763648 | bytes 4751464 | tf_op jit(solution)/shard_map/skj,dsk->dsj/dot_general | solution.py:156
  1562.7 4.6 convolution_convert_fusion
  1567.3 111.0 %add_bitcast_fusion = f32[8,24,8,512]{3,2,1,0:T(8,128)S(1)} fusion(f32[8,192,512]{2,1,0:T(8,128)S(1)} %fusion.40, f32[8]{0:T(128)S(1)} %copy-done.29, s32[8,512]{1,0:T(8,128)S(1)} %copy-done.13, f32[8]{0:T(128)S(1)} %copy-done.25, pred[8]{0:T(512)(128)(4,1)S(1)} %copy-done.23, s32[8]{0:T(128)S(1)} %copy-done.19, s32[8,512]{1,0:T(8,128)S(1)} %copy-done.11, ...), kind=kOutput, calls=%fused_computation.65 | convolution fusion | flops 837550080 | bytes 7897192 | tf_op jit(solution)/shard_map/skj,dsk->dsj/dot_general | solution.py:155
  1678.6 1.5 copy-done.1
  1680.1 1.0 copy-done.2
  1681.1 2.7 fusion.119
  1683.8 3.4 copy.70
  1687.2 1.4 copy.71
  (93 shorter events, 1.6 us)
Async XLA Ops:
  7.2 612.9 %copy-start = (bf16[768,768]{1,0:T(8,128)(2,1)S(1)}, bf16[768,768]{1,0:T(8,128)(2,1)}, u32[]{:S(2)}) copy-start(bf16[768,768]{1,0:T(8,128)(2,1)} %param.15) | copy-start | bytes 3538948
  7.2 454.6 %reduce-scatter.4.cloned.1.call-start = ((), (), s32[]{:S(2)}) async-start(), calls=%async_computation.3 | async-start | bytes 15728640 | tf_op jit(solution)/shard_map/reduce_scatter | solution.py:112
  8.0 115.2 %copy-start.22 = (pred[8]{0:T(512)(128)(4,1)}, pred[8]{0:T(512)(128)(4,1)S(1)}, u32[]{:S(2)}) copy-start(pred[8]{0:T(512)(128)(4,1)S(1)} %broadcast_compare_fusion.1) | copy-start | bytes 28
  8.7 114.5 %copy-start.28 = (f32[8]{0:T(128)}, f32[8]{0:T(128)S(1)}, u32[]{:S(2)}) copy-start(f32[8]{0:T(128)S(1)} %convert_rsqrt_fusion) | copy-start | bytes 100
  9.3 113.9 %copy-start.18 = (s32[8]{0:T(128)}, s32[8]{0:T(128)S(1)}, u32[]{:S(2)}) copy-start(s32[8]{0:T(128)S(1)} %get-tuple-element.44) | copy-start | bytes 100
  9.3 113.9 %copy-start.24 = (f32[8]{0:T(128)}, f32[8]{0:T(128)S(1)}, u32[]{:S(2)}) copy-start(f32[8]{0:T(128)S(1)} %get-tuple-element.46) | copy-start | bytes 100
  9.8 113.4 %copy-start.10 = (s32[8,512]{1,0:T(8,128)}, s32[8,512]{1,0:T(8,128)S(1)}, u32[]{:S(2)}) copy-start(s32[8,512]{1,0:T(8,128)S(1)} %get-tuple-element.49) | copy-start | bytes 49156
  9.8 113.4 %copy-start.12 = (s32[8,512]{1,0:T(8,128)}, s32[8,512]{1,0:T(8,128)S(1)}, u32[]{:S(2)}) copy-start(s32[8,512]{1,0:T(8,128)S(1)} %get-tuple-element.50) | copy-start | bytes 49156
  9.8 113.4 %copy-start.5 = (bf16[192,4096]{1,0:T(8,128)(2,1)S(1)}, bf16[192,4096]{1,0:T(8,128)(2,1)}, u32[]{:S(2)}) copy-start(bf16[192,4096]{1,0:T(8,128)(2,1)} %param.13) | copy-start | bytes 4718596
  234.3 5.8 copy-start.14
  247.1 214.7 %copy-start.6 = (bf16[192,4096]{1,0:T(8,128)(2,1)S(1)}, bf16[192,4096]{1,0:T(8,128)(2,1)}, u32[]{:S(2)}) copy-start(bf16[192,4096]{1,0:T(8,128)(2,1)} %param.13) | copy-start | bytes 4718596
  247.1 255.1 %copy-start.7 = (f32[192]{0:T(256)S(1)}, f32[192]{0:T(256)}, u32[]{:S(2)}) copy-start(f32[192]{0:T(256)} %param.19) | copy-start | bytes 2308
  247.1 255.1 %copy-start.17 = (f32[192]{0:T(256)S(1)}, f32[192]{0:T(256)}, u32[]{:S(2)}) copy-start(f32[192]{0:T(256)} %param.20) | copy-start | bytes 2308
  247.1 372.9 %all-gather.4.cloned.1.call-start = ((), (), s32[]{:S(2)}) async-start(), calls=%async_computation.4 | async-start | bytes 7864320 | tf_op jit(solution)/shard_map/all_gather | solution.py:116
  484.3 135.7 %copy-start.27 = (f32[768]{0:T(1024)S(1)}, f32[768]{0:T(1024)}, u32[]{:S(2)}) copy-start(f32[768]{0:T(1024)} %param.16) | copy-start | bytes 9220
  505.8 151.7 %copy-start.26 = (bf16[768,768]{1,0:T(8,128)(2,1)S(1)}, bf16[768,768]{1,0:T(8,128)(2,1)}, u32[]{:S(2)}) copy-start(bf16[768,768]{1,0:T(8,128)(2,1)} %param.17) | copy-start | bytes 3538948
  505.8 369.8 %reduce-scatter.6.cloned.1.call-start = ((), (), s32[]{:S(2)}) async-start(), calls=%async_computation.5 | async-start | bytes 15728640 | tf_op jit(solution)/shard_map/reduce_scatter | solution.py:121
  654.9 2.6 copy-start.30
  665.4 0.7 copy-start.8
  665.4 0.7 copy-start.9
  665.4 210.3 %copy-start.20 = (f32[192]{0:T(256)S(1)}, f32[192]{0:T(256)}, u32[]{:S(2)}) copy-start(f32[192]{0:T(256)} %param.18) | copy-start | bytes 2308
  665.4 393.9 %all-gather.6.cloned.1.call-start = ((), (), s32[]{:S(2)}) async-start(), calls=%async_computation.6 | async-start | bytes 7864320 | tf_op jit(solution)/shard_map/all_gather | solution.py:136
  666.1 251.3 %copy-start.3 = (bf16[192,4096]{1,0:T(8,128)(2,1)S(1)}, bf16[192,4096]{1,0:T(8,128)(2,1)}, u32[]{:S(2)}) copy-start(bf16[192,4096]{1,0:T(8,128)(2,1)} %param.25) | copy-start | bytes 4718596
  666.1 251.3 %copy-start.16 = (f32[192]{0:T(256)S(1)}, f32[192]{0:T(256)}, u32[]{:S(2)}) copy-start(f32[192]{0:T(256)} %param.21) | copy-start | bytes 2308
  666.1 251.3 %copy-start.21 = (f32[192]{0:T(256)S(1)}, f32[192]{0:T(256)}, u32[]{:S(2)}) copy-start(f32[192]{0:T(256)} %param.22) | copy-start | bytes 2308
  945.0 355.0 %reduce-scatter.8.cloned.1.call-start = ((), (), s32[]{:S(2)}) async-start(), calls=%async_computation.7 | async-start | bytes 15728640 | tf_op jit(solution)/shard_map/reduce_scatter | solution.py:144
  1089.7 354.9 %all-gather.8.cloned.1.call-start = ((), (), s32[]{:S(2)}) async-start(), calls=%async_computation.8 | async-start | bytes 7864320 | tf_op jit(solution)/shard_map/all_gather | solution.py:148
  1329.7 354.1 %all-reduce.6.cloned.1.call-start = ((), (), s32[]{:S(2)}) async-start(), calls=%async_computation.9 | async-start | bytes 9437184 | tf_op jit(solution)/shard_map/psum | solution.py:160
  1398.0 46.5 %copy-start.15 = (s32[192]{0:T(256)S(1)}, s32[192]{0:T(256)}, u32[]{:S(2)}) copy-start(s32[192]{0:T(256)} %copy-done.14) | copy-start | bytes 2308
  1412.8 38.3 %copy-start.11 = (s32[8,512]{1,0:T(8,128)S(1)}, s32[8,512]{1,0:T(8,128)}, u32[]{:S(2)}) copy-start(s32[8,512]{1,0:T(8,128)} %copy-done.10) | copy-start | bytes 49156
  1412.8 38.3 %copy-start.13 = (s32[8,512]{1,0:T(8,128)S(1)}, s32[8,512]{1,0:T(8,128)}, u32[]{:S(2)}) copy-start(s32[8,512]{1,0:T(8,128)} %copy-done.12) | copy-start | bytes 49156
  1412.8 38.3 %copy-start.19 = (s32[8]{0:T(128)S(1)}, s32[8]{0:T(128)}, u32[]{:S(2)}) copy-start(s32[8]{0:T(128)} %copy-done.18) | copy-start | bytes 100
  1412.8 38.3 %copy-start.23 = (pred[8]{0:T(512)(128)(4,1)S(1)}, pred[8]{0:T(512)(128)(4,1)}, u32[]{:S(2)}) copy-start(pred[8]{0:T(512)(128)(4,1)} %copy-done.22) | copy-start | bytes 28
  1412.9 38.3 %copy-start.25 = (f32[8]{0:T(128)S(1)}, f32[8]{0:T(128)}, u32[]{:S(2)}) copy-start(f32[8]{0:T(128)} %copy-done.24) | copy-start | bytes 100
  1412.9 38.3 %copy-start.29 = (f32[8]{0:T(128)S(1)}, f32[8]{0:T(128)}, u32[]{:S(2)}) copy-start(f32[8]{0:T(128)} %copy-done.28) | copy-start | bytes 100
  1444.6 118.1 %slice-start = ((s8[6291456]{0:T(1024)(128)(4,1)}), s8[4194304]{0:T(1024)(128)(4,1)S(1)}, s32[]{:S(2)}) async-start(s8[6291456]{0:T(1024)(128)(4,1)} %bitcast.145), calls=%async_computation.10 | async-start | bytes 8388608
  1451.2 111.5 %slice-start.1 = ((s8[6291456]{0:T(1024)(128)(4,1)}), s8[2097152]{0:T(1024)(128)(4,1)S(1)}, s32[]{:S(2)}) async-start(s8[6291456]{0:T(1024)(128)(4,1)} %bitcast.145), calls=%async_computation.11 | async-start | bytes 4194304
  1678.2 1.9 copy-start.1
  1678.2 2.8 copy-start.2
  1683.8 3.4 copy-start.4
Sparse Core Ops, SparseCore 0:
  247.2 214.5 reduce-scatter.3
  505.9 114.0 all-gather.3
  665.5 210.0 reduce-scatter.5
  945.1 114.1 all-gather.5
  1089.8 210.0 reduce-scatter.7
  1329.8 114.7 all-gather.7
  1448.5 85.3 all-reduce.5
where the time goes:
time: 1710 us; the launch traced here: 1700 us
  waiting for transfers between devices  895 us (52%)
  matrix products  562 us (33%)
  blocking collectives  166 us (10%)
  other arithmetic  44.3 us (3%)
    reduce_scatter x1, waiting for transfers between devices, body(): lax.psum_scatter(partial_mix, 'mp', scatter_dimension=0, tiled=True)  215 us
    reduce_scatter x1, waiting for transfers between devices, body(): lax.psum_scatter(back_part, 'mp', scatter_dimension=0, tiled=True)  210 us
    reduce_scatter x1, waiting for transfers between devices, body(): lax.psum_scatter(contract_first(w_out, act_low), 'mp', scatter_dimension=...  209 us
    all_gather x1, waiting for transfers between devices, body(): piece = lax.all_gather(ffn_grad, 'mp', axis=0, tiled=True)  114 us
    all_gather x1, waiting for transfers between devices, body(): piece = lax.all_gather(hidden_low, 'mp', axis=0, tiled=True)  114 us
    dot_general x1, matrix products, seq_transform(): jnp.einsum('sjk,dsk->dsj', sin_seq, blocks, preferred_element_type=jnp.fl...  113 us
    dot_general x1, matrix products, body(): jnp.einsum('skj,dsk->dsj', sin_seq, grad_sine, preferred_element_type=jnp...  111 us
    dot_general x1, matrix products, seq_transform(): jnp.einsum('sjk,dsk->dsj', cos_seq, blocks, preferred_element_type=jnp.fl...  111 us
  transfers between devices with their start and end apart: 7, of which 6 were waited for; matrix products, arithmetic and copies ran while one was open for 15% of the time, Pallas kernels for 0%

commit v1 on v0

v1 whole, which is shorter than its diff:
```python
import math

import jax
import jax.numpy as jnp
import numpy as np
from jax import lax
from jax.sharding import PartitionSpec as P

EPSILON = 1e-05


def dft_pair(length):
    places = np.arange(length)
    angles = (places[:, None] * places[None, :] % length) * (2.0 * math.pi / length)
    scale = 1.0 / math.sqrt(length)
    return (np.cos(angles) * scale).astype(np.float32), (np.sin(angles) * scale).astype(np.float32)


def seq_tables(slot_length):
    cosines, sines = [], []
    for bucket in range(3):
        length = slot_length // 4 << bucket
        cosine, sine = dft_pair(length)
        copies = np.eye(slot_length // length, dtype=np.float32)
        cosines.append(np.kron(copies, cosine))
        sines.append(np.kron(copies, sine))
    return (
        jnp.asarray(np.stack(cosines), jnp.bfloat16),
        jnp.asarray(np.stack(sines), jnp.bfloat16),
    )


def dot(left, right, left_dim, right_dim):
    return lax.dot_general(
        left,
        right,
        (((left_dim,), (right_dim,)), ((), ())),
        preferred_element_type=jnp.float32,
    )


def shift_pairs(shards, step):
    return [(i, (i + step) % shards) for i in range(shards)]


def to_tokens(local, me, shards):
    width, tokens = local.shape
    chunk = tokens // shards
    whole = jnp.zeros((width * shards, chunk), local.dtype)
    for step in range(shards):
        target = (me + step) % shards
        piece = lax.dynamic_slice(local, (0, target * chunk), (width, chunk))
        if step:
            piece = lax.ppermute(piece, "mp", shift_pairs(shards, step))
        source = (me - step) % shards
        whole = lax.dynamic_update_slice(whole, piece, (source * width, 0))
    return whole


def to_features(whole, me, shards):
    full, chunk = whole.shape
    width = full // shards
    local = jnp.zeros((width, chunk * shards), whole.dtype)
    for step in range(shards):
        target = (me + step) % shards
        piece = lax.dynamic_slice(whole, (target * width, 0), (width, chunk))
        if step:
            piece = lax.ppermute(piece, "mp", shift_pairs(shards, step))
        source = (me - step) % shards
        local = lax.dynamic_update_slice(local, piece, (0, source * chunk))
    return local


def norm(residual, gain, shift):
    means = jnp.mean(residual, axis=0)
    centered = residual - means[None, :]
    inverse = lax.rsqrt(jnp.mean(centered * centered, axis=0) + EPSILON)
    normed = centered * inverse[None, :]
    return normed * gain[:, None] + shift[:, None], normed, inverse


def norm_back(upstream, normed, inverse, gain):
    scaled = upstream * gain[:, None]
    first = jnp.mean(scaled, axis=0)
    second = jnp.mean(scaled * normed, axis=0)
    grad = inverse[None, :] * (scaled - first[None, :] - normed * second[None, :])
    return grad, jnp.sum(upstream * normed, axis=1), jnp.sum(upstream, axis=1)


def gelu_exact(values):
    return jax.nn.gelu(values, approximate=False)


def body(
    tokens,
    bucket,
    w_in,
    b_in,
    w_out,
    b_out,
    gain_one,
    shift_one,
    gain_two,
    shift_two,
    mask,
    labels,
    cotangent,
):
    shards = lax.axis_size("mp")
    groups = lax.axis_size("dp")
    me = lax.axis_index("mp")
    mine = lax.axis_index("dp")
    local_width, token_count = tokens.shape
    width = local_width * shards
    units = w_in.shape[1]
    chunk = token_count // shards
    slot_length = token_count // bucket.shape[0]
    slots = chunk // slot_length

    small = jnp.concatenate([b_in, b_out, gain_one, shift_one, gain_two, shift_two])
    small = lax.all_gather(small, "mp")
    b_in_all = small[:, :units].reshape(-1)
    b_out, gain_one, shift_one, gain_two, shift_two = [
        small[:, units + i * local_width : units + (i + 1) * local_width].reshape(-1)
        for i in range(5)
    ]

    x_low = to_tokens(tokens, me, shards)
    cot_in, x_low = lax.optimization_barrier((cotangent, x_low))

    pair = jnp.concatenate([w_in, w_out.T], axis=0)
    part = pair.shape[0] // groups
    own = lax.dynamic_slice(pair, (mine * part, 0), (part, units))
    own = lax.all_gather(own, "mp")
    pair_all = lax.all_gather(own, "dp")

    cos_tables, sin_tables = seq_tables(slot_length)
    my_buckets = lax.dynamic_slice(bucket, (me * slots,), (slots,))
    cos_hid, sin_hid = (jnp.asarray(t, jnp.bfloat16) for t in dft_pair(width))

    seq_cos, seq_sin, tables = [], [], []
    for slot in range(slots):
        cosine = lax.dynamic_index_in_dim(cos_tables, my_buckets[slot], 0, False)
        sine = lax.dynamic_index_in_dim(sin_tables, my_buckets[slot], 0, False)
        cosine, sine = lax.optimization_barrier((cosine, sine))
        tables.append((cosine, sine))
        block = x_low[:, slot * slot_length : (slot + 1) * slot_length]
        seq_cos.append(dot(block, cosine, 1, 0).astype(jnp.bfloat16))
        seq_sin.append(dot(block, sine, 1, 0).astype(jnp.bfloat16))
    seq_cos = jnp.concatenate(seq_cos, axis=1)
    seq_sin = jnp.concatenate(seq_sin, axis=1)
    mixing = dot(cos_hid, seq_cos, 0, 0) - dot(sin_hid, seq_sin, 0, 0)
    first_res = x_low.astype(jnp.float32) + mixing
    hidden_one, normed_one, inverse_one = norm(first_res, gain_one, shift_one)
    hidden_low = hidden_one.astype(jnp.bfloat16)

    pair_all = pair_all.transpose(1, 0, 2, 3).reshape(shards, 2, width, units)
    win_all = pair_all[:, 0]
    wout_all = pair_all[:, 1]
    acts, pulls = [], []
    ffn_out = b_out[:, None]
    for s in range(shards):
        pre = dot(win_all[s], hidden_low, 0, 0) + b_in_all[s * units : (s + 1) * units, None]
        act, pull = jax.vjp(gelu_exact, pre)
        act = act.astype(jnp.bfloat16)
        acts.append(act)
        pulls.append(pull)
        ffn_out = ffn_out + dot(wout_all[s], act, 1, 0)
    second_res = hidden_one + ffn_out
    result, normed_two, inverse_two = norm(second_res, gain_two, shift_two)

    my_labels = lax.dynamic_slice(labels, (me * chunk,), (chunk,))
    my_mask = lax.dynamic_slice(mask, (me * chunk,), (chunk,))
    chosen = jnp.arange(width, dtype=jnp.int32)[:, None] == my_labels[None, :]
    picked = jnp.sum(jnp.where(chosen, result, 0.0), axis=0)
    own_hits = jnp.sum(jnp.where(my_mask == 1, jax.nn.sigmoid(2.0 * picked), 0.0))

    cot_low = to_tokens(cot_in, me, shards)
    upstream = cot_low.astype(jnp.float32)
    grad_two, d_gain_two, d_shift_two = norm_back(upstream, normed_two, inverse_two, gain_two)
    ffn_grad = grad_two.astype(jnp.bfloat16)
    d_b_out = jnp.sum(ffn_grad.astype(jnp.float32), axis=1)
    out_low, ffn_grad = lax.optimization_barrier((result.astype(jnp.bfloat16), ffn_grad))
    output = to_features(out_low, me, shards)

    grad_hidden = grad_two
    d_b_in, d_w_in, d_w_out = [], [], []
    for s in range(shards):
        grad_act = dot(wout_all[s], ffn_grad, 0, 0)
        grad_pre = pulls[s](grad_act)[0].astype(jnp.bfloat16)
        d_b_in.append(jnp.sum(grad_pre.astype(jnp.float32), axis=1))
        d_w_out.append(dot(acts[s], ffn_grad, 1, 1))
        d_w_in.append(dot(hidden_low, grad_pre, 1, 1))
        grad_hidden = grad_hidden + dot(win_all[s], grad_pre, 1, 0)
    grad_one, d_gain_one, d_shift_one = norm_back(grad_hidden, normed_one, inverse_one, gain_one)
    mix_grad = grad_one.astype(jnp.bfloat16)
    grad_cos = dot(cos_hid, mix_grad, 0, 0).astype(jnp.bfloat16)
    grad_sin = -dot(sin_hid, mix_grad, 0, 0).astype(jnp.bfloat16)
    back = []
    for slot in range(slots):
        cosine, sine = tables[slot]
        columns = slice(slot * slot_length, (slot + 1) * slot_length)
        back.append(dot(grad_cos[:, columns], cosine, 1, 0) + dot(grad_sin[:, columns], sine, 1, 0))
    d_x = (grad_one + jnp.concatenate(back, axis=1)).astype(jnp.bfloat16)
    d_tokens = to_features(d_x, me, shards).astype(jnp.float32)

    grads = jnp.concatenate([jnp.stack(d_w_in), jnp.stack(d_w_out)], axis=1)
    grads = lax.psum_scatter(grads.astype(jnp.bfloat16), "dp", scatter_dimension=1, tiled=True)
    grads = lax.psum_scatter(grads.astype(jnp.float32), "mp", scatter_dimension=0, tiled=True)
    grads = lax.all_gather(grads[0], "dp", axis=0, tiled=True)
    d_w_in = grads[:width]
    d_w_out = grads[width:]

    sums = jnp.concatenate(
        d_b_in + [d_b_out, d_gain_one, d_shift_one, d_gain_two, d_shift_two, own_hits[None]]
    )
    sums = lax.psum(sums, ("dp", "mp"))
    d_b_in = lax.dynamic_slice(sums, (me * units,), (units,))
    rest = [
        lax.dynamic_slice(sums, (shards * units + i * width + me * local_width,), (local_width,))
        for i in range(5)
    ]
    score = sums[-1] * 8.0 / (token_count * groups)
    return (output, d_tokens, d_w_in, d_b_in, d_w_out, *rest, score)


def solution(mesh):
    in_specs = (
        P("mp", "dp"),
        P("dp"),
        P(None, "mp"),
        P("mp"),
        P("mp", None),
        P("mp"),
        P("mp"),
        P("mp"),
        P("mp"),
        P("mp"),
        P("dp"),
        P("dp"),
        P("mp", "dp"),
    )
    out_specs = (
        P("mp", "dp"),
        P("mp", "dp"),
        P(None, "mp"),
        P("mp"),
        P("mp", None),
        P("mp"),
        P("mp"),
        P("mp"),
        P("mp"),
        P("mp"),
        P(),
    )
    return jax.shard_map(body, mesh=mesh, in_specs=in_specs, out_specs=out_specs, check_vma=False)
```

time: 1710 us -> 532 us (0.31)
  the two profiles are of different devices: /device:TPU:0 before, /device:TPU:9 now
where the time goes in v1:
time: 532 us; the launch traced here: 524 us
  waiting for transfers between devices  198 us (37%)
  matrix products  112 us (21%)
  blocking collectives  83 us (16%)
  local copies, waits for them, and re-layouts  69.2 us (13%)
  other arithmetic  24 us (5%)
  between operations  21.4 us (4%)
  starting transfers between devices  16 us (3%)
    dot_general x36, matrix products, dot(): lax.dot_general(left, right, (((left_dim,), (right_dim,)), ((), ())), pre...  112 us
    reduce_scatter x1, waiting for transfers between devices, body(): lax.psum_scatter(grads.astype(jnp.bfloat16), 'dp', scatter_dimension=1, t...  75.9 us
    reduce_scatter x1, waiting for transfers between devices, body(): lax.psum_scatter(grads.astype(jnp.float32), 'mp', scatter_dimension=0, ti...  45.4 us
    psum x1, blocking collectives, body(): sums = lax.psum(sums, ('dp', 'mp'))  44.9 us
    unnamed x1, blocking collectives  38.2 us
    all_gather x1, waiting for transfers between devices, body(): own = lax.all_gather(own, 'mp')  30.2 us
    ppermute x6, waiting for transfers between devices, to_tokens(): piece = lax.ppermute(piece, 'mp', shift_pairs(shards, step))  26.5 us
    unnamed x141, local copies, waits for them, and re-layouts  23.4 us
  transfers between devices with their start and end apart: 17, of which 7 were waited for; matrix products, arithmetic and copies ran while one was open for 15% of the time, Pallas kernels for 0%

profile of v1, /device:TPU:9, one launch (start us, length us, event | category | flops | bytes accessed | tf_op | source)
XLA Modules:
  0.0 523.5 jit_solution(3051413069576430154)
XLA Ops:
  7.2 1.6 copy.39
  8.8 2.0 fusion.77
  10.9 30.2 %all-gather.8.cloned.1.call-done = bf16[768,768]{1,0:T(8,128)(2,1)} async-done(((bf16[192,768]{1,0:T(8,128)(2,1)}), bf16[768,768]{1,0:T(8,128)(2,1)}) %all-gather.8.cloned.1.call-update) | async-done | bytes 1179664 | tf_op jit(solution)/shard_map/all_gather | solution.py:134
  43.5 1.4 collective-permute-start.1
  48.0 38.2 %all-reduce = f32[6912]{0:T(1024)S(1)} all-reduce(f32[6912]{0:T(1024)S(1)} %dynamic-update-slice), channel_id=2, replica_groups=mesh['dp'=8,'mp'=4] {'mp'}, use_global_device_ids=true, to_apply=%add | all-reduce | flops 6912 | bytes 55296
  92.1 2.5 dynamic-slice_bitcast_fusion.2
  98.1 1.5 slice_reduce_fusion
  105.0 1.8 collective-permute-start.3
  109.4 1.5 fusion.34
  110.9 1.6 fusion.88
  112.9 2.6 collective-permute-start.4
  116.9 23.7 %collective-permute-done.4 = bf16[192,1024]{1,0:T(8,128)(2,1)S(1)} collective-permute-done((bf16[192,1024]{1,0:T(8,128)(2,1)S(1)}, bf16[192,1024]{1,0:T(8,128)(2,1)S(1)}, u32[]{:S(2)}, u32[]{:S(2)}) %collective-permute-start.4) | collective-permute-done | bytes 393248 | tf_op jit(solution)/shard_map/ppermute | solution.py:54
  141.4 2.8 collective-permute-done.5
  145.0 8.3 %copy.40 = bf16[4,8,192,768]{3,2,1,0:T(8,128)(2,1)} copy(bf16[4,8,192,768]{3,2,0,1:T(8,128)(2,1)} %bitcast.165) | data formatting | bytes 18874368 | tf_op jit(solution)/shard_map/transpose | solution.py:157
  153.3 11.2 %multiply_convert_fusion.3 = (bf16[768,1024]{1,0:T(8,128)(2,1)S(1)}, f32[768,1024]{1,0:T(8,128)}, f32[768,1024]{1,0:T(8,128)}) fusion(f32[768]{0:T(1024)S(1)} %copy-done.41, bf16[768,1024]{1,0:T(8,128)(2,1)S(1)} %fusion.32, bf16[4,2,768,768]{3,2,1,0:T(8,128)(2,1)} %bitcast.149), kind=kOutput, calls=%fused_computation.79 | convolution fusion | flops 1259864064 | bytes 10619904 | tf_op jit(solution)/shard_map/dot_general | solution.py:34
  166.0 9.5 %multiply_convert_fusion.2 = (bf16[768,1024]{1,0:T(8,128)(2,1)S(1)}, f32[768,1024]{1,0:T(8,128)}, f32[768,1024]{1,0:T(8,128)}) fusion(f32[768]{0:T(1024)S(1)} %copy-done.40, bf16[768,1024]{1,0:T(8,128)(2,1)S(1)} %fusion.32, bf16[4,2,768,768]{3,2,1,0:T(8,128)(2,1)S(1)} %bitcast.155), kind=kOutput, calls=%fused_computation.66 | convolution fusion | flops 1259864064 | bytes 10620928 | tf_op jit(solution)/shard_map/dot_general | solution.py:34
  176.9 24.8 %multiply_convert_fusion.1 = (bf16[768,1024]{1,0:T(8,128)(2,1)S(1)}, f32[768,1024]{1,0:T(8,128)}, f32[768,1024]{1,0:T(8,128)}) fusion(f32[768]{0:T(1024)S(1)} %get-tuple-element.37, bf16[768,1024]{1,0:T(8,128)(2,1)S(1)} %fusion.32, bf16[4,2,768,768]{3,2,1,0:T(8,128)(2,1)S(1)} %bitcast.157), kind=kOutput, calls=%fused_computation.53 | convolution fusion | flops 1259864064 | bytes 10620928 | tf_op jit(solution)/shard_map/dot_general | solution.py:34
  203.1 9.5 %multiply_convert_fusion = (bf16[768,1024]{1,0:T(8,128)(2,1)S(1)}, f32[768,1024]{1,0:T(8,128)}, f32[768,1024]{1,0:T(8,128)}) fusion(f32[768]{0:T(1024)S(1)} %get-tuple-element.36, bf16[768,1024]{1,0:T(8,128)(2,1)S(1)} %copy-done.20, bf16[4,2,768,768]{3,2,1,0:T(8,128)(2,1)S(1)} %bitcast.159), kind=kOutput, calls=%fused_computation.40 | convolution fusion | flops 1259864064 | bytes 10620928 | tf_op jit(solution)/shard_map/dot_general | solution.py:34
  212.6 2.1 fusion.89
  215.5 4.6 fusion.10
  220.1 2.7 convert_reduce_fusion.1
  222.8 1.4 fusion.46
  225.7 1.4 fusion.48
  227.2 1.4 fusion.49
  230.0 3.5 convert_reduce_fusion.5
  236.9 3.5 convert_reduce_fusion.4
  243.8 3.5 convert_reduce_fusion.3
  250.7 3.5 convert_reduce_fusion.2
  255.6 5.7 %maximum_maximum_fusion = bf16[4,1536,768]{2,1,0:T(8,128)(2,1)} fusion(bf16[1,768,768]{2,1,0:T(8,128)(2,1)S(1)} %fusion.49, bf16[1,768,768]{2,1,0:T(8,128)(2,1)S(1)} %fusion.48, bf16[1,768,768]{2,1,0:T(8,128)(2,1)S(1)} %fusion.47, bf16[1,768,768]{2,1,0:T(8,128)(2,1)S(1)} %fusion.46, bf16[1,768,768]{2,1,0:T(8,128)(2,1)S(1)} %fusion.45, ...), kind=kLoop, calls=%fused_computation | loop fusion | flops 75497472 | bytes 18874368 | tf_op jit(solution)/shard_map/concatenate | solution.py:207
  261.4 75.9 %reduce-scatter.3.cloned.1.call-done = bf16[4,192,768]{2,1,0:T(8,128)(2,1)} async-done(((bf16[4,1536,768]{2,1,0:T(8,128)(2,1)}), bf16[4,192,768]{2,1,0:T(8,128)(2,1)}) %reduce-scatter.3.cloned.1.call-update) | async-done | bytes 1179664 | tf_op jit(solution)/shard_map/reduce_scatter | solution.py:208
  337.3 2.9 convert_element_type.112
  340.7 45.4 %reduce-scatter.5.cloned.1.call-done = f32[1,192,768]{2,1,0:T(8,128)} async-done(((f32[4,192,768]{2,1,0:T(8,128)}), f32[1,192,768]{2,1,0:T(8,128)}) %reduce-scatter.5.cloned.1.call-update) | async-done | bytes 589840 | tf_op jit(solution)/shard_map/reduce_scatter | solution.py:209
  386.2 3.3 fusion.52
  389.4 2.8 fusion.56
  392.3 2.8 fusion.60
  395.1 5.4 %multiply_reduce_fusion = (f32[768]{0:T(1024)S(1)}, f32[1024]{0:T(1024)S(1)}, f32[1024]{0:T(1024)S(1)}, f32[768]{0:T(1024)S(1)}, f32[768,1024]{1,0:T(8,128)S(1)}) fusion(f32[768,1024]{1,0:T(8,128)S(1)} %copy-done.1, f32[1024]{0:T(1024)S(1)} %copy-done.29, f32[1024]{0:T(1024)S(1)} %copy-done.24, f32[768]{0:T(1024)S(1)} %copy-done.27, ...), kind=kOutput, calls=%fused_computation.24 | convolution fusion | flops 1224471040 | bytes 23244800 | tf_op jit(solution)/shard_map/dot_general | solution.py:34
  401.8 1.4 fusion.41
  404.6 1.5 negate_bitcast_fusion
  409.9 3.4 collective-permute-start.9
  415.9 1.5 collective-permute-start.6
  430.3 1.9 constant_dynamic-update-slice_fusion.12
  432.2 44.9 %psum.7 = f32[6913]{0:T(1024)} all-reduce(f32[6913]{0:T(1024)} %constant_dynamic-update-slice_fusion.12), channel_id=1, replica_groups=mesh['dp'=8,'mp'=4] {'dp','mp'}, use_global_device_ids=true, to_apply=%region_21.22 | all-reduce | flops 6913 | bytes 55304 | tf_op jit(solution)/shard_map/psum | solution.py:217
  477.1 1.5 fusion.85
  481.1 2.1 collective-permute-start.7
  487.1 2.0 convert_element_type.111
  490.2 18.5 %collective-permute-done.7 = bf16[192,1024]{1,0:T(8,128)(2,1)S(1)} collective-permute-done((bf16[192,1024]{1,0:T(8,128)(2,1)}, bf16[192,1024]{1,0:T(8,128)(2,1)S(1)}, u32[]{:S(2)}, u32[]{:S(2)}) %collective-permute-start.7) | collective-permute-done | bytes 393248 | tf_op jit(solution)/shard_map/ppermute | solution.py:68
  508.7 1.5 collective-permute-done.8
  510.3 5.4 %slice_bitcast_fusion = (f32[768,768]{1,0:T(8,128)}, f32[768,768]{1,0:T(8,128)}) fusion(f32[1,1536,768]{2,1,0:T(8,128)} %all-gather.12.cloned.1.call-done), kind=kLoop, calls=%fused_computation.103 | loop fusion | bytes 9437184 | tf_op jit(solution)/shard_map/slice | solution.py:212
  (231 shorter events, 70.2 us)
Async XLA Ops:
  7.2 33.9 %all-gather.8.cloned.1.call-start = ((), (), s32[]{:S(2)}) async-start(), calls=%async_computation.4 | async-start | bytes 1474560 | tf_op jit(solution)/shard_map/all_gather | solution.py:134
  8.8 32.6 %copy-start.16 = (bf16[192,4096]{1,0:T(8,128)(2,1)S(1)}, bf16[192,4096]{1,0:T(8,128)(2,1)}, u32[]{:S(2)}) copy-start(bf16[192,4096]{1,0:T(8,128)(2,1)} %param.17) | copy-start | bytes 4718596
  10.8 36.1 %copy-start.35 = (f32[768]{0:T(1024)S(1)}, f32[768]{0:T(1024)}, u32[]{:S(2)}) copy-start(f32[768]{0:T(1024)} %param.20) | copy-start | bytes 9220
  10.8 36.1 %copy-start.46 = (f32[192]{0:T(256)S(1)}, f32[192]{0:T(256)}, u32[]{:S(2)}) copy-start(f32[192]{0:T(256)} %param.22) | copy-start | bytes 2308
  10.8 36.1 %copy-start.47 = (f32[192]{0:T(256)S(1)}, f32[192]{0:T(256)}, u32[]{:S(2)}) copy-start(f32[192]{0:T(256)} %param.23) | copy-start | bytes 2308
  10.8 36.1 %copy-start.48 = (f32[192]{0:T(256)S(1)}, f32[192]{0:T(256)}, u32[]{:S(2)}) copy-start(f32[192]{0:T(256)} %param.24) | copy-start | bytes 2308
  10.8 134.2 %all-gather.10.cloned.1.call-start = ((), (), s32[]{:S(2)}) async-start(), calls=%async_computation.5 | async-start | bytes 10616832 | tf_op jit(solution)/shard_map/all_gather | solution.py:135
  41.1 296.2 %reduce-scatter.3.cloned.1.call-start = ((), (), s32[]{:S(2)}) async-start(), calls=%async_computation.2 | async-start | bytes 10616832 | tf_op jit(solution)/shard_map/reduce_scatter | solution.py:208
  42.5 57.1 %collective-permute-start = (bf16[192,1024]{1,0:T(8,128)(2,1)}, bf16[192,1024]{1,0:T(8,128)(2,1)}, u32[]{:S(2)}, u32[]{:S(2)}) collective-permute-start(bf16[192,1024]{1,0:T(8,128)(2,1)} %get-tuple-element.70), channel_id=1, source_target_pairs={{0,1},{1,2},{2,3},{3,0},{4,5},{5,6},{6,7},{7,4},{8,9},{9,10},{10,1... | collective-permute-start | bytes 1179656 | tf_op jit(solution)/shard_map/ppermute | solution.py:54
  43.5 57.1 %collective-permute-start.1 = (bf16[192,1024]{1,0:T(8,128)(2,1)}, bf16[192,1024]{1,0:T(8,128)(2,1)}, u32[]{:S(2)}, u32[]{:S(2)}) collective-permute-start(bf16[192,1024]{1,0:T(8,128)(2,1)} %get-tuple-element.72), channel_id=1, source_target_pairs={{0,2},{1,3},{2,0},{3,1},{4,6},{5,7},{6,4},{7,5},{8,10},{9,11},{10,... | collective-permute-start | bytes 1179656 | tf_op jit(solution)/shard_map/ppermute | solution.py:54
  45.0 56.7 %collective-permute-start.2 = (bf16[192,1024]{1,0:T(8,128)(2,1)S(1)}, bf16[192,1024]{1,0:T(8,128)(2,1)}, u32[]{:S(2)}, u32[]{:S(2)}) collective-permute-start(bf16[192,1024]{1,0:T(8,128)(2,1)S(1)} %get-tuple-element.69), channel_id=1, source_target_pairs={{0,3},{1,0},{2,1},{3,2},{4,7},{5,4},{6,5},{7,6},{8,11},{9,8},{10,9... | collective-permute-start | bytes 1179656 | tf_op jit(solution)/shard_map/ppermute | solution.py:54
  86.2 5.2 copy-start.25
  94.6 12.3 %copy-start.10 = (bf16[512,512]{1,0:T(8,128)(2,1)}, bf16[512,512]{1,0:T(8,128)(2,1)S(1)}, u32[]{:S(2)}) copy-start(bf16[512,512]{1,0:T(8,128)(2,1)S(1)} %get-tuple-element.21) | copy-start | bytes 1572868
  94.6 13.6 %copy-start.6 = (bf16[512,512]{1,0:T(8,128)(2,1)}, bf16[512,512]{1,0:T(8,128)(2,1)S(1)}, u32[]{:S(2)}) copy-start(bf16[512,512]{1,0:T(8,128)(2,1)S(1)} %get-tuple-element.23) | copy-start | bytes 1572868
  94.6 14.2 %copy-start.8 = (bf16[512,512]{1,0:T(8,128)(2,1)}, bf16[512,512]{1,0:T(8,128)(2,1)S(1)}, u32[]{:S(2)}) copy-start(bf16[512,512]{1,0:T(8,128)(2,1)S(1)} %get-tuple-element.22) | copy-start | bytes 1572868
  94.6 20.9 %copy-start.26 = (f32[768]{0:T(1024)}, f32[768]{0:T(1024)S(1)}, u32[]{:S(2)}) copy-start(f32[768]{0:T(1024)S(1)} %mul.301) | copy-start | bytes 9220
  95.4 20.1 %copy-start.31 = (f32[768]{0:T(1024)}, f32[768]{0:T(1024)S(1)}, u32[]{:S(2)}) copy-start(f32[768]{0:T(1024)S(1)} %add.327) | copy-start | bytes 9220
  98.1 6.0 %copy-start.17 = (bf16[192,4096]{1,0:T(8,128)(2,1)S(1)}, bf16[192,4096]{1,0:T(8,128)(2,1)}, u32[]{:S(2)}) copy-start(bf16[192,4096]{1,0:T(8,128)(2,1)} %param.29) | copy-start | bytes 4718596
  99.6 77.3 %copy-start.38 = (f32[768]{0:T(1024)}, f32[768]{0:T(1024)S(1)}, u32[]{:S(2)}) copy-start(f32[768]{0:T(1024)S(1)} %get-tuple-element.37) | copy-start | bytes 9220
  99.6 103.4 %copy-start.36 = (f32[768]{0:T(1024)}, f32[768]{0:T(1024)S(1)}, u32[]{:S(2)}) copy-start(f32[768]{0:T(1024)S(1)} %get-tuple-element.36) | copy-start | bytes 9220
  105.0 11.1 %collective-permute-start.3 = (bf16[192,1024]{1,0:T(8,128)(2,1)S(1)}, bf16[192,1024]{1,0:T(8,128)(2,1)S(1)}, u32[]{:S(2)}, u32[]{:S(2)}) collective-permute-start(bf16[192,1024]{1,0:T(8,128)(2,1)S(1)} %get-tuple-element.63), channel_id=1, source_target_pairs={{0,1},{1,2},{2,3},{3,0},{4,5},{5,6},{6,7},{7,4},{8,9},{9,10},{10,1... | collective-permute-start | bytes 1179656 | tf_op jit(solution)/shard_map/ppermute | solution.py:54
  112.9 28.5 %copy-start.28 = (f32[1024]{0:T(1024)}, f32[1024]{0:T(1024)S(1)}, u32[]{:S(2)}) copy-start(f32[1024]{0:T(1024)S(1)} %add_rsqrt_fusion.1) | copy-start | bytes 12292
  112.9 27.8 %collective-permute-start.4 = (bf16[192,1024]{1,0:T(8,128)(2,1)S(1)}, bf16[192,1024]{1,0:T(8,128)(2,1)S(1)}, u32[]{:S(2)}, u32[]{:S(2)}) collective-permute-start(bf16[192,1024]{1,0:T(8,128)(2,1)S(1)} %get-tuple-element.62), channel_id=1, source_target_pairs={{0,2},{1,3},{2,0},{3,1},{4,6},{5,7},{6,4},{7,5},{8,10},{9,11},{10,... | collective-permute-start | bytes 1179656 | tf_op jit(solution)/shard_map/ppermute | solution.py:54
  115.5 28.7 %collective-permute-start.5 = (bf16[192,1024]{1,0:T(8,128)(2,1)S(1)}, bf16[192,1024]{1,0:T(8,128)(2,1)S(1)}, u32[]{:S(2)}, u32[]{:S(2)}) collective-permute-start(bf16[192,1024]{1,0:T(8,128)(2,1)S(1)} %get-tuple-element.61), channel_id=1, source_target_pairs={{0,3},{1,0},{2,1},{3,2},{4,7},{5,4},{6,5},{7,6},{8,11},{9,8},{10,9... | collective-permute-start | bytes 1179656 | tf_op jit(solution)/shard_map/ppermute | solution.py:54
  116.0 60.8 %copy-start.19 = (bf16[768,1024]{1,0:T(8,128)(2,1)}, bf16[768,1024]{1,0:T(8,128)(2,1)S(1)}, u32[]{:S(2)}) copy-start(bf16[768,1024]{1,0:T(8,128)(2,1)S(1)} %fusion.32) | copy-start | bytes 4718596
  145.0 8.3 %copy-start.41 = (f32[768]{0:T(1024)S(1)}, f32[768]{0:T(1024)}, u32[]{:S(2)}) copy-start(f32[768]{0:T(1024)} %get-tuple-element.39) | copy-start | bytes 9220
  153.3 11.2 %copy-start.4 = (bf16[4,8,192,768]{3,2,1,0:T(8,128)(2,1)S(1)}, bf16[4,8,192,768]{3,2,1,0:T(8,128)(2,1)}, u32[]{:S(2)}) copy-start(bf16[4,8,192,768]{3,2,1,0:T(8,128)(2,1)} %copy.40) | copy-start | bytes 28311556
  203.1 9.5 %copy-start.1 = (f32[768,1024]{1,0:T(8,128)S(1)}, f32[768,1024]{1,0:T(8,128)}, u32[]{:S(2)}) copy-start(f32[768,1024]{1,0:T(8,128)} %copy-done) | copy-start | bytes 9437188
  203.1 9.5 %copy-start.24 = (f32[1024]{0:T(1024)S(1)}, f32[1024]{0:T(1024)}, u32[]{:S(2)}) copy-start(f32[1024]{0:T(1024)} %copy-done.23) | copy-start | bytes 12292
  203.1 9.5 %copy-start.27 = (f32[768]{0:T(1024)S(1)}, f32[768]{0:T(1024)}, u32[]{:S(2)}) copy-start(f32[768]{0:T(1024)} %copy-done.26) | copy-start | bytes 9220
  203.1 9.5 %copy-start.29 = (f32[1024]{0:T(1024)S(1)}, f32[1024]{0:T(1024)}, u32[]{:S(2)}) copy-start(f32[1024]{0:T(1024)} %copy-done.28) | copy-start | bytes 12292
  203.1 9.5 %copy-start.32 = (f32[768]{0:T(1024)S(1)}, f32[768]{0:T(1024)}, u32[]{:S(2)}) copy-start(f32[768]{0:T(1024)} %copy-done.31) | copy-start | bytes 9220
  203.1 9.5 %copy-start.34 = (f32[768]{0:T(1024)S(1)}, f32[768]{0:T(1024)}, u32[]{:S(2)}) copy-start(f32[768]{0:T(1024)} %add.330) | copy-start | bytes 9220
  214.8 5.3 %copy-start.2 = (f32[768,1024]{1,0:T(8,128)}, f32[768,1024]{1,0:T(8,128)S(1)}, u32[]{:S(2)}) copy-start(f32[768,1024]{1,0:T(8,128)S(1)} %get-tuple-element.92) | copy-start | bytes 9437188
  261.3 124.7 %reduce-scatter.5.cloned.1.call-start = ((), (), s32[]{:S(2)}) async-start(), calls=%async_computation.3 | async-start | bytes 2949120 | tf_op jit(solution)/shard_map/reduce_scatter | solution.py:209
  340.2 170.0 %all-gather.12.cloned.1.call-start = ((), (), s32[]{:S(2)}) async-start(), calls=%async_computation.6 | async-start | bytes 5308416 | tf_op jit(solution)/shard_map/all_gather | solution.py:210
  408.5 6.4 %copy-start.5 = (bf16[768,1024]{1,0:T(8,128)(2,1)S(1)}, bf16[768,1024]{1,0:T(8,128)(2,1)}, u32[]{:S(2)}) copy-start(bf16[768,1024]{1,0:T(8,128)(2,1)} %get-tuple-element.25) | copy-start | bytes 4718596
  409.9 7.4 %copy-start.42 = (f32[768]{0:T(1024)S(1)}, f32[768]{0:T(1024)}, u32[]{:S(2)}) copy-start(f32[768]{0:T(1024)} %get-tuple-element.94) | copy-start | bytes 9220
  409.9 8.7 %copy-start.43 = (f32[768]{0:T(1024)S(1)}, f32[768]{0:T(1024)}, u32[]{:S(2)}) copy-start(f32[768]{0:T(1024)} %get-tuple-element.96) | copy-start | bytes 9220
  409.9 10.0 %copy-start.44 = (f32[768]{0:T(1024)S(1)}, f32[768]{0:T(1024)}, u32[]{:S(2)}) copy-start(f32[768]{0:T(1024)} %get-tuple-element.98) | copy-start | bytes 9220
  409.9 11.3 %copy-start.45 = (f32[768]{0:T(1024)S(1)}, f32[768]{0:T(1024)}, u32[]{:S(2)}) copy-start(f32[768]{0:T(1024)} %get-tuple-element.100) | copy-start | bytes 9220
  409.9 74.0 %collective-permute-start.9 = (bf16[192,1024]{1,0:T(8,128)(2,1)}, bf16[192,1024]{1,0:T(8,128)(2,1)}, u32[]{:S(2)}, u32[]{:S(2)}) collective-permute-start(bf16[192,1024]{1,0:T(8,128)(2,1)} %get-tuple-element.55), channel_id=1, source_target_pairs={{0,1},{1,2},{2,3},{3,0},{4,5},{5,6},{6,7},{7,4},{8,9},{9,10},{10,1... | collective-permute-start | bytes 1179656 | tf_op jit(solution)/shard_map/ppermute | solution.py:68
  413.3 71.7 %collective-permute-start.10 = (bf16[192,1024]{1,0:T(8,128)(2,1)}, bf16[192,1024]{1,0:T(8,128)(2,1)}, u32[]{:S(2)}, u32[]{:S(2)}) collective-permute-start(bf16[192,1024]{1,0:T(8,128)(2,1)} %get-tuple-element.54), channel_id=1, source_target_pairs={{0,2},{1,3},{2,0},{3,1},{4,6},{5,7},{6,4},{7,5},{8,10},{9,11},{10,... | collective-permute-start | bytes 1179656 | tf_op jit(solution)/shard_map/ppermute | solution.py:68
  414.7 71.4 %collective-permute-start.11 = (bf16[192,1024]{1,0:T(8,128)(2,1)}, bf16[192,1024]{1,0:T(8,128)(2,1)}, u32[]{:S(2)}, u32[]{:S(2)}) collective-permute-start(bf16[192,1024]{1,0:T(8,128)(2,1)} %get-tuple-element.53), channel_id=1, source_target_pairs={{0,3},{1,0},{2,1},{3,2},{4,7},{5,4},{6,5},{7,6},{8,11},{9,8},{10,9... | collective-permute-start | bytes 1179656 | tf_op jit(solution)/shard_map/ppermute | solution.py:68
  415.9 73.2 %collective-permute-start.6 = (bf16[192,1024]{1,0:T(8,128)(2,1)}, bf16[192,1024]{1,0:T(8,128)(2,1)}, u32[]{:S(2)}, u32[]{:S(2)}) collective-permute-start(bf16[192,1024]{1,0:T(8,128)(2,1)} %get-tuple-element.59), channel_id=1, source_target_pairs={{0,1},{1,2},{2,3},{3,0},{4,5},{5,6},{6,7},{7,4},{8,9},{9,10},{10,1... | collective-permute-start | bytes 1179656 | tf_op jit(solution)/shard_map/ppermute | solution.py:68
  481.1 27.5 %collective-permute-start.7 = (bf16[192,1024]{1,0:T(8,128)(2,1)}, bf16[192,1024]{1,0:T(8,128)(2,1)S(1)}, u32[]{:S(2)}, u32[]{:S(2)}) collective-permute-start(bf16[192,1024]{1,0:T(8,128)(2,1)} %get-tuple-element.58), channel_id=1, source_target_pairs={{0,2},{1,3},{2,0},{3,1},{4,6},{5,7},{6,4},{7,5},{8,10},{9,11},{10,... | collective-permute-start | bytes 1179656 | tf_op jit(solution)/shard_map/ppermute | solution.py:68
  483.9 26.2 %collective-permute-start.8 = (bf16[192,1024]{1,0:T(8,128)(2,1)S(1)}, bf16[192,1024]{1,0:T(8,128)(2,1)S(1)}, u32[]{:S(2)}, u32[]{:S(2)}) collective-permute-start(bf16[192,1024]{1,0:T(8,128)(2,1)S(1)} %get-tuple-element.57), channel_id=1, source_target_pairs={{0,3},{1,0},{2,1},{3,2},{4,7},{5,4},{6,5},{7,6},{8,11},{9,8},{10,9... | collective-permute-start | bytes 1179656 | tf_op jit(solution)/shard_map/ppermute | solution.py:68
  510.2 5.5 %copy-start.18 = (bf16[192,4096]{1,0:T(8,128)(2,1)}, bf16[192,4096]{1,0:T(8,128)(2,1)S(1)}, u32[]{:S(2)}) copy-start(bf16[192,4096]{1,0:T(8,128)(2,1)S(1)} %constant_dynamic-update-slice_fusion.3) | copy-start | bytes 4718596
  (34 other events, 71.5 us)
Sparse Core Ops, SparseCore 0:
  10.9 30.0 all-gather.7
  43.0 59.0 all-gather.9
  261.5 75.8 reduce-scatter.2
  340.3 45.6 reduce-scatter.4
  387.8 41.1 all-gather.11

commit v2 on v0

v2 whole, which is shorter than its diff:
```python
import functools
import math

import jax
import jax.numpy as jnp
import numpy as np
from jax import lax
from jax.experimental import pallas as pl
from jax.experimental.pallas import tpu as pltpu
from jax.sharding import PartitionSpec as P

EPSILON = 1e-05
BF = jnp.bfloat16
F32 = jnp.float32
ANY = pl.BlockSpec(memory_space=pl.ANY)
VMEM = pl.BlockSpec(memory_space=pltpu.VMEM)
SMEM = pl.BlockSpec(memory_space=pltpu.SMEM)
VMEM_LIMIT = 66_000_000


def dft_pair(length):
    places = np.arange(length)
    angles = (places[:, None] * places[None, :] % length) * (2.0 * math.pi / length)
    scale = 1.0 / math.sqrt(length)
    return (np.cos(angles) * scale).astype(np.float32), (np.sin(angles) * scale).astype(np.float32)


def seq_tables(slot_length):
    cosines, sines = [], []
    for bucket in range(3):
        length = slot_length // 4 << bucket
        cosine, sine = dft_pair(length)
        copies = np.eye(slot_length // length, dtype=np.float32)
        cosines.append(np.kron(copies, cosine))
        sines.append(np.kron(copies, sine))
    return jnp.asarray(np.stack(cosines), BF), jnp.asarray(np.stack(sines), BF)


def dot(left, right, left_dim=1, right_dim=0):
    return lax.dot_general(
        left, right, (((left_dim,), (right_dim,)), ((), ())), preferred_element_type=F32
    )


def remote(source, target, send_sem, recv_sem, device):
    return pltpu.make_async_remote_copy(
        src_ref=source,
        dst_ref=target,
        send_sem=send_sem,
        recv_sem=recv_sem,
        device_id=device,
        device_id_type=pl.DeviceIdType.MESH,
    )


def greet(peers):
    barrier = pltpu.get_barrier_semaphore()
    for peer in peers:
        pl.semaphore_signal(barrier, inc=1, device_id=peer, device_id_type=pl.DeviceIdType.MESH)
    pl.semaphore_wait(barrier, len(peers))


def lanes(values):
    return sum(values[:, i : i + 128] for i in range(128, values.shape[1], 128)) + values[:, :128]


def layer_kernel(
    shards,
    groups,
    tok,
    cot,
    w_in,
    w_out,
    small,
    bucket,
    labels,
    mask,
    cos_seq,
    sin_seq,
    cos_hid,
    sin_hid,
    out,
    dx,
    d_w,
    sums,
    x_all,
    c_all,
    w_all,
    small_all,
    cos_tab,
    sin_tab,
    cos_h,
    sin_h,
    n_one,
    inv_one,
    hid,
    act,
    slope,
    n_two,
    inv_two,
    grad,
    seq_c,
    seq_s,
    vecs,
    bias,
    acc,
    bias_acc,
    hits,
    stage,
    load_sem,
    own_sem,
    tok_send,
    tok_recv,
    cot_send,
    cot_recv,
    small_send,
    small_recv,
    wz_send,
    wz_recv,
    wp_send,
    wp_recv,
    ws_send,
    ws_recv,
    out_send,
    out_recv,
    dx_send,
    dx_recv,
    stage_sem,
):
    me = lax.axis_index("mp")
    group = lax.axis_index("dp")
    width_local = tok.shape[0]
    width = width_local * shards
    units = w_in.shape[1]
    chunk = tok.shape[1] // shards
    slot_length = cos_seq.shape[1]
    slots = chunk // slot_length
    part = 2 * width // groups
    chips = groups // 2
    rows = min(256, width)
    cols = min(256, slot_length)
    ring = range(1, shards)
    others = range(1, chips)

    def mp_peer(step):
        return lax.rem(me + step, shards)

    def dp_peer(step):
        return lax.rem(group + 2 * step, groups)

    sibling = {"dp": group + 1 - 2 * lax.rem(group, 2)}
    greet(
        [{"mp": mp_peer(d)} for d in ring] + [{"dp": dp_peer(k)} for k in others] + [sibling]
    )

    own_w = [
        pltpu.make_async_copy(w_in, w_all.at[0, :width], own_sem.at[0]),
        pltpu.make_async_copy(w_out, w_all.at[0, width:], own_sem.at[1]),
    ]
    my_cols = pl.ds(pl.multiple_of(me * chunk, 128), chunk)
    my_rows = pl.ds(pl.multiple_of(me * width_local, 16), width_local)
    loads = [
        pltpu.make_async_copy(source, target, load_sem.at[i])
        for i, (source, target) in enumerate(
            [
                (small, small_all.at[0]),
                (cos_seq, cos_tab),
                (sin_seq, sin_tab),
                (cos_hid, cos_h),
                (sin_hid, sin_h),
                (tok.at[:, my_cols], x_all.at[my_rows]),
                (cot.at[:, my_cols], c_all.at[my_rows]),
            ]
        )
    ]
    for copy in own_w + loads:
        copy.start()

    def exchange(source, target, send, recv):
        copies = []
        for d in ring:
            peer = mp_peer(d)
            copies.append(
                remote(
                    source.at[:, pl.ds(pl.multiple_of(peer * chunk, 128), chunk)],
                    target.at[my_rows],
                    send.at[d],
                    recv.at[d],
                    {"mp": peer},
                )
            )
        return copies

    small_copies = [
        remote(
            small,
            small_all.at[shards - d],
            small_send.at[d],
            small_recv.at[d],
            {"mp": mp_peer(d)},
        )
        for d in ring
    ]
    for copy in small_copies:
        copy.start()
    for copy in own_w:
        copy.wait()
    my_part = pl.ds(pl.multiple_of(group * part, 16), part)
    wz = [
        remote(
            w_all.at[0, my_part],
            w_all.at[shards - d, my_part],
            wz_send.at[d],
            wz_recv.at[d],
            {"mp": mp_peer(d)},
        )
        for d in ring
    ]
    for copy in wz:
        copy.start()
    tok_copies = exchange(tok, x_all, tok_send, tok_recv)
    for copy in tok_copies:
        copy.start()

    for copy in loads:
        copy.wait()
    for copy in small_copies:
        copy.wait_recv()
    for r in range(shards):
        shard = lax.rem(me + r, shards)
        at = pl.ds(pl.multiple_of(shard * width_local, 8), width_local)
        bias[r] = jnp.broadcast_to(small_all[r, 0:1, :units], (128, units)).T
        for i in range(5):
            line = small_all[r, i + 1 : i + 2, : (width_local + 127) // 128 * 128]
            vecs[i, at] = jnp.broadcast_to(line, (128, line.shape[1])).T[:width_local]

    for copy in wz:
        copy.wait_recv()

    def weights_from(who):
        return w_all.at[pl.ds(1, shards - 1), pl.ds(pl.multiple_of(who * part, 16), part)]

    wp = [
        remote(
            weights_from(group),
            weights_from(group),
            wp_send.at[k],
            wp_recv.at[k],
            {"dp": dp_peer(k)},
        )
        for k in others
    ]
    ws = [
        remote(
            weights_from(lax.rem(group + groups - 2 * k, groups)),
            weights_from(lax.rem(group + groups - 2 * k, groups)),
            ws_send.at[k],
            ws_recv.at[k],
            sibling,
        )
        for k in range(chips)
    ]
    for copy in wp:
        copy.start()
    ws[0].start()
    for copy in tok_copies:
        copy.wait_recv()
    cot_copies = exchange(cot, c_all, cot_send, cot_recv)
    for copy in cot_copies:
        copy.start()

    @pl.loop(0, slots)
    def _(slot):
        at = pl.ds(pl.multiple_of(slot * slot_length, 128), slot_length)
        which = bucket[me * slots + slot]
        seq_c[...] = dot(x_all[:, at], cos_tab[which]).astype(BF)
        seq_s[...] = dot(x_all[:, at], sin_tab[which]).astype(BF)

        @pl.loop(0, width // rows)
        def _(i):
            row = pl.ds(pl.multiple_of(i * rows, rows), rows)
            mixing = dot(cos_h[row], seq_c[...]) - dot(sin_h[row], seq_s[...])
            n_one[row, at] = x_all[row, at].astype(F32) + mixing

        @pl.loop(0, slot_length // 128)
        def _(i):
            col = pl.ds(pl.multiple_of(slot * slot_length + i * 128, 128), 128)
            value = n_one[:, col]
            centered = value - jnp.mean(value, axis=0, keepdims=True)
            inverse = lax.rsqrt(jnp.mean(centered * centered, axis=0, keepdims=True) + EPSILON)
            normed = centered * inverse
            n_one[:, col] = normed
            inv_one[:, col] = inverse
            hid[:, col] = (normed * vecs[1] + vecs[2]).astype(BF)

    for k in others:
        wp[k - 1].wait_recv()
        ws[k].start()

    def first_matmul(r):
        @pl.loop(0, units // rows)
        def _(i):
            row = pl.ds(pl.multiple_of(i * rows, rows), rows)
            pre = dot(w_all[r, pl.ds(0, width), row], hid[...], 0, 0) + bias[r, row, 0:1]
            cdf = 0.5 + 0.5 * lax.erf(pre * (1.0 / math.sqrt(2.0)))
            pdf = jnp.exp(-0.5 * pre * pre) * (1.0 / math.sqrt(2.0 * math.pi))
            act[r, row] = (pre * cdf).astype(BF)
            slope[r, row] = (cdf + pre * pdf).astype(BF)

    first_matmul(0)
    for copy in ws:
        copy.wait_recv()
    pl.loop(1, shards)(first_matmul)

    hits[...] = jnp.zeros_like(hits)
    acc[...] = jnp.zeros_like(acc)

    @pl.loop(0, chunk // cols)
    def _(i):
        col = pl.ds(pl.multiple_of(i * cols, cols), cols)
        second = n_one[:, col] * vecs[1, :, 0:1] + vecs[2, :, 0:1] + vecs[0, :, 0:1]
        total = dot(w_all[0, pl.ds(width, units)], act[0, :, col], 0, 0)
        for r in ring:
            total += dot(w_all[r, pl.ds(width, units)], act[r, :, col], 0, 0)
        second += total
        centered = second - jnp.mean(second, axis=0, keepdims=True)
        inverse = lax.rsqrt(jnp.mean(centered * centered, axis=0, keepdims=True) + EPSILON)
        normed = centered * inverse
        n_two[:, col] = normed
        inv_two[:, col] = inverse
        result = normed * vecs[3, :, 0:1] + vecs[4, :, 0:1]
        x_all[:, col] = result.astype(BF)
        feature = lax.broadcasted_iota(jnp.int32, (width, cols), 0)
        chosen = feature == labels[pl.ds(me, 1), col]
        picked = jnp.sum(jnp.where(chosen, result, 0.0), axis=0, keepdims=True)
        soft = 1.0 / (1.0 + jnp.exp(-2.0 * picked))
        hits[...] += jnp.where(mask[pl.ds(me, 1), col] == 1, soft, 0.0)

    def send_back(source, target, send, recv, first, length):
        copies = []
        for d in ring:
            peer = mp_peer(d)
            copies.append(
                remote(
                    source.at[
                        pl.ds(pl.multiple_of(peer * width_local, 16), width_local),
                        pl.ds(first, length),
                    ],
                    target.at[:, pl.ds(pl.multiple_of(me * chunk + first, 128), length)],
                    send.at[d],
                    recv.at[d],
                    {"mp": peer},
                )
            )
        return copies

    out_copies = send_back(x_all, out, out_send, out_recv, 0, chunk)
    out_own = pltpu.make_async_copy(x_all.at[my_rows], out.at[:, my_cols], own_sem.at[0])
    for copy in out_copies + [out_own]:
        copy.start()

    for copy in cot_copies:
        copy.wait_recv()

    @pl.loop(0, chunk // cols)
    def _(i):
        col = pl.ds(pl.multiple_of(i * cols, cols), cols)
        upstream = c_all[:, col].astype(F32)
        normed = n_two[:, col]
        scaled = upstream * vecs[3, :, 0:1]
        first = jnp.mean(scaled, axis=0, keepdims=True)
        both = jnp.mean(scaled * normed, axis=0, keepdims=True)
        grad_two = inv_two[:, col] * (scaled - first - normed * both)
        n_two[:, col] = grad_two
        low = grad_two.astype(BF)
        grad[:, col] = low
        acc[0] += lanes(low.astype(F32))
        acc[3] += lanes(upstream * normed)
        acc[4] += lanes(upstream)

    @pl.loop(0, shards)
    def _(r):
        @pl.loop(0, units // rows)
        def _(i):
            row = pl.ds(pl.multiple_of(i * rows, rows), rows)
            grad_act = dot(w_all[r, pl.ds(pl.multiple_of(width + i * rows, rows), rows)], grad[...])
            low = (grad_act * slope[r, row].astype(F32)).astype(BF)
            slope[r, row] = low
            bias_acc[r, row] = lanes(low.astype(F32))

    @pl.loop(0, chunk // cols)
    def _(i):
        col = pl.ds(pl.multiple_of(i * cols, cols), cols)
        total = dot(w_all[0, pl.ds(0, width)], slope[0, :, col])
        for r in ring:
            total += dot(w_all[r, pl.ds(0, width)], slope[r, :, col])
        upstream = n_two[:, col] + total
        normed = n_one[:, col]
        scaled = upstream * vecs[1, :, 0:1]
        first = jnp.mean(scaled, axis=0, keepdims=True)
        both = jnp.mean(scaled * normed, axis=0, keepdims=True)
        grad_one = inv_one[:, col] * (scaled - first - normed * both)
        n_two[:, col] = grad_one
        c_all[:, col] = grad_one.astype(BF)
        acc[1] += lanes(upstream * normed)
        acc[2] += lanes(upstream)

    dx_copies = []
    for slot in range(slots):
        at = pl.ds(slot * slot_length, slot_length)
        which = bucket[me * slots + slot]

        @pl.loop(0, width // rows)
        def _(i):
            row = pl.ds(pl.multiple_of(i * rows, rows), rows)
            seq_c[row] = dot(cos_h[row], c_all[:, at]).astype(BF)
            seq_s[row] = -dot(sin_h[row], c_all[:, at]).astype(BF)

        @pl.loop(0, width // rows)
        def _(i):
            row = pl.ds(pl.multiple_of(i * rows, rows), rows)
            back = dot(seq_c[row], cos_tab[which]) + dot(seq_s[row], sin_tab[which])
            c_all[row, at] = (n_two[row, at] + back).astype(BF)

        copies = send_back(
            c_all, dx, dx_send.at[slot], dx_recv.at[slot], slot * slot_length, slot_length
        )
        copies.append(
            pltpu.make_async_copy(
                c_all.at[my_rows, at],
                dx.at[
                    :,
                    pl.ds(pl.multiple_of(me * chunk + slot * slot_length, 128), slot_length),
                ],
                own_sem.at[1 + slot],
            )
        )
        for copy in copies:
            copy.start()
        dx_copies += copies

    def put(r, half):
        return pltpu.make_async_copy(stage.at[half], d_w.at[r, half], stage_sem.at[half])

    @pl.loop(0, shards)
    def _(r):
        @pl.when(r > 0)
        def _():
            put(r, 0).wait()

        @pl.loop(0, width // rows)
        def _(i):
            row = pl.ds(pl.multiple_of(i * rows, rows), rows)
            stage[0, row] = dot(hid[row], slope[r], 1, 1).astype(BF)

        put(r, 0).start()

        @pl.when(r > 0)
        def _():
            put(r, 1).wait()

        @pl.loop(0, units // rows)
        def _(i):
            row = pl.ds(pl.multiple_of(i * rows, rows), rows)
            stage[1, row] = dot(act[r, row], grad[...], 1, 1).astype(BF)

        put(r, 1).start()

    put(0, 0).wait()
    put(0, 1).wait()

    lane = lax.broadcasted_iota(jnp.int32, (width_local, 128), 1)
    total_hits = jnp.sum(hits[...], axis=1, keepdims=True)
    for r in range(shards):
        shard = lax.rem(me + r, shards)
        at = pl.ds(pl.multiple_of(shard * width_local, 8), width_local)
        sums[r, 0:1] = jnp.broadcast_to(
            jnp.sum(bias_acc[r], axis=1, keepdims=True), (units, 128)
        ).T[0:1]
        line = jnp.where(lane == 6, total_hits, 0.0)
        for i in range(5):
            line += jnp.where(lane == i + 1, jnp.sum(acc[i, at], axis=1, keepdims=True), 0.0)
        spare = (-width_local) % 128
        if spare:
            line = jnp.concatenate([line, jnp.zeros((spare, 128), F32)], axis=0)
        sums[r, 1:8, : width_local + spare] = line.T[1:8]
        sums[r, 1:8, width_local + spare :] = jnp.zeros((7, units - width_local - spare), F32)

    for copy in small_copies + wz + wp + ws + tok_copies + cot_copies:
        copy.wait_send()
    for copy in out_copies + [out_own] + dx_copies:
        copy.wait()


def layer_call(shards, groups, tok, cot, w_in, w_out, small, bucket, labels, mask):
    width_local, tokens = tok.shape
    width = width_local * shards
    units = w_in.shape[1]
    chunk = tokens // shards
    slot_length = tokens // bucket.shape[0]
    slots = chunk // slot_length
    cols = min(256, slot_length)
    cos_seq, sin_seq = seq_tables(slot_length)
    cos_hid, sin_hid = (jnp.asarray(t, BF) for t in dft_pair(width))
    dma = pltpu.SemaphoreType.DMA
    chips = groups // 2
    return pl.pallas_call(
        functools.partial(layer_kernel, shards, groups),
        out_shape=[
            jax.ShapeDtypeStruct((width_local, tokens), BF),
            jax.ShapeDtypeStruct((width_local, tokens), BF),
            jax.ShapeDtypeStruct((shards, 2, width, units), BF),
            jax.ShapeDtypeStruct((shards, 8, units), F32),
        ],
        in_specs=[ANY] * 5 + [SMEM, VMEM, VMEM] + [ANY] * 4,
        out_specs=[ANY, ANY, ANY, VMEM],
        scratch_shapes=[
            pltpu.VMEM((width, chunk), BF),
            pltpu.VMEM((width, chunk), BF),
            pltpu.VMEM((shards, 2 * width, units), BF),
            pltpu.VMEM((shards, 8, units), F32),
            pltpu.VMEM((3, slot_length, slot_length), BF),
            pltpu.VMEM((3, slot_length, slot_length), BF),
            pltpu.VMEM((width, width), BF),
            pltpu.VMEM((width, width), BF),
            pltpu.VMEM((width, chunk), F32),
            pltpu.VMEM((1, chunk), F32),
            pltpu.VMEM((width, chunk), BF),
            pltpu.VMEM((shards, units, chunk), BF),
            pltpu.VMEM((shards, units, chunk), BF),
            pltpu.VMEM((width, chunk), F32),
            pltpu.VMEM((1, chunk), F32),
            pltpu.VMEM((width, chunk), BF),
            pltpu.VMEM((width, slot_length), BF),
            pltpu.VMEM((width, slot_length), BF),
            pltpu.VMEM((5, width, 128), F32),
            pltpu.VMEM((shards, units, 128), F32),
            pltpu.VMEM((5, width, 128), F32),
            pltpu.VMEM((shards, units, 128), F32),
            pltpu.VMEM((1, cols), F32),
            pltpu.VMEM((2, width, units), BF),
            dma((7,)),
            dma((1 + slots,)),
        ]
        + [dma((shards,))] * 8
        + [dma((chips,))] * 4
        + [dma((shards,))] * 2
        + [dma((slots, shards))] * 2
        + [dma((2,))],
        compiler_params=pltpu.CompilerParams(
            collective_id=0, has_side_effects=True, vmem_limit_bytes=VMEM_LIMIT
        ),
        name="layer",
    )(tok, cot, w_in, w_out, small, bucket, labels, mask, cos_seq, sin_seq, cos_hid, sin_hid)


def body(
    tokens,
    bucket,
    w_in,
    b_in,
    w_out,
    b_out,
    gain_one,
    shift_one,
    gain_two,
    shift_two,
    mask,
    labels,
    cotangent,
):
    shards = lax.axis_size("mp")
    groups = lax.axis_size("dp")
    width_local, token_count = tokens.shape
    width = width_local * shards
    units = w_in.shape[1]
    vectors = jnp.stack([b_out, gain_one, shift_one, gain_two, shift_two])
    small = jnp.concatenate(
        [b_in[None, :], jnp.pad(vectors, ((0, 2), (0, units - width_local)))], axis=0
    )
    output, d_x, grads, sums = layer_call(
        shards,
        groups,
        tokens,
        cotangent,
        w_in,
        w_out,
        small,
        bucket,
        labels.reshape(shards, -1),
        mask.reshape(shards, -1),
    )
    d_tokens = d_x.astype(F32)
    me = lax.axis_index("mp")
    grads = jnp.roll(grads, me, axis=0).reshape(shards, 2 * width, units)
    grads = lax.psum_scatter(grads, "dp", scatter_dimension=1, tiled=True)
    grads = lax.psum_scatter(grads.astype(F32), "mp", scatter_dimension=0, tiled=True)
    grads = lax.all_gather(grads[0], "dp", axis=0, tiled=True)
    sums = lax.psum(jnp.roll(sums, me, axis=0), ("dp", "mp"))
    sums = lax.dynamic_index_in_dim(sums, me, 0, False)
    rest = [sums[i + 1, :width_local] for i in range(5)]
    score = sums[6, 0] * 8.0 / (token_count * groups)
    return (output, d_tokens, grads[:width], sums[0], grads[width:], *rest, score)


def solution(mesh):
    in_specs = (
        P("mp", "dp"),
        P("dp"),
        P(None, "mp"),
        P("mp"),
        P("mp", None),
        P("mp"),
        P("mp"),
        P("mp"),
        P("mp"),
        P("mp"),
        P("dp"),
        P("dp"),
        P("mp", "dp"),
    )
    out_specs = (
        P("mp", "dp"),
        P("mp", "dp"),
        P(None, "mp"),
        P("mp"),
        P("mp", None),
        P("mp"),
        P("mp"),
        P("mp"),
        P("mp"),
        P("mp"),
        P(),
    )
    return jax.shard_map(body, mesh=mesh, in_specs=in_specs, out_specs=out_specs, check_vma=False)
```

time: 1710 us -> 450 us (0.26)
  waiting for transfers between devices: 895 us -> 233 us
  matrix products: 562 us -> 0 us
  Pallas kernels: 0 us -> 170 us
  blocking collectives: 166 us -> 0 us
  other arithmetic: 44.3 us -> 16.6 us
    dot_general x14 -> x0, matrix products: 562 us -> none  [the longest x1 113 us: seq_transform(): jnp.einsum('sjk,dsk->dsj', sin_seq, blocks, preferred_element_type=jnp.fl...]
    reduce_scatter x3 -> x2, waiting for transfers between devices: 634 us -> 127 us  [the longest x1 79.5 us: body(): grads = lax.psum_scatter(grads, 'dp', scatter_dimension=1, tiled=True)]
    all_gather x3 -> x1, waiting for transfers between devices: 260 us -> 0.01 us  [body(): grads = lax.all_gather(grads[0], 'dp', axis=0, tiled=True)]
    pallas_call x0 -> x1, Pallas kernels: none -> 170 us  [layer_call(): pl.pallas_call(functools.partial(layer_kernel, shards, groups), out_shape...]
    psum x8 -> x0, blocking collectives: 166 us -> none  [the longest x1 47.5 us: body(): all_hits = lax.psum(own_hits, ('dp', 'mp'))]
    psum x1, waiting for transfers between devices: 0.01 us -> 105 us  [body(): sums = lax.psum(jnp.roll(sums, me, axis=0), ('dp', 'mp'))]
    reduce_sum x7 -> x0, other arithmetic: 30.6 us -> none  [the longest x2 12.2 us: norm_back(): jnp.sum(upstream * normed, axis=1)]
  transfers between devices with their start and end apart: 7 -> 4, of which waited for: 6 -> 3; matrix products, arithmetic and copies ran while one was open for 15% -> 1% of each run, Pallas kernels for 0% -> 0%
where the time goes in v2:
time: 450 us; the launch traced here: 449 us
  waiting for transfers between devices  233 us (52%)
  Pallas kernels  170 us (38%)
  between operations  17 us (4%)
  other arithmetic  16.6 us (4%)
  local copies, waits for them, and re-layouts  13.4 us (3%)
    pallas_call x1, Pallas kernels, layer_call(): pl.pallas_call(functools.partial(layer_kernel, shards, groups), out_shape...  170 us
    psum x1, waiting for transfers between devices, body(): sums = lax.psum(jnp.roll(sums, me, axis=0), ('dp', 'mp'))  105 us
    reduce_scatter x1, waiting for transfers between devices, body(): grads = lax.psum_scatter(grads, 'dp', scatter_dimension=1, tiled=True)  79.5 us
    reduce_scatter x1, waiting for transfers between devices, body(): lax.psum_scatter(grads.astype(F32), 'mp', scatter_dimension=0, tiled=True)  47.6 us
    concatenate x1, other arithmetic, body(): grads = jnp.roll(grads, me, axis=0).reshape(shards, 2 * width, units)  10.4 us
  transfers between devices with their start and end apart: 4, of which 3 were waited for; matrix products, arithmetic and copies ran while one was open for 1% of the time, Pallas kernels for 0%

profile of v2, /device:TPU:0, one launch (start us, length us, event | category | flops | bytes accessed | tf_op | source)
XLA Modules:
  0.0 449.5 jit_solution(16990883021289806772)
XLA Ops:
  8.0 0.0 reduce-scatter.3.cloned.1.call-start
  8.1 0.7 broadcast_in_dim.3
  8.8 1.3 reshape.36.mask
  10.1 1.3 reshape.35.labels
  11.4 0.8 stack.23
  12.2 0.6 select_maximum_fusion.small
  12.8 169.7 %layer.1 = (bf16[192,4096]{1,0:T(8,128)(2,1)}, bf16[192,4096]{1,0:T(8,128)(2,1)}, bf16[4,2,768,768]{3,2,1,0:T(8,128)(2,1)}, f32[4,8,768]{2,1,0:T(8,128)}) custom-call(bf16[192,4096]{1,0:T(8,128)(2,1)} %tok.1, bf16[192,4096]{1,0:T(8,128)(2,1)} %cot.1, bf16[768,768]{1,0:T(8,128)(2,1)} %w_in.1, bf16[768,768]{1,0:T(8,128)(2,1)} %w_out.1, ...), custom_call_target="tpu_custom_call" | custom-call | tf_op jit(solution)/shard_map/layer/pallas_call | solution.py:507
  182.5 10.4 %fusion = bf16[4,2,768,768]{3,2,1,0:T(8,128)(2,1)} fusion(s32[]{:T(128)S(6)} %select_n.24, bf16[4,2,768,768]{3,2,1,0:T(8,128)(2,1)} %get-tuple-element.17), kind=kLoop, calls=%fused_computation.2 | loop fusion | flops 4718592 | bytes 18874372 | tf_op jit(solution)/shard_map/jit(_roll_dynamic)/concatenate | solution.py:595
  193.0 0.0 reduce-scatter.3.cloned.1.call-update
  193.0 0.0 copy-start.2
  193.0 0.0 reduce-scatter.5.cloned.1.call-start
  193.1 79.5 %reduce-scatter.3.cloned.1.call-done = bf16[4,192,768]{2,1,0:T(8,128)(2,1)} async-done(((bf16[4,1536,768]{2,1,0:T(8,128)(2,1)}), bf16[4,192,768]{2,1,0:T(8,128)(2,1)}) %reduce-scatter.3.cloned.1.call-update) | async-done | bytes 1179664 | tf_op jit(solution)/shard_map/reduce_scatter | solution.py:596
  272.5 2.9 convert_element_type.9
  275.4 0.0 copy-start.1
  275.4 0.0 reduce-scatter.5.cloned.1.call-update
  275.4 0.0 all-reduce.3.cloned.1.call-start
  275.5 0.0 copy-done.2
  275.5 0.7 fusion.1
  276.1 0.0 all-reduce.3.cloned.1.call-update
  276.2 0.0 all-gather.3.cloned.1.call-start
  276.2 47.6 %reduce-scatter.5.cloned.1.call-done = f32[1,192,768]{2,1,0:T(8,128)} async-done(((f32[4,192,768]{2,1,0:T(8,128)}), f32[1,192,768]{2,1,0:T(8,128)}) %reduce-scatter.5.cloned.1.call-update) | async-done | bytes 589840 | tf_op jit(solution)/shard_map/reduce_scatter | solution.py:597
  323.8 0.0 all-gather.3.cloned.1.call-update
  323.8 0.0 copy-done.1
  323.8 2.0 convert_element_type.8
  325.8 105.5 %all-reduce.3.cloned.1.call-done = f32[4,8,768]{2,1,0:T(8,128)} async-done(((f32[4,8,768]{2,1,0:T(8,128)}), f32[4,8,768]{2,1,0:T(8,128)}) %all-reduce.3.cloned.1.call-update) | async-done | bytes 98320 | tf_op jit(solution)/shard_map/psum | solution.py:599
  431.3 0.7 dynamic-slice_bitcast_fusion
  432.0 0.5 slice.46
  433.2 1.3 dynamic-slice_reduce_fusion
  434.5 0.6 fusion.2
  435.1 0.0 copy-start
  435.1 0.0 all-gather.3.cloned.1.call-done
  435.1 5.0 %slice_bitcast_fusion = (f32[768,768]{1,0:T(8,128)}, f32[768,768]{1,0:T(8,128)}) fusion(f32[1,1536,768]{2,1,0:T(8,128)} %all-gather.3.cloned.1.call-done), kind=kLoop, calls=%fused_computation.3 | loop fusion | bytes 9437184 | tf_op jit(solution)/shard_map/slice | solution.py:603
  440.1 0.0 copy-done
  440.1 1.1 copy.30
Async XLA Ops:
  8.0 264.5 %reduce-scatter.3.cloned.1.call-start = ((), (), s32[]{:S(2)}) async-start(), calls=%async_computation.2 | async-start | bytes 10616832 | tf_op jit(solution)/shard_map/reduce_scatter | solution.py:596
  193.0 82.5 %copy-start.2 = (f32[4,8,768]{2,1,0:T(8,128)S(1)}, f32[4,8,768]{2,1,0:T(8,128)}, u32[]{:S(2)}) copy-start(f32[4,8,768]{2,1,0:T(8,128)} %get-tuple-element.18) | copy-start | bytes 294916
  193.0 130.8 %reduce-scatter.5.cloned.1.call-start = ((), (), s32[]{:S(2)}) async-start(), calls=%async_computation.3 | async-start | bytes 2949120 | tf_op jit(solution)/shard_map/reduce_scatter | solution.py:597
  275.4 48.4 %copy-start.1 = (bf16[192,4096]{1,0:T(8,128)(2,1)S(1)}, bf16[192,4096]{1,0:T(8,128)(2,1)}, u32[]{:S(2)}) copy-start(bf16[192,4096]{1,0:T(8,128)(2,1)} %get-tuple-element.16) | copy-start | bytes 4718596
  275.4 155.9 %all-reduce.3.cloned.1.call-start = ((), (), s32[]{:S(2)}) async-start(), calls=%async_computation.4 | async-start | bytes 196608 | tf_op jit(solution)/shard_map/psum | solution.py:599
  276.2 158.9 %all-gather.3.cloned.1.call-start = ((), (), s32[]{:S(2)}) async-start(), calls=%async_computation.5 | async-start | bytes 5308416 | tf_op jit(solution)/shard_map/all_gather | solution.py:598
  435.1 5.0 %copy-start = (bf16[192,4096]{1,0:T(8,128)(2,1)S(1)}, bf16[192,4096]{1,0:T(8,128)(2,1)}, u32[]{:S(2)}) copy-start(bf16[192,4096]{1,0:T(8,128)(2,1)} %get-tuple-element.37) | copy-start | bytes 4718596
Sparse Core Ops, SparseCore 0:
  193.1 79.3 reduce-scatter.2
  275.5 48.1 reduce-scatter.4
  325.7 38.5 all-gather.2
Sparse Core Ops, SparseCore 1:
  282.1 149.2 all-reduce.2

commit v3 on v2

--- a/solution.py
+++ b/solution.py
@@ -104,9 +104,17 @@
     vecs,
     bias,
     acc,
-    bias_acc,
     hits,
-    stage,
+    near,
+    far,
+    part_low,
+    line_in,
+    own_part,
+    done_low,
+    sums_own,
+    sums_mp,
+    sums_mid,
+    sums_dp,
     load_sem,
     own_sem,
     tok_send,
@@ -125,7 +133,20 @@
     out_recv,
     dx_send,
     dx_recv,
-    stage_sem,
+    near_send,
+    near_recv,
+    far_send,
+    far_recv,
+    line_send,
+    line_recv,
+    done_send,
+    done_recv,
+    share_send,
+    share_recv,
+    mp_send,
+    mp_recv,
+    dp_send,
+    dp_recv,
 ):
     me = lax.axis_index("mp")
     group = lax.axis_index("dp")
@@ -148,10 +169,10 @@
     def dp_peer(step):
         return lax.rem(group + 2 * step, groups)
 
-    sibling = {"dp": group + 1 - 2 * lax.rem(group, 2)}
-    greet(
-        [{"mp": mp_peer(d)} for d in ring] + [{"dp": dp_peer(k)} for k in others] + [sibling]
-    )
+    core = lax.rem(group, 2)
+    sibling = {"dp": group + 1 - 2 * core}
+    plane = [{"dp": lax.rem(group + q, groups)} for q in range(1, groups)]
+    greet([{"mp": mp_peer(d)} for d in ring] + plane)
 
     own_w = [
         pltpu.make_async_copy(w_in, w_all.at[0, :width], own_sem.at[0]),
@@ -378,6 +399,124 @@
         acc[3] += lanes(upstream * normed)
         acc[4] += lanes(upstream)
 
+    half = width // 2
+    split = 1 if half // chips % 16 == 0 else 2
+    piece_rows = half * split // chips
+    piece_cols = width // split
+    keep = pl.ds(pl.multiple_of(core * half, 16), half)
+    give = pl.ds(pl.multiple_of((1 - core) * half, 16), half)
+
+    def piece(who):
+        chip = who // 2
+        first = core * half + chip // split * piece_rows
+        return (
+            pl.ds(pl.multiple_of(first, 16), piece_rows),
+            pl.ds(pl.multiple_of(lax.rem(chip, split) * piece_cols, 128), piece_cols),
+        )
+
+    d_out = act.at[:, :, pl.ds(0, width)]
+    d_in = w_all.at[:, pl.ds(0, width)]
+
+    def near_copy(x, r):
+        source = (d_in, d_out)[x]
+        return remote(
+            source.at[r, give], near.at[x, r], near_send.at[x, r], near_recv.at[x, r], sibling
+        )
+
+    def add_near(x):
+        source = (d_in, d_out)[x]
+
+        @pl.loop(0, shards)
+        def _(r):
+            near_copy(x, r).wait_recv()
+            source[r, keep] = (source[r, keep].astype(F32) + near[x, r].astype(F32)).astype(BF)
+
+        copies = []
+        for k in others:
+            at, across = piece(dp_peer(k))
+            copies.append(
+                remote(
+                    source.at[:, at, across],
+                    far.at[x, k - 1],
+                    far_send.at[x, k],
+                    far_recv.at[x, k],
+                    {"dp": dp_peer(k)},
+                )
+            )
+        for copy in copies:
+            copy.start()
+        return copies
+
+    my_at, my_across = piece(group)
+
+    def add_far(x, copies):
+        source = (d_in, d_out)[x]
+        for copy in copies:
+            copy.wait_recv()
+
+        @pl.loop(0, shards)
+        def _(r):
+            total = source[r, my_at, my_across].astype(F32)
+            for k in others:
+                total += far[x, k - 1, r].astype(F32)
+            part_low[x, r] = total.astype(BF)
+
+            @pl.when(r == 0)
+            def _():
+                own_part[x] = total
+
+        copies = [
+            remote(
+                part_low.at[x, d],
+                line_in.at[x, d - 1],
+                line_send.at[x, d],
+                line_recv.at[x, d],
+                {"mp": mp_peer(d)},
+            )
+            for d in ring
+        ]
+        for copy in copies:
+            copy.start()
+        return copies
+
+    def add_line(x, copies):
+        for copy in copies:
+            copy.wait_recv()
+        total = own_part[x]
+        for d in ring:
+            total += line_in[x, d - 1].astype(F32)
+        done_low[x] = total.astype(BF)
+        target = d_w.at[x, my_at, my_across]
+        copies = [
+            remote(
+                done_low.at[x], target, done_send.at[x, k], done_recv.at[x, k], {"dp": dp_peer(k)}
+            )
+            for k in others
+        ]
+        own = pltpu.make_async_copy(done_low.at[x], target, own_sem.at[1 + slots + x])
+        for copy in copies + [own]:
+            copy.start()
+        return copies, own
+
+    def share(x, copies, own):
+        own.wait()
+        for copy in copies:
+            copy.wait_recv()
+        copy = remote(
+            d_w.at[x, keep], d_w.at[x, keep], share_send.at[x], share_recv.at[x], sibling
+        )
+        copy.start()
+        return copy
+
+    @pl.loop(0, shards)
+    def _(r):
+        @pl.loop(0, units // rows)
+        def _(i):
+            row = pl.ds(pl.multiple_of(i * rows, rows), rows)
+            d_out[r, row] = dot(act[r, row], grad[...], 1, 1).astype(BF)
+
+        near_copy(1, r).start()
+
     @pl.loop(0, shards)
     def _(r):
         @pl.loop(0, units // rows)
@@ -386,7 +525,9 @@
             grad_act = dot(w_all[r, pl.ds(pl.multiple_of(width + i * rows, rows), rows)], grad[...])
             low = (grad_act * slope[r, row].astype(F32)).astype(BF)
             slope[r, row] = low
-            bias_acc[r, row] = lanes(low.astype(F32))
+            bias[r, row] = lanes(low.astype(F32))
+
+    far_out = add_near(1)
 
     @pl.loop(0, chunk // cols)
     def _(i):
@@ -439,43 +580,13 @@
             copy.start()
         dx_copies += copies
 
-    def put(r, half):
-        return pltpu.make_async_copy(stage.at[half], d_w.at[r, half], stage_sem.at[half])
-
-    @pl.loop(0, shards)
-    def _(r):
-        @pl.when(r > 0)
-        def _():
-            put(r, 0).wait()
-
-        @pl.loop(0, width // rows)
-        def _(i):
-            row = pl.ds(pl.multiple_of(i * rows, rows), rows)
-            stage[0, row] = dot(hid[row], slope[r], 1, 1).astype(BF)
-
-        put(r, 0).start()
-
-        @pl.when(r > 0)
-        def _():
-            put(r, 1).wait()
-
-        @pl.loop(0, units // rows)
-        def _(i):
-            row = pl.ds(pl.multiple_of(i * rows, rows), rows)
-            stage[1, row] = dot(act[r, row], grad[...], 1, 1).astype(BF)
-
-        put(r, 1).start()
-
-    put(0, 0).wait()
-    put(0, 1).wait()
-
     lane = lax.broadcasted_iota(jnp.int32, (width_local, 128), 1)
     total_hits = jnp.sum(hits[...], axis=1, keepdims=True)
     for r in range(shards):
         shard = lax.rem(me + r, shards)
         at = pl.ds(pl.multiple_of(shard * width_local, 8), width_local)
-        sums[r, 0:1] = jnp.broadcast_to(
-            jnp.sum(bias_acc[r], axis=1, keepdims=True), (units, 128)
+        sums_own[r, 0:1] = jnp.broadcast_to(
+            jnp.sum(bias[r], axis=1, keepdims=True), (units, 128)
         ).T[0:1]
         line = jnp.where(lane == 6, total_hits, 0.0)
         for i in range(5):
@@ -483,12 +594,59 @@
         spare = (-width_local) % 128
         if spare:
             line = jnp.concatenate([line, jnp.zeros((spare, 128), F32)], axis=0)
-        sums[r, 1:8, : width_local + spare] = line.T[1:8]
-        sums[r, 1:8, width_local + spare :] = jnp.zeros((7, units - width_local - spare), F32)
-
-    for copy in small_copies + wz + wp + ws + tok_copies + cot_copies:
+        sums_own[r, 1:8, : width_local + spare] = line.T[1:8]
+        sums_own[r, 1:8, width_local + spare :] = jnp.zeros((7, units - width_local - spare), F32)
+    mp_sums = [
+        remote(sums_own.at[d], sums_mp.at[me], mp_send.at[d], mp_recv.at[d], {"mp": mp_peer(d)})
+        for d in ring
+    ]
+    for copy in mp_sums:
+        copy.start()
+    sums_mp[me] = sums_own[0]
+
+    for copy in wz + wp + ws:
         copy.wait_send()
-    for copy in out_copies + [out_own] + dx_copies:
+
+    @pl.loop(0, shards)
+    def _(r):
+        @pl.loop(0, width // rows)
+        def _(i):
+            row = pl.ds(pl.multiple_of(i * rows, rows), rows)
+            d_in[r, row] = dot(hid[row], slope[r], 1, 1).astype(BF)
+
+        near_copy(0, r).start()
+
+    line_out = add_far(1, far_out)
+    far_in = add_near(0)
+    for copy in mp_sums:
+        copy.wait_recv()
+    sums_mid[...] = sum(sums_mp[s] for s in range(shards))
+    dp_sums = [
+        remote(sums_mid, sums_dp.at[group], dp_send.at[q], dp_recv.at[q], peer)
+        for q, peer in enumerate(plane)
+    ]
+    for copy in dp_sums:
+        copy.start()
+    sums_dp[group] = sums_mid[...]
+    done_out, own_out = add_line(1, line_out)
+    line_from_in = add_far(0, far_in)
+    share_out = share(1, done_out, own_out)
+    for copy in dp_sums:
+        copy.wait_recv()
+    sums[...] = sum(sums_dp[q] for q in range(groups))
+    done_in, own_in = add_line(0, line_from_in)
+    share_in = share(0, done_in, own_in)
+
+    @pl.loop(0, shards)
+    def _(r):
+        near_copy(0, r).wait_send()
+        near_copy(1, r).wait_send()
+
+    for copy in small_copies + tok_copies + cot_copies + mp_sums + dp_sums:
+        copy.wait_send()
+    for copy in far_out + far_in + line_out + line_from_in + done_out + done_in:
+        copy.wait_send()
+    for copy in out_copies + [out_own] + dx_copies + [share_out, share_in]:
         copy.wait()
 
 
@@ -504,13 +662,15 @@
     cos_hid, sin_hid = (jnp.asarray(t, BF) for t in dft_pair(width))
     dma = pltpu.SemaphoreType.DMA
     chips = groups // 2
+    split = 1 if width // 2 // chips % 16 == 0 else 2
+    piece = (width // 2 * split // chips, width // split)
     return pl.pallas_call(
         functools.partial(layer_kernel, shards, groups),
         out_shape=[
             jax.ShapeDtypeStruct((width_local, tokens), BF),
             jax.ShapeDtypeStruct((width_local, tokens), BF),
-            jax.ShapeDtypeStruct((shards, 2, width, units), BF),
-            jax.ShapeDtypeStruct((shards, 8, units), F32),
+            jax.ShapeDtypeStruct((2, width, units), BF),
+            jax.ShapeDtypeStruct((8, units), F32),
         ],
         in_specs=[ANY] * 5 + [SMEM, VMEM, VMEM] + [ANY] * 4,
         out_specs=[ANY, ANY, ANY, VMEM],
@@ -536,17 +696,31 @@
             pltpu.VMEM((5, width, 128), F32),
             pltpu.VMEM((shards, units, 128), F32),
             pltpu.VMEM((5, width, 128), F32),
-            pltpu.VMEM((shards, units, 128), F32),
             pltpu.VMEM((1, cols), F32),
-            pltpu.VMEM((2, width, units), BF),
+            pltpu.VMEM((2, shards, width // 2, width), BF),
+            pltpu.VMEM((2, chips - 1, shards) + piece, BF),
+            pltpu.VMEM((2, shards) + piece, BF),
+            pltpu.VMEM((2, shards - 1) + piece, BF),
+            pltpu.VMEM((2,) + piece, F32),
+            pltpu.VMEM((2,) + piece, BF),
+            pltpu.VMEM((shards, 8, units), F32),
+            pltpu.VMEM((shards, 8, units), F32),
+            pltpu.VMEM((8, units), F32),
+            pltpu.VMEM((groups, 8, units), F32),
             dma((7,)),
-            dma((1 + slots,)),
+            dma((3 + slots,)),
         ]
         + [dma((shards,))] * 8
         + [dma((chips,))] * 4
         + [dma((shards,))] * 2
         + [dma((slots, shards))] * 2
-        + [dma((2,))],
+        + [dma((2, shards))] * 2
+        + [dma((2, chips))] * 2
+        + [dma((2, shards))] * 2
+        + [dma((2, chips))] * 2
+        + [dma((2,))] * 2
+        + [dma((shards,))] * 2
+        + [dma((groups,))] * 2,
         compiler_params=pltpu.CompilerParams(
             collective_id=0, has_side_effects=True, vmem_limit_bytes=VMEM_LIMIT
         ),
@@ -572,7 +746,6 @@
     shards = lax.axis_size("mp")
     groups = lax.axis_size("dp")
     width_local, token_count = tokens.shape
-    width = width_local * shards
     units = w_in.shape[1]
     vectors = jnp.stack([b_out, gain_one, shift_one, gain_two, shift_two])
     small = jnp.concatenate(
@@ -591,16 +764,10 @@
         mask.reshape(shards, -1),
     )
     d_tokens = d_x.astype(F32)
-    me = lax.axis_index("mp")
-    grads = jnp.roll(grads, me, axis=0).reshape(shards, 2 * width, units)
-    grads = lax.psum_scatter(grads, "dp", scatter_dimension=1, tiled=True)
-    grads = lax.psum_scatter(grads.astype(F32), "mp", scatter_dimension=0, tiled=True)
-    grads = lax.all_gather(grads[0], "dp", axis=0, tiled=True)
-    sums = lax.psum(jnp.roll(sums, me, axis=0), ("dp", "mp"))
-    sums = lax.dynamic_index_in_dim(sums, me, 0, False)
+    grads = grads.astype(F32)
     rest = [sums[i + 1, :width_local] for i in range(5)]
     score = sums[6, 0] * 8.0 / (token_count * groups)
-    return (output, d_tokens, grads[:width], sums[0], grads[width:], *rest, score)
+    return (output, d_tokens, grads[0], sums[0], grads[1], *rest, score)
 
 
 def solution(mesh):

time: 450 us -> 241 us (0.54)
  waiting for transfers between devices: 233 us -> 0 us
  Pallas kernels: 170 us -> 218 us
  between operations: 17 us -> 2.46 us
  other arithmetic: 16.6 us -> 4.66 us
    reduce_scatter x2 -> x0, waiting for transfers between devices: 127 us -> none  [the longest x1 79.5 us: body(): grads = lax.psum_scatter(grads, 'dp', scatter_dimension=1, tiled=True)]
    psum x1 -> x0, waiting for transfers between devices: 105 us -> none  [body(): sums = lax.psum(jnp.roll(sums, me, axis=0), ('dp', 'mp'))]
    pallas_call x1, Pallas kernels: 170 us -> 218 us  [layer_call(): pl.pallas_call(functools.partial(layer_kernel, shards, groups), out_shape...]
    concatenate x2 -> x0, other arithmetic: 11.1 us -> none  [the longest x1 10.4 us: body(): grads = jnp.roll(grads, me, axis=0).reshape(shards, 2 * width, units)]
    slice x2 -> x1, local copies, waits for them, and re-layouts: 6.33 us -> 1.34 us  [body(): return (output, d_tokens, grads[0], sums[0], grads[1], *rest, score)]
  transfers between devices with their start and end apart: 4 -> 0, of which waited for: 3 -> 0; matrix products, arithmetic and copies ran while one was open for 1% -> 0% of each run, Pallas kernels for 0% -> 0%
where the time goes in v3:
time: 241 us; the launch traced here: 236 us
  Pallas kernels  218 us (90%)
  local copies, waits for them, and re-layouts  11.7 us (5%)
  other arithmetic  4.66 us (2%)
  between operations  2.46 us (1%)
    pallas_call x1, Pallas kernels, layer_call(): pl.pallas_call(functools.partial(layer_kernel, shards, groups), out_shape...  218 us

profile of v3, /device:TPU:0, one launch (start us, length us, event | category | flops | bytes accessed | tf_op | source)
XLA Modules:
  0.0 236.4 jit_solution(14415258095844916446)
XLA Ops:
  0.6 0.8 stack.23
  1.4 0.7 broadcast_in_dim.3
  2.1 0.6 select_maximum_fusion.small
  2.7 1.3 reshape.30.labels
  4.0 1.3 reshape.31.mask
  5.4 217.5 %layer.1 = (bf16[192,4096]{1,0:T(8,128)(2,1)}, bf16[192,4096]{1,0:T(8,128)(2,1)}, bf16[2,768,768]{2,1,0:T(8,128)(2,1)}, f32[8,768]{1,0:T(8,128)}) custom-call(bf16[192,4096]{1,0:T(8,128)(2,1)} %tok.1, bf16[192,4096]{1,0:T(8,128)(2,1)} %cot.1, bf16[768,768]{1,0:T(8,128)(2,1)} %w_in.1, bf16[768,768]{1,0:T(8,128)(2,1)} %w_out.1, ...), custom_call_target="tpu_custom_call" | custom-call | tf_op jit(solution)/shard_map/layer/pallas_call | solution.py:667
  222.9 1.5 fusion
  224.4 1.3 slice_reduce_fusion
  225.7 1.2 slice.35
  227.6 2.0 convert_element_type.9
  229.6 0.0 copy-start.1
  229.6 2.5 %slice_bitcast_fusion = (f32[768,768]{1,0:T(8,128)}, f32[768,768]{1,0:T(8,128)}) fusion(f32[2,768,768]{2,1,0:T(8,128)S(1)} %convert_element_type.9), kind=kLoop, calls=%fused_computation | loop fusion | bytes 9437184 | tf_op jit(solution)/shard_map/squeeze | solution.py:770
  232.1 0.0 copy-done.1
  232.1 0.0 copy-start
  232.1 2.0 convert_element_type.8
  234.1 0.0 copy-done
  234.1 1.1 copy.29
Async XLA Ops:
  229.6 2.5 %copy-start.1 = (bf16[192,4096]{1,0:T(8,128)(2,1)S(1)}, bf16[192,4096]{1,0:T(8,128)(2,1)}, u32[]{:S(2)}) copy-start(bf16[192,4096]{1,0:T(8,128)(2,1)} %get-tuple-element.16) | copy-start | bytes 4718596
  232.1 2.0 copy-start

commit v4 on v3

--- a/solution.py
+++ b/solution.py
@@ -3,7 +3,6 @@
 
 import jax
 import jax.numpy as jnp
-import numpy as np
 from jax import lax
 from jax.experimental import pallas as pl
 from jax.experimental.pallas import tpu as pltpu
@@ -18,22 +17,24 @@
 VMEM_LIMIT = 66_000_000
 
 
-def dft_pair(length):
-    places = np.arange(length)
-    angles = (places[:, None] * places[None, :] % length) * (2.0 * math.pi / length)
-    scale = 1.0 / math.sqrt(length)
-    return (np.cos(angles) * scale).astype(np.float32), (np.sin(angles) * scale).astype(np.float32)
-
-
-def seq_tables(slot_length):
-    cosines, sines = [], []
-    for bucket in range(3):
-        length = slot_length // 4 << bucket
-        cosine, sine = dft_pair(length)
-        copies = np.eye(slot_length // length, dtype=np.float32)
-        cosines.append(np.kron(copies, cosine))
-        sines.append(np.kron(copies, sine))
-    return jnp.asarray(np.stack(cosines), BF), jnp.asarray(np.stack(sines), BF)
+def turns(phase):
+    quarter = jnp.floor(phase * 4.0 + 0.5)
+    angle = (phase - quarter * 0.25) * (2.0 * math.pi)
+    square = angle * angle
+    cosine = 1.0 + square * (
+        -1 / 2 + square * (1 / 24 + square * (-1 / 720 + square * (1 / 40320)))
+    )
+    sine = angle * (
+        1.0
+        + square * (-1 / 6 + square * (1 / 120 + square * (-1 / 5040 + square * (1 / 362880))))
+    )
+    odd = (quarter == 1.0) | (quarter == 3.0)
+    first = jnp.where(odd, sine, cosine)
+    second = jnp.where(odd, cosine, sine)
+    return (
+        jnp.where((quarter == 1.0) | (quarter == 2.0), -first, first),
+        jnp.where((quarter == 2.0) | (quarter == 3.0), -second, second),
+    )
 
 
 def dot(left, right, left_dim=1, right_dim=0):
@@ -75,10 +76,6 @@
     bucket,
     labels,
     mask,
-    cos_seq,
-    sin_seq,
-    cos_hid,
-    sin_hid,
     out,
     dx,
     d_w,
@@ -154,8 +151,8 @@
     width = width_local * shards
     units = w_in.shape[1]
     chunk = tok.shape[1] // shards
-    slot_length = cos_seq.shape[1]
-    slots = chunk // slot_length
+    slots = cos_tab.shape[0]
+    slot_length = chunk // slots
     part = 2 * width // groups
     chips = groups // 2
     rows = min(256, width)
@@ -163,8 +160,14 @@
     ring = range(1, shards)
     others = range(1, chips)
 
+    inner = jnp.where(me < shards // 2, 1, -1)
+    at_end = (me == 0) | (me == shards - 1)
+
     def mp_peer(step):
         return lax.rem(me + step, shards)
+
+    def inward(step):
+        return lax.rem(me + step * inner + shards, shards)
 
     def dp_peer(step):
         return lax.rem(group + 2 * step, groups)
@@ -185,10 +188,6 @@
         for i, (source, target) in enumerate(
             [
                 (small, small_all.at[0]),
-                (cos_seq, cos_tab),
-                (sin_seq, sin_tab),
-                (cos_hid, cos_h),
-                (sin_hid, sin_h),
                 (tok.at[:, my_cols], x_all.at[my_rows]),
                 (cot.at[:, my_cols], c_all.at[my_rows]),
             ]
@@ -197,16 +196,20 @@
     for copy in own_w + loads:
         copy.start()
 
-    def exchange(source, target, send, recv):
+    def exchange(source, target, send, recv, slot, steps=(1, 2, 3)):
         copies = []
-        for d in ring:
-            peer = mp_peer(d)
+        for step in steps:
+            peer = inward(step)
+            d = lax.rem(peer - me + shards, shards)
+            first = pl.multiple_of(peer * chunk + slot * slot_length, 128)
             copies.append(
                 remote(
-                    source.at[:, pl.ds(pl.multiple_of(peer * chunk, 128), chunk)],
-                    target.at[my_rows],
-                    send.at[d],
-                    recv.at[d],
+                    source.at[:, pl.ds(first, slot_length)],
+                    target.at[
+                        my_rows, pl.ds(pl.multiple_of(slot * slot_length, 128), slot_length)
+                    ],
+                    send.at[slot, d],
+                    recv.at[slot, d],
                     {"mp": peer},
                 )
             )
@@ -227,21 +230,155 @@
     for copy in own_w:
         copy.wait()
     my_part = pl.ds(pl.multiple_of(group * part, 16), part)
-    wz = [
+
+    def weight_copy(shard, target, send):
+        place = lax.rem(shard - me + 2 * shards, shards)
+        there = lax.rem(shard - target + 2 * shards, shards)
+        return remote(
+            w_all.at[place, my_part],
+            w_all.at[there, my_part],
+            wz_send.at[send],
+            wz_recv.at[there],
+            {"mp": target},
+        )
+
+    def weight_wait(place):
         remote(
             w_all.at[0, my_part],
-            w_all.at[shards - d, my_part],
-            wz_send.at[d],
-            wz_recv.at[d],
-            {"mp": mp_peer(d)},
-        )
-        for d in ring
-    ]
+            w_all.at[place, my_part],
+            wz_send.at[0],
+            wz_recv.at[place],
+            {"mp": inward(1)},
+        ).wait_recv()
+
+    near_step = jnp.where(at_end, 1, 3)
+    far_step = jnp.where(at_end, 2, 1)
+    wz = [weight_copy(me, inward(far_step), 0), weight_copy(me, inward(near_step), 1)]
     for copy in wz:
         copy.start()
-    tok_copies = exchange(tok, x_all, tok_send, tok_recv)
-    for copy in tok_copies:
+    for slot in range(slots):
+        for copy in exchange(tok, x_all, tok_send, tok_recv, slot, (1, 2)):
+            copy.start()
+
+    def pass_on(step, send):
+        return weight_copy(inward(step), inward(3), send)
+
+    @pl.when(jnp.logical_not(at_end))
+    def _():
+        for step, send in ((1, 2), (2, 3)):
+            weight_wait(lax.rem(step * inner + shards, shards))
+            pass_on(step, send).start()
+
+    for slot in range(slots):
+        for copy in exchange(tok, x_all, tok_send, tok_recv, slot, (3,)):
+            copy.start()
+
+    @pl.when(at_end)
+    def _():
+        for place in (1, 2, 3):
+            weight_wait(place)
+
+    @pl.when(jnp.logical_not(at_end))
+    def _():
+        weight_wait(lax.rem(3 * inner + shards, shards))
+
+    side = math.isqrt(chips)
+    chip_x, chip_y = lax.rem(group // 2, side), group // 2 // side
+    halves = (pl.ds(0, units // 2), pl.ds(units // 2, units // 2))
+
+    def at_chip(x, y):
+        return (lax.rem(y + side, side) * side + lax.rem(x + side, side)) * 2 + core
+
+    def weights_of(who, across):
+        rows_of = pl.ds(pl.multiple_of(who * part, 16), part)
+        return w_all.at[pl.ds(1, shards - 1), rows_of, across]
+
+    def plane_copy(who, across, to, sem):
+        return remote(
+            weights_of(who, across), weights_of(who, across), wp_send.at[sem], wp_recv.at[sem], to
+        )
+
+    first_plane, second_plane = [], []
+    for h, across in enumerate(halves):
+        for a in range(1, side):
+            along = (a, 0) if h == 0 else (0, a)
+            first_plane.append(
+                (
+                    plane_copy(
+                        group,
+                        across,
+                        {"dp": at_chip(chip_x + along[0], chip_y + along[1])},
+                        h * chips + a,
+                    ),
+                    at_chip(chip_x - along[0], chip_y - along[1]),
+                    across,
+                )
+            )
+            for b in range(side):
+                source = at_chip(chip_x + b, chip_y) if h == 0 else at_chip(chip_x, chip_y + b)
+                to = at_chip(chip_x, chip_y + a) if h == 0 else at_chip(chip_x + a, chip_y)
+                back = (
+                    at_chip(chip_x + b, chip_y - a) if h == 0 else at_chip(chip_x - a, chip_y + b)
+                )
+                second_plane.append(
+                    (
+                        plane_copy(source, across, {"dp": to}, h * chips + side * a + b),
+                        back,
+                        across,
+                    )
+                )
+
+    def to_sibling(who, across, sem):
+        return remote(
+            weights_of(who, across),
+            weights_of(who, across),
+            ws_send.at[sem],
+            ws_recv.at[sem],
+            sibling,
+        )
+
+    ws = [to_sibling(group, pl.ds(0, units), 0)]
+    for n, (_, who, across) in enumerate(first_plane + second_plane):
+        ws.append(to_sibling(who, across, n + 1))
+    for copy, _, _ in first_plane:
         copy.start()
+    ws[0].start()
+
+    turn_rows = min(64, slot_length)
+
+    @pl.loop(0, width // turn_rows)
+    def _(i):
+        row = pl.ds(pl.multiple_of(i * turn_rows, 16), turn_rows)
+        shape = (turn_rows, width)
+        product = (
+            (lax.broadcasted_iota(jnp.int32, shape, 0) + i * turn_rows)
+            * lax.broadcasted_iota(jnp.int32, shape, 1)
+        ).astype(F32)
+        phase = product * (1.0 / width)
+        phase = (product - jnp.floor(phase) * width) * (1.0 / width)
+        cosine, sine = turns(phase)
+        cos_h[row] = (cosine * (1.0 / math.sqrt(width))).astype(BF)
+        sin_h[row] = (sine * (1.0 / math.sqrt(width))).astype(BF)
+
+    @pl.loop(0, slots * slot_length // turn_rows)
+    def _(i):
+        slot = i // (slot_length // turn_rows)
+        first = lax.rem(i, slot_length // turn_rows) * turn_rows
+        row = pl.ds(pl.multiple_of(first, 16), turn_rows)
+        shape = (turn_rows, slot_length)
+        which = bucket[me * slots + slot]
+        length = jnp.where(which == 0, slot_length // 4, slot_length // 2)
+        length = jnp.where(which == 2, slot_length, length)
+        at = lax.broadcasted_iota(jnp.int32, shape, 0) + first
+        to = lax.broadcasted_iota(jnp.int32, shape, 1)
+        inner = length - 1
+        phase = ((at & inner) * (to & inner)) & inner
+        scale = jnp.full((1, 1), length, jnp.int32).astype(F32)
+        cosine, sine = turns(phase.astype(F32) / scale)
+        scale = jnp.where((at ^ to) < length, lax.rsqrt(scale), 0.0)
+        cos_tab[slot, row] = (cosine * scale).astype(BF)
+        sin_tab[slot, row] = (sine * scale).astype(BF)
+
 
     for copy in loads:
         copy.wait()
@@ -255,47 +392,26 @@
             line = small_all[r, i + 1 : i + 2, : (width_local + 127) // 128 * 128]
             vecs[i, at] = jnp.broadcast_to(line, (128, line.shape[1])).T[:width_local]
 
-    for copy in wz:
+    for n, (copy, _, _) in enumerate(first_plane):
         copy.wait_recv()
-
-    def weights_from(who):
-        return w_all.at[pl.ds(1, shards - 1), pl.ds(pl.multiple_of(who * part, 16), part)]
-
-    wp = [
-        remote(
-            weights_from(group),
-            weights_from(group),
-            wp_send.at[k],
-            wp_recv.at[k],
-            {"dp": dp_peer(k)},
-        )
-        for k in others
-    ]
-    ws = [
-        remote(
-            weights_from(lax.rem(group + groups - 2 * k, groups)),
-            weights_from(lax.rem(group + groups - 2 * k, groups)),
-            ws_send.at[k],
-            ws_recv.at[k],
-            sibling,
-        )
-        for k in range(chips)
-    ]
-    for copy in wp:
-        copy.start()
-    ws[0].start()
-    for copy in tok_copies:
-        copy.wait_recv()
-    cot_copies = exchange(cot, c_all, cot_send, cot_recv)
-    for copy in cot_copies:
+        ws[n + 1].start()
+    for copy, _, _ in second_plane:
         copy.start()
 
     @pl.loop(0, slots)
     def _(slot):
         at = pl.ds(pl.multiple_of(slot * slot_length, 128), slot_length)
-        which = bucket[me * slots + slot]
-        seq_c[...] = dot(x_all[:, at], cos_tab[which]).astype(BF)
-        seq_s[...] = dot(x_all[:, at], sin_tab[which]).astype(BF)
+        for copy in exchange(tok, x_all, tok_send, tok_recv, slot):
+            copy.wait_recv()
+
+        @pl.when(slot == slots - 1)
+        def _():
+            for later in range(slots):
+                for copy in exchange(cot, c_all, cot_send, cot_recv, later):
+                    copy.start()
+
+        seq_c[...] = dot(x_all[:, at], cos_tab[slot]).astype(BF)
+        seq_s[...] = dot(x_all[:, at], sin_tab[slot]).astype(BF)
 
         @pl.loop(0, width // rows)
         def _(i):
@@ -314,9 +430,9 @@
             inv_one[:, col] = inverse
             hid[:, col] = (normed * vecs[1] + vecs[2]).astype(BF)
 
-    for k in others:
-        wp[k - 1].wait_recv()
-        ws[k].start()
+    for n, (copy, _, _) in enumerate(second_plane):
+        copy.wait_recv()
+        ws[len(first_plane) + n + 1].start()
 
     def first_matmul(r):
         @pl.loop(0, units // rows)
@@ -352,10 +468,11 @@
         result = normed * vecs[3, :, 0:1] + vecs[4, :, 0:1]
         x_all[:, col] = result.astype(BF)
         feature = lax.broadcasted_iota(jnp.int32, (width, cols), 0)
-        chosen = feature == labels[pl.ds(me, 1), col]
+        here = pl.ds(pl.multiple_of(me * chunk + i * cols, cols), cols)
+        chosen = feature == labels[here].reshape(1, cols)
         picked = jnp.sum(jnp.where(chosen, result, 0.0), axis=0, keepdims=True)
         soft = 1.0 / (1.0 + jnp.exp(-2.0 * picked))
-        hits[...] += jnp.where(mask[pl.ds(me, 1), col] == 1, soft, 0.0)
+        hits[...] += jnp.where(mask[here].reshape(1, cols) == 1, soft, 0.0)
 
     def send_back(source, target, send, recv, first, length):
         copies = []
@@ -380,6 +497,8 @@
     for copy in out_copies + [out_own]:
         copy.start()
 
+    cot_copies = sum((exchange(cot, c_all, cot_send, cot_recv, s) for s in range(slots)), [])
+    tok_copies = sum((exchange(tok, x_all, tok_send, tok_recv, s) for s in range(slots)), [])
     for copy in cot_copies:
         copy.wait_recv()
 
@@ -415,7 +534,7 @@
         )
 
     d_out = act.at[:, :, pl.ds(0, width)]
-    d_in = w_all.at[:, pl.ds(0, width)]
+    d_in = w_all.at[:, pl.ds(width, units)]
 
     def near_copy(x, r):
         source = (d_in, d_out)[x]
@@ -529,6 +648,23 @@
 
     far_out = add_near(1)
 
+    for copy in wz + [copy for copy, _, _ in first_plane + second_plane] + ws:
+        copy.wait_send()
+
+    @pl.when(jnp.logical_not(at_end))
+    def _():
+        pass_on(1, 2).wait_send()
+        pass_on(2, 3).wait_send()
+
+    @pl.loop(0, shards)
+    def _(r):
+        @pl.loop(0, width // rows)
+        def _(i):
+            row = pl.ds(pl.multiple_of(i * rows, rows), rows)
+            d_in[r, row] = dot(hid[row], slope[r], 1, 1).astype(BF)
+
+        near_copy(0, r).start()
+
     @pl.loop(0, chunk // cols)
     def _(i):
         col = pl.ds(pl.multiple_of(i * cols, cols), cols)
@@ -546,10 +682,10 @@
         acc[1] += lanes(upstream * normed)
         acc[2] += lanes(upstream)
 
+    far_in = add_near(0)
     dx_copies = []
     for slot in range(slots):
         at = pl.ds(slot * slot_length, slot_length)
-        which = bucket[me * slots + slot]
 
         @pl.loop(0, width // rows)
         def _(i):
@@ -560,7 +696,7 @@
         @pl.loop(0, width // rows)
         def _(i):
             row = pl.ds(pl.multiple_of(i * rows, rows), rows)
-            back = dot(seq_c[row], cos_tab[which]) + dot(seq_s[row], sin_tab[which])
+            back = dot(seq_c[row], cos_tab[slot]) + dot(seq_s[row], sin_tab[slot])
             c_all[row, at] = (n_two[row, at] + back).astype(BF)
 
         copies = send_back(
@@ -576,9 +712,10 @@
                 own_sem.at[1 + slot],
             )
         )
-        for copy in copies:
-            copy.start()
-        dx_copies += copies
+        dx_copies.append(copies)
+        if slot == 0:
+            for copy in copies:
+                copy.start()
 
     lane = lax.broadcasted_iota(jnp.int32, (width_local, 128), 1)
     total_hits = jnp.sum(hits[...], axis=1, keepdims=True)
@@ -604,20 +741,7 @@
         copy.start()
     sums_mp[me] = sums_own[0]
 
-    for copy in wz + wp + ws:
-        copy.wait_send()
-
-    @pl.loop(0, shards)
-    def _(r):
-        @pl.loop(0, width // rows)
-        def _(i):
-            row = pl.ds(pl.multiple_of(i * rows, rows), rows)
-            d_in[r, row] = dot(hid[row], slope[r], 1, 1).astype(BF)
-
-        near_copy(0, r).start()
-
     line_out = add_far(1, far_out)
-    far_in = add_near(0)
     for copy in mp_sums:
         copy.wait_recv()
     sums_mid[...] = sum(sums_mp[s] for s in range(shards))
@@ -628,13 +752,16 @@
     for copy in dp_sums:
         copy.start()
     sums_dp[group] = sums_mid[...]
+    line_from_in = add_far(0, far_in)
+    for copies in dx_copies[1:]:
+        for copy in copies:
+            copy.start()
     done_out, own_out = add_line(1, line_out)
-    line_from_in = add_far(0, far_in)
-    share_out = share(1, done_out, own_out)
     for copy in dp_sums:
         copy.wait_recv()
     sums[...] = sum(sums_dp[q] for q in range(groups))
     done_in, own_in = add_line(0, line_from_in)
+    share_out = share(1, done_out, own_out)
     share_in = share(0, done_in, own_in)
 
     @pl.loop(0, shards)
@@ -646,7 +773,7 @@
         copy.wait_send()
     for copy in far_out + far_in + line_out + line_from_in + done_out + done_in:
         copy.wait_send()
-    for copy in out_copies + [out_own] + dx_copies + [share_out, share_in]:
+    for copy in out_copies + [out_own] + sum(dx_copies, []) + [share_out, share_in]:
         copy.wait()
 
 
@@ -658,8 +785,6 @@
     slot_length = tokens // bucket.shape[0]
     slots = chunk // slot_length
     cols = min(256, slot_length)
-    cos_seq, sin_seq = seq_tables(slot_length)
-    cos_hid, sin_hid = (jnp.asarray(t, BF) for t in dft_pair(width))
     dma = pltpu.SemaphoreType.DMA
     chips = groups // 2
     split = 1 if width // 2 // chips % 16 == 0 else 2
@@ -672,15 +797,15 @@
             jax.ShapeDtypeStruct((2, width, units), BF),
             jax.ShapeDtypeStruct((8, units), F32),
         ],
-        in_specs=[ANY] * 5 + [SMEM, VMEM, VMEM] + [ANY] * 4,
+        in_specs=[ANY] * 5 + [SMEM, VMEM, VMEM],
         out_specs=[ANY, ANY, ANY, VMEM],
         scratch_shapes=[
             pltpu.VMEM((width, chunk), BF),
             pltpu.VMEM((width, chunk), BF),
             pltpu.VMEM((shards, 2 * width, units), BF),
             pltpu.VMEM((shards, 8, units), F32),
-            pltpu.VMEM((3, slot_length, slot_length), BF),
-            pltpu.VMEM((3, slot_length, slot_length), BF),
+            pltpu.VMEM((slots, slot_length, slot_length), BF),
+            pltpu.VMEM((slots, slot_length, slot_length), BF),
             pltpu.VMEM((width, width), BF),
             pltpu.VMEM((width, width), BF),
             pltpu.VMEM((width, chunk), F32),
@@ -707,11 +832,12 @@
             pltpu.VMEM((shards, 8, units), F32),
             pltpu.VMEM((8, units), F32),
             pltpu.VMEM((groups, 8, units), F32),
-            dma((7,)),
+            dma((3,)),
             dma((3 + slots,)),
         ]
-        + [dma((shards,))] * 8
-        + [dma((chips,))] * 4
+        + [dma((slots, shards))] * 4
+        + [dma((shards,))] * 4
+        + [dma((2 * chips,))] * 4
         + [dma((shards,))] * 2
         + [dma((slots, shards))] * 2
         + [dma((2, shards))] * 2
@@ -725,7 +851,7 @@
             collective_id=0, has_side_effects=True, vmem_limit_bytes=VMEM_LIMIT
         ),
         name="layer",
-    )(tok, cot, w_in, w_out, small, bucket, labels, mask, cos_seq, sin_seq, cos_hid, sin_hid)
+    )(tok, cot, w_in, w_out, small, bucket, labels, mask)
 
 
 def body(
@@ -760,8 +886,8 @@
         w_out,
         small,
         bucket,
-        labels.reshape(shards, -1),
-        mask.reshape(shards, -1),
+        labels,
+        mask,
     )
     d_tokens = d_x.astype(F32)
     grads = grads.astype(F32)

time: 241 us -> 212 us (0.88); the launches traced: 236 us -> 212 us
  Pallas kernels: 218 us -> 195 us
  local copies, waits for them, and re-layouts: 11.7 us -> 9.08 us
    pallas_call x1, Pallas kernels: 218 us -> 195 us  [layer_call(): pl.pallas_call(functools.partial(layer_kernel, shards, groups), out_shape...]
    reshape x2 -> x0, local copies, waits for them, and re-layouts: 2.66 us -> none  [the longest x1 1.33 us: body(): labels.reshape(shards, -1)]
where the time goes in v4:
time: 212 us
  Pallas kernels  195 us (92%)
  local copies, waits for them, and re-layouts  9.08 us (4%)
  other arithmetic  4.66 us (2%)
  between operations  2.46 us (1%)
    pallas_call x1, Pallas kernels, layer_call(): pl.pallas_call(functools.partial(layer_kernel, shards, groups), out_shape...  195 us

profile of v4, /device:TPU:0, one launch (start us, length us, event | category | flops | bytes accessed | tf_op | source)
XLA Modules:
  0.0 211.6 jit_solution(623790995999977451)
XLA Ops:
  0.6 0.8 stack.23
  1.4 0.7 broadcast_in_dim.3
  2.1 0.6 select_maximum_fusion.small
  2.7 195.4 %layer.1 = (bf16[192,4096]{1,0:T(8,128)(2,1)}, bf16[192,4096]{1,0:T(8,128)(2,1)}, bf16[2,768,768]{2,1,0:T(8,128)(2,1)}, f32[8,768]{1,0:T(8,128)}) custom-call(bf16[192,4096]{1,0:T(8,128)(2,1)} %tok.1, bf16[192,4096]{1,0:T(8,128)(2,1)} %cot.1, bf16[768,768]{1,0:T(8,128)(2,1)} %w_in.1, bf16[768,768]{1,0:T(8,128)(2,1)} %w_out.1, ...), custom_call_target="tpu_custom_call" | custom-call | tf_op jit(solution)/shard_map/layer/pallas_call | solution.py:792
  198.2 1.5 fusion
  199.6 1.3 slice_reduce_fusion
  201.0 1.2 slice.35
  202.8 2.0 convert_element_type.9
  204.8 0.0 copy-start.1
  204.8 2.5 %slice_bitcast_fusion = (f32[768,768]{1,0:T(8,128)}, f32[768,768]{1,0:T(8,128)}) fusion(f32[2,768,768]{2,1,0:T(8,128)S(1)} %convert_element_type.9), kind=kLoop, calls=%fused_computation | loop fusion | bytes 9437184 | tf_op jit(solution)/shard_map/squeeze | solution.py:896
  207.3 0.0 copy-done.1
  207.3 0.0 copy-start
  207.3 2.0 convert_element_type.8
  209.4 0.0 copy-done
  209.4 1.1 copy.25
Async XLA Ops:
  204.8 2.5 %copy-start.1 = (bf16[192,4096]{1,0:T(8,128)(2,1)S(1)}, bf16[192,4096]{1,0:T(8,128)(2,1)}, u32[]{:S(2)}) copy-start(bf16[192,4096]{1,0:T(8,128)(2,1)} %get-tuple-element.16) | copy-start | bytes 4718596
  207.3 2.0 copy-start

commit v5 on v4

--- a/solution.py
+++ b/solution.py
@@ -14,7 +14,7 @@
 ANY = pl.BlockSpec(memory_space=pl.ANY)
 VMEM = pl.BlockSpec(memory_space=pltpu.VMEM)
 SMEM = pl.BlockSpec(memory_space=pltpu.SMEM)
-VMEM_LIMIT = 66_000_000
+VMEM_LIMIT = 67_000_000
 
 
 def turns(phase):
@@ -104,6 +104,7 @@
     hits,
     near,
     far,
+    turn,
     part_low,
     line_in,
     own_part,
@@ -134,6 +135,8 @@
     near_recv,
     far_send,
     far_recv,
+    turn_send,
+    turn_recv,
     line_send,
     line_recv,
     done_send,
@@ -155,8 +158,9 @@
     slot_length = chunk // slots
     part = 2 * width // groups
     chips = groups // 2
-    rows = min(256, width)
-    cols = min(256, slot_length)
+    rows = width
+    some = width // 2
+    cols = slot_length
     ring = range(1, shards)
     others = range(1, chips)
 
@@ -175,8 +179,6 @@
     core = lax.rem(group, 2)
     sibling = {"dp": group + 1 - 2 * core}
     plane = [{"dp": lax.rem(group + q, groups)} for q in range(1, groups)]
-    greet([{"mp": mp_peer(d)} for d in ring] + plane)
-
     own_w = [
         pltpu.make_async_copy(w_in, w_all.at[0, :width], own_sem.at[0]),
         pltpu.make_async_copy(w_out, w_all.at[0, width:], own_sem.at[1]),
@@ -196,6 +198,8 @@
     for copy in own_w + loads:
         copy.start()
 
+    greet([{"mp": mp_peer(d)} for d in ring] + plane)
+
     def exchange(source, target, send, recv, slot, steps=(1, 2, 3)):
         copies = []
         for step in steps:
@@ -253,96 +257,84 @@
 
     near_step = jnp.where(at_end, 1, 3)
     far_step = jnp.where(at_end, 2, 1)
-    wz = [weight_copy(me, inward(far_step), 0), weight_copy(me, inward(near_step), 1)]
+    wz = [weight_copy(me, inward(near_step), 1), weight_copy(me, inward(far_step), 0)]
     for copy in wz:
         copy.start()
     for slot in range(slots):
         for copy in exchange(tok, x_all, tok_send, tok_recv, slot, (1, 2)):
             copy.start()
 
+        @pl.when(at_end)
+        def _():
+            for copy in exchange(tok, x_all, tok_send, tok_recv, slot, (3,)):
+                copy.start()
+
     def pass_on(step, send):
         return weight_copy(inward(step), inward(3), send)
-
-    @pl.when(jnp.logical_not(at_end))
-    def _():
-        for step, send in ((1, 2), (2, 3)):
-            weight_wait(lax.rem(step * inner + shards, shards))
-            pass_on(step, send).start()
-
-    for slot in range(slots):
-        for copy in exchange(tok, x_all, tok_send, tok_recv, slot, (3,)):
-            copy.start()
-
-    @pl.when(at_end)
-    def _():
-        for place in (1, 2, 3):
-            weight_wait(place)
-
-    @pl.when(jnp.logical_not(at_end))
-    def _():
-        weight_wait(lax.rem(3 * inner + shards, shards))
 
     side = math.isqrt(chips)
     chip_x, chip_y = lax.rem(group // 2, side), group // 2 // side
     halves = (pl.ds(0, units // 2), pl.ds(units // 2, units // 2))
+    arrival = [
+        lax.rem(step * inner + shards, shards)
+        for step in (1, jnp.where(at_end, 2, 3), jnp.where(at_end, 3, 2))
+    ]
 
     def at_chip(x, y):
         return (lax.rem(y + side, side) * side + lax.rem(x + side, side)) * 2 + core
 
-    def weights_of(who, across):
+    def weights_of(n, who, across):
         rows_of = pl.ds(pl.multiple_of(who * part, 16), part)
-        return w_all.at[pl.ds(1, shards - 1), rows_of, across]
-
-    def plane_copy(who, across, to, sem):
-        return remote(
-            weights_of(who, across), weights_of(who, across), wp_send.at[sem], wp_recv.at[sem], to
-        )
-
-    first_plane, second_plane = [], []
-    for h, across in enumerate(halves):
-        for a in range(1, side):
-            along = (a, 0) if h == 0 else (0, a)
-            first_plane.append(
-                (
-                    plane_copy(
-                        group,
-                        across,
-                        {"dp": at_chip(chip_x + along[0], chip_y + along[1])},
-                        h * chips + a,
-                    ),
-                    at_chip(chip_x - along[0], chip_y - along[1]),
-                    across,
-                )
-            )
-            for b in range(side):
-                source = at_chip(chip_x + b, chip_y) if h == 0 else at_chip(chip_x, chip_y + b)
-                to = at_chip(chip_x, chip_y + a) if h == 0 else at_chip(chip_x + a, chip_y)
-                back = (
-                    at_chip(chip_x + b, chip_y - a) if h == 0 else at_chip(chip_x - a, chip_y + b)
-                )
-                second_plane.append(
-                    (
-                        plane_copy(source, across, {"dp": to}, h * chips + side * a + b),
-                        back,
-                        across,
-                    )
-                )
-
-    def to_sibling(who, across, sem):
-        return remote(
-            weights_of(who, across),
-            weights_of(who, across),
-            ws_send.at[sem],
-            ws_recv.at[sem],
-            sibling,
-        )
-
-    ws = [to_sibling(group, pl.ds(0, units), 0)]
-    for n, (_, who, across) in enumerate(first_plane + second_plane):
-        ws.append(to_sibling(who, across, n + 1))
-    for copy, _, _ in first_plane:
-        copy.start()
-    ws[0].start()
+        return w_all.at[arrival[n], rows_of, across]
+
+    def plane_copy(n, who, across, to, sem):
+        at = weights_of(n, who, across)
+        return remote(at, at, wp_send.at[n, sem], wp_recv.at[n, sem], to)
+
+    def to_sibling(n, who, across, sem):
+        at = weights_of(n, who, across)
+        return remote(at, at, ws_send.at[n, sem], ws_recv.at[n, sem], sibling)
+
+    first_plane, second_plane = [[], [], []], [[], [], []]
+    first_ws, second_ws = [[], [], []], [[], [], []]
+    own_ws = [to_sibling(n, group, pl.ds(0, units), 0) for n in range(3)]
+    for n in range(3):
+        for h, across in enumerate(halves):
+            for p in range(1, side):
+                step_x, step_y = (p, 0) if h == 0 else (0, p)
+                to = {"dp": at_chip(chip_x + step_x, chip_y + step_y)}
+                first_plane[n].append(plane_copy(n, group, across, to, h * chips + p))
+                who = at_chip(chip_x - step_x, chip_y - step_y)
+                first_ws[n].append(to_sibling(n, who, across, 1 + h * (side - 1) + p - 1))
+                for q in range(side):
+                    if h == 0:
+                        source, to = at_chip(chip_x + q, chip_y), at_chip(chip_x, chip_y + p)
+                        who = at_chip(chip_x + q, chip_y - p)
+                    else:
+                        source, to = at_chip(chip_x, chip_y + q), at_chip(chip_x + p, chip_y)
+                        who = at_chip(chip_x - p, chip_y + q)
+                    sem = h * chips + side * p + q
+                    second_plane[n].append(plane_copy(n, source, across, {"dp": to}, sem))
+                    sem = 1 + 2 * (side - 1) + (h * (side - 1) + p - 1) * side + q
+                    second_ws[n].append(to_sibling(n, who, across, sem))
+
+    def line_arrived(n):
+        weight_wait(arrival[n])
+        for copy in first_plane[n]:
+            copy.start()
+        own_ws[n].start()
+
+    def first_arrived(n):
+        for copy in first_plane[n]:
+            copy.wait_recv()
+        for copy in second_plane[n] + first_ws[n]:
+            copy.start()
+
+    def second_arrived(n):
+        for copy in second_plane[n]:
+            copy.wait_recv()
+        for copy in second_ws[n]:
+            copy.start()
 
     turn_rows = min(64, slot_length)
 
@@ -380,6 +372,26 @@
         sin_tab[slot, row] = (sine * scale).astype(BF)
 
 
+    line_arrived(0)
+
+    @pl.when(jnp.logical_not(at_end))
+    def _():
+        pass_on(1, 2).start()
+
+    line_arrived(1)
+    first_arrived(0)
+    line_arrived(2)
+
+    @pl.when(jnp.logical_not(at_end))
+    def _():
+        pass_on(2, 3).start()
+        for slot in range(slots):
+            for copy in exchange(tok, x_all, tok_send, tok_recv, slot, (3,)):
+                copy.start()
+
+    first_arrived(1)
+    first_arrived(2)
+
     for copy in loads:
         copy.wait()
     for copy in small_copies:
@@ -392,20 +404,12 @@
             line = small_all[r, i + 1 : i + 2, : (width_local + 127) // 128 * 128]
             vecs[i, at] = jnp.broadcast_to(line, (128, line.shape[1])).T[:width_local]
 
-    for n, (copy, _, _) in enumerate(first_plane):
-        copy.wait_recv()
-        ws[n + 1].start()
-    for copy, _, _ in second_plane:
-        copy.start()
-
-    @pl.loop(0, slots)
-    def _(slot):
+    for slot in range(slots):
         at = pl.ds(pl.multiple_of(slot * slot_length, 128), slot_length)
         for copy in exchange(tok, x_all, tok_send, tok_recv, slot):
             copy.wait_recv()
 
-        @pl.when(slot == slots - 1)
-        def _():
+        if slot == slots - 1:
             for later in range(slots):
                 for copy in exchange(cot, c_all, cot_send, cot_recv, later):
                     copy.start()
@@ -430,14 +434,14 @@
             inv_one[:, col] = inverse
             hid[:, col] = (normed * vecs[1] + vecs[2]).astype(BF)
 
-    for n, (copy, _, _) in enumerate(second_plane):
-        copy.wait_recv()
-        ws[len(first_plane) + n + 1].start()
+        if slot == 0:
+            for n in range(3):
+                second_arrived(n)
 
     def first_matmul(r):
-        @pl.loop(0, units // rows)
+        @pl.loop(0, units // some)
         def _(i):
-            row = pl.ds(pl.multiple_of(i * rows, rows), rows)
+            row = pl.ds(pl.multiple_of(i * some, some), some)
             pre = dot(w_all[r, pl.ds(0, width), row], hid[...], 0, 0) + bias[r, row, 0:1]
             cdf = 0.5 + 0.5 * lax.erf(pre * (1.0 / math.sqrt(2.0)))
             pdf = jnp.exp(-0.5 * pre * pre) * (1.0 / math.sqrt(2.0 * math.pi))
@@ -445,6 +449,7 @@
             slope[r, row] = (cdf + pre * pdf).astype(BF)
 
     first_matmul(0)
+    ws = sum(first_ws + second_ws, own_ws)
     for copy in ws:
         copy.wait_recv()
     pl.loop(1, shards)(first_matmul)
@@ -494,13 +499,13 @@
 
     out_copies = send_back(x_all, out, out_send, out_recv, 0, chunk)
     out_own = pltpu.make_async_copy(x_all.at[my_rows], out.at[:, my_cols], own_sem.at[0])
-    for copy in out_copies + [out_own]:
-        copy.start()
 
     cot_copies = sum((exchange(cot, c_all, cot_send, cot_recv, s) for s in range(slots)), [])
     tok_copies = sum((exchange(tok, x_all, tok_send, tok_recv, s) for s in range(slots)), [])
     for copy in cot_copies:
         copy.wait_recv()
+    for copy in out_copies + [out_own]:
+        copy.start()
 
     @pl.loop(0, chunk // cols)
     def _(i):
@@ -525,8 +530,8 @@
     keep = pl.ds(pl.multiple_of(core * half, 16), half)
     give = pl.ds(pl.multiple_of((1 - core) * half, 16), half)
 
-    def piece(who):
-        chip = who // 2
+    def piece(x, y):
+        chip = lax.rem(y, side) * side + lax.rem(x, side)
         first = core * half + chip // split * piece_rows
         return (
             pl.ds(pl.multiple_of(first, 16), piece_rows),
@@ -542,68 +547,138 @@
             source.at[r, give], near.at[x, r], near_send.at[x, r], near_recv.at[x, r], sibling
         )
 
-    def add_near(x):
+    def far_copies(x, r):
+        copies = []
+        for p in range(1, side):
+            peer = at_chip(
+                chip_x + jnp.where(r < 2, p, 0), chip_y + jnp.where(r < 2, 0, p)
+            )
+            for q in range(side):
+                at, across = piece(
+                    chip_x + jnp.where(r < 2, p, q), chip_y + jnp.where(r < 2, q, p)
+                )
+                n = (p - 1) * side + q
+                copies.append(
+                    remote(
+                        (d_in, d_out)[x].at[r, at, across],
+                        far.at[x, n, r],
+                        far_send.at[x, n, r],
+                        far_recv.at[x, n, r],
+                        {"dp": peer},
+                    )
+                )
+        return copies
+
+    def turn_copies(x, r):
+        copies = []
+        for q in range(1, side):
+            to = chip_x + jnp.where(r < 2, 0, q), chip_y + jnp.where(r < 2, q, 0)
+            at, across = piece(*to)
+            copies.append(
+                remote(
+                    (d_in, d_out)[x].at[r, at, across],
+                    turn.at[x, q - 1, r],
+                    turn_send.at[x, q - 1, r],
+                    turn_recv.at[x, q - 1, r],
+                    {"dp": at_chip(*to)},
+                )
+            )
+        return copies
+
+    def add_near(x, r):
         source = (d_in, d_out)[x]
-
+        near_copy(x, r).wait_recv()
+        source[r, keep] = (source[r, keep].astype(F32) + near[x, r].astype(F32)).astype(BF)
+        for copy in far_copies(x, r):
+            copy.start()
+
+    def in_turn(i):
+        return lax.rem(i, 2) * 2 + i // 2
+
+    def reduce_blocks(x, compute):
+        @pl.loop(0, shards)
+        def _(i):
+            compute(in_turn(i))
+            near_copy(x, in_turn(i)).start()
+
+            @pl.when(i > 0)
+            def _():
+                add_near(x, in_turn(i - 1))
+
+        add_near(x, shards - 1)
+
+    def far_sum(x, r, q):
+        at, across = piece(
+            chip_x + jnp.where(r < 2, 0, q), chip_y + jnp.where(r < 2, q, 0)
+        )
+        total = (d_in, d_out)[x][r, at, across].astype(F32)
+        for p in range(1, side):
+            total += far[x, (p - 1) * side + q, r].astype(F32)
+        return total
+
+    def add_far(x):
+        @pl.loop(0, shards)
+        def _(i):
+            r = in_turn(i)
+            for copy in far_copies(x, r):
+                copy.wait_recv()
+            for q in range(1, side):
+                at, across = piece(
+                    chip_x + jnp.where(r < 2, 0, q), chip_y + jnp.where(r < 2, q, 0)
+                )
+                (d_in, d_out)[x][r, at, across] = far_sum(x, r, q).astype(BF)
+            for copy in turn_copies(x, r):
+                copy.start()
+
+    my_at, my_across = piece(chip_x, chip_y)
+
+    def add_turn(x):
         @pl.loop(0, shards)
         def _(r):
-            near_copy(x, r).wait_recv()
-            source[r, keep] = (source[r, keep].astype(F32) + near[x, r].astype(F32)).astype(BF)
-
-        copies = []
-        for k in others:
-            at, across = piece(dp_peer(k))
-            copies.append(
-                remote(
-                    source.at[:, at, across],
-                    far.at[x, k - 1],
-                    far_send.at[x, k],
-                    far_recv.at[x, k],
-                    {"dp": dp_peer(k)},
-                )
-            )
-        for copy in copies:
-            copy.start()
-        return copies
-
-    my_at, my_across = piece(group)
-
-    def add_far(x, copies):
-        source = (d_in, d_out)[x]
-        for copy in copies:
-            copy.wait_recv()
-
-        @pl.loop(0, shards)
-        def _(r):
-            total = source[r, my_at, my_across].astype(F32)
-            for k in others:
-                total += far[x, k - 1, r].astype(F32)
+            for copy in turn_copies(x, r):
+                copy.wait_recv()
+            total = far_sum(x, r, 0)
+            for q in range(1, side):
+                total += turn[x, q - 1, r].astype(F32)
             part_low[x, r] = total.astype(BF)
 
             @pl.when(r == 0)
             def _():
                 own_part[x] = total
 
-        copies = [
-            remote(
-                part_low.at[x, d],
-                line_in.at[x, d - 1],
-                line_send.at[x, d],
-                line_recv.at[x, d],
-                {"mp": mp_peer(d)},
-            )
-            for d in ring
-        ]
-        for copy in copies:
-            copy.start()
-        return copies
-
-    def add_line(x, copies):
-        for copy in copies:
-            copy.wait_recv()
-        total = own_part[x]
-        for d in ring:
-            total += line_in[x, d - 1].astype(F32)
+        @pl.when(at_end)
+        def _():
+            for step, place in ((2, 2), (3, 3), (1, 0)):
+                line_copy(x, step, inward(1), place).start()
+
+        @pl.when(jnp.logical_not(at_end))
+        def _():
+            line_copy(x, 3, inward(3), 0).start()
+
+    def line_copy(x, step, target, place):
+        return remote(
+            part_low.at[x, lax.rem(step * inner + shards, shards)],
+            line_in.at[x, place],
+            line_send.at[x, step],
+            line_recv.at[x, place],
+            {"mp": target},
+        )
+
+    def line_on(x):
+        @pl.when(jnp.logical_not(at_end))
+        def _():
+            for step in (1, 2):
+                line_copy(x, step, inward(step), step + 1).wait_recv()
+                r = lax.rem(step * inner + shards, shards)
+                part_low[x, r] = (
+                    part_low[x, r].astype(F32) + line_in[x, step + 1].astype(F32)
+                ).astype(BF)
+                line_copy(x, step, inward(step), 1).start()
+
+    def add_line(x):
+        for place in (0, 1):
+            line_copy(x, 1, inward(1), place).wait_recv()
+        total = own_part[x] + line_in[x, 0].astype(F32) + line_in[x, 1].astype(F32)
         done_low[x] = total.astype(BF)
         target = d_w.at[x, my_at, my_across]
         copies = [
@@ -627,28 +702,25 @@
         copy.start()
         return copy
 
-    @pl.loop(0, shards)
-    def _(r):
+    def second_weight(r):
         @pl.loop(0, units // rows)
         def _(i):
             row = pl.ds(pl.multiple_of(i * rows, rows), rows)
             d_out[r, row] = dot(act[r, row], grad[...], 1, 1).astype(BF)
 
-        near_copy(1, r).start()
+    reduce_blocks(1, second_weight)
 
     @pl.loop(0, shards)
     def _(r):
-        @pl.loop(0, units // rows)
+        @pl.loop(0, units // some)
         def _(i):
-            row = pl.ds(pl.multiple_of(i * rows, rows), rows)
-            grad_act = dot(w_all[r, pl.ds(pl.multiple_of(width + i * rows, rows), rows)], grad[...])
+            row = pl.ds(pl.multiple_of(i * some, some), some)
+            grad_act = dot(w_all[r, pl.ds(pl.multiple_of(width + i * some, some), some)], grad[...])
             low = (grad_act * slope[r, row].astype(F32)).astype(BF)
             slope[r, row] = low
             bias[r, row] = lanes(low.astype(F32))
 
-    far_out = add_near(1)
-
-    for copy in wz + [copy for copy, _, _ in first_plane + second_plane] + ws:
+    for copy in wz + sum(first_plane + second_plane, ws):
         copy.wait_send()
 
     @pl.when(jnp.logical_not(at_end))
@@ -656,14 +728,14 @@
         pass_on(1, 2).wait_send()
         pass_on(2, 3).wait_send()
 
-    @pl.loop(0, shards)
-    def _(r):
+    def first_weight(r):
         @pl.loop(0, width // rows)
         def _(i):
             row = pl.ds(pl.multiple_of(i * rows, rows), rows)
             d_in[r, row] = dot(hid[row], slope[r], 1, 1).astype(BF)
 
-        near_copy(0, r).start()
+    reduce_blocks(0, first_weight)
+    add_far(1)
 
     @pl.loop(0, chunk // cols)
     def _(i):
@@ -682,7 +754,6 @@
         acc[1] += lanes(upstream * normed)
         acc[2] += lanes(upstream)
 
-    far_in = add_near(0)
     dx_copies = []
     for slot in range(slots):
         at = pl.ds(slot * slot_length, slot_length)
@@ -716,6 +787,9 @@
         if slot == 0:
             for copy in copies:
                 copy.start()
+
+    add_turn(1)
+    add_far(0)
 
     lane = lax.broadcasted_iota(jnp.int32, (width_local, 128), 1)
     total_hits = jnp.sum(hits[...], axis=1, keepdims=True)
@@ -741,7 +815,13 @@
         copy.start()
     sums_mp[me] = sums_own[0]
 
-    line_out = add_far(1, far_out)
+    add_turn(0)
+    line_on(1)
+    line_on(0)
+    for copies in dx_copies[1:]:
+        for copy in copies:
+            copy.start()
+    done_out, own_out = add_line(1)
     for copy in mp_sums:
         copy.wait_recv()
     sums_mid[...] = sum(sums_mp[s] for s in range(shards))
@@ -752,26 +832,26 @@
     for copy in dp_sums:
         copy.start()
     sums_dp[group] = sums_mid[...]
-    line_from_in = add_far(0, far_in)
-    for copies in dx_copies[1:]:
-        for copy in copies:
-            copy.start()
-    done_out, own_out = add_line(1, line_out)
+    done_in, own_in = add_line(0)
+    share_out = share(1, done_out, own_out)
     for copy in dp_sums:
         copy.wait_recv()
     sums[...] = sum(sums_dp[q] for q in range(groups))
-    done_in, own_in = add_line(0, line_from_in)
-    share_out = share(1, done_out, own_out)
     share_in = share(0, done_in, own_in)
 
     @pl.loop(0, shards)
     def _(r):
-        near_copy(0, r).wait_send()
-        near_copy(1, r).wait_send()
+        for x in range(2):
+            for copy in [near_copy(x, r)] + far_copies(x, r) + turn_copies(x, r):
+                copy.wait_send()
+
+            @pl.when(r > 0)
+            def _():
+                line_copy(x, r, inward(1), 0).wait_send()
 
     for copy in small_copies + tok_copies + cot_copies + mp_sums + dp_sums:
         copy.wait_send()
-    for copy in far_out + far_in + line_out + line_from_in + done_out + done_in:
+    for copy in done_out + done_in:
         copy.wait_send()
     for copy in out_copies + [out_own] + sum(dx_copies, []) + [share_out, share_in]:
         copy.wait()
@@ -784,9 +864,10 @@
     chunk = tokens // shards
     slot_length = tokens // bucket.shape[0]
     slots = chunk // slot_length
-    cols = min(256, slot_length)
+    cols = slot_length
     dma = pltpu.SemaphoreType.DMA
     chips = groups // 2
+    side = math.isqrt(chips)
     split = 1 if width // 2 // chips % 16 == 0 else 2
     piece = (width // 2 * split // chips, width // split)
     return pl.pallas_call(
@@ -823,9 +904,10 @@
             pltpu.VMEM((5, width, 128), F32),
             pltpu.VMEM((1, cols), F32),
             pltpu.VMEM((2, shards, width // 2, width), BF),
-            pltpu.VMEM((2, chips - 1, shards) + piece, BF),
+            pltpu.VMEM((2, (side - 1) * side, shards) + piece, BF),
+            pltpu.VMEM((2, side - 1, shards) + piece, BF),
             pltpu.VMEM((2, shards) + piece, BF),
-            pltpu.VMEM((2, shards - 1) + piece, BF),
+            pltpu.VMEM((2, shards) + piece, BF),
             pltpu.VMEM((2,) + piece, F32),
             pltpu.VMEM((2,) + piece, BF),
             pltpu.VMEM((shards, 8, units), F32),
@@ -837,11 +919,12 @@
         ]
         + [dma((slots, shards))] * 4
         + [dma((shards,))] * 4
-        + [dma((2 * chips,))] * 4
+        + [dma((shards - 1, 2 * chips))] * 4
         + [dma((shards,))] * 2
         + [dma((slots, shards))] * 2
         + [dma((2, shards))] * 2
-        + [dma((2, chips))] * 2
+        + [dma((2, (side - 1) * side, shards))] * 2
+        + [dma((2, side - 1, shards))] * 2
         + [dma((2, shards))] * 2
         + [dma((2, chips))] * 2
         + [dma((2,))] * 2
@@ -852,6 +935,52 @@
         ),
         name="layer",
     )(tok, cot, w_in, w_out, small, bucket, labels, mask)
+
+
+def finish_kernel(scale, low_x, low_w, sums, d_tokens, d_w_in, d_w_out, hits, d_b_in, *rest):
+    d_tokens[...] = low_x[...].astype(F32)
+    d_w_in[...] = low_w[0].astype(F32)
+    d_w_out[...] = low_w[1].astype(F32)
+
+    @pl.when(pl.program_id(0) == 0)
+    def _():
+        d_b_in[...] = sums[0]
+        for i, target in enumerate(rest):
+            target[...] = sums[i + 1, : target.shape[0]]
+        hits[0, 0] = jnp.sum(sums[6:7, 0:1]) * scale
+
+
+def finish_call(scale, low_x, low_w, sums):
+    width_local, tokens = low_x.shape
+    _, width, units = low_w.shape
+    steps = 8
+    whole = lambda length: pl.BlockSpec((length,), lambda i: (0,))
+    return pl.pallas_call(
+        functools.partial(finish_kernel, scale),
+        grid=(steps,),
+        out_shape=[
+            jax.ShapeDtypeStruct((width_local, tokens), F32),
+            jax.ShapeDtypeStruct((width, units), F32),
+            jax.ShapeDtypeStruct((units, width), F32),
+            jax.ShapeDtypeStruct((1, 1), F32),
+            jax.ShapeDtypeStruct((units,), F32),
+        ]
+        + [jax.ShapeDtypeStruct((width_local,), F32)] * 5,
+        in_specs=[
+            pl.BlockSpec((width_local, tokens // steps), lambda i: (0, i)),
+            pl.BlockSpec((2, width // steps, units), lambda i: (0, i, 0)),
+            pl.BlockSpec((8, units), lambda i: (0, 0)),
+        ],
+        out_specs=[
+            pl.BlockSpec((width_local, tokens // steps), lambda i: (0, i)),
+            pl.BlockSpec((width // steps, units), lambda i: (i, 0)),
+            pl.BlockSpec((units // steps, width), lambda i: (i, 0)),
+            pl.BlockSpec(memory_space=pltpu.SMEM),
+            whole(units),
+        ]
+        + [whole(width_local)] * 5,
+        name="finish",
+    )(low_x, low_w, sums)
 
 
 def body(
@@ -889,11 +1018,10 @@
         labels,
         mask,
     )
-    d_tokens = d_x.astype(F32)
-    grads = grads.astype(F32)
-    rest = [sums[i + 1, :width_local] for i in range(5)]
-    score = sums[6, 0] * 8.0 / (token_count * groups)
-    return (output, d_tokens, grads[0], sums[0], grads[1], *rest, score)
+    d_tokens, d_w_in, d_w_out, hits, d_b_in, *rest = finish_call(
+        8.0 / (token_count * groups), d_x, grads, sums
+    )
+    return (output, d_tokens, d_w_in, d_b_in, d_w_out, *rest, hits[0, 0])
 
 
 def solution(mesh):

time: 212 us -> 197 us (0.929)
  local copies, waits for them, and re-layouts: 9.08 us -> 2.6 us
  other arithmetic: 4.66 us -> 0.62 us
    pallas_call x1, Pallas kernels: 195 us -> 185 us  [layer_call(): pl.pallas_call(functools.partial(layer_kernel, shards, groups), out_shape...]
    pallas_call x0 -> x1, Pallas kernels: none -> 7.71 us  [finish_call(): pl.pallas_call(functools.partial(finish_kernel, scale), grid=(steps,), ou...]
    convert_element_type x2 -> x0, other arithmetic: 4.05 us -> none  [the longest x1 2.02 us: body(): grads = grads.astype(F32)]
    slice x3 -> x0, local copies, waits for them, and re-layouts: 4 us -> none  [the longest x1 1.46 us: body(): rest = [sums[i + 1, :width_local] for i in range(5)]]
    squeeze x1 -> x0, local copies, waits for them, and re-layouts: 2.49 us -> none  [body(): return (output, d_tokens, grads[0], sums[0], grads[1], *rest, score)]
where the time goes in v5:
time: 197 us
  Pallas kernels  193 us (98%)
  local copies, waits for them, and re-layouts  2.6 us (1%)
    pallas_call x1, Pallas kernels, layer_call(): pl.pallas_call(functools.partial(layer_kernel, shards, groups), out_shape...  185 us
    pallas_call x1, Pallas kernels, finish_call(): pl.pallas_call(functools.partial(finish_kernel, scale), grid=(steps,), ou...  7.71 us

profile of v5, /device:TPU:0, one launch (start us, length us, event | category | flops | bytes accessed | tf_op | source)
XLA Modules:
  0.0 196.9 jit_solution(1397378153755442948)
XLA Ops:
  0.6 0.7 broadcast_in_dim.3
  1.3 0.8 stack.23
  2.1 0.6 select_maximum_fusion.small
  2.7 185.3 %layer.1 = (bf16[192,4096]{1,0:T(8,128)(2,1)}, bf16[192,4096]{1,0:T(8,128)(2,1)}, bf16[2,768,768]{2,1,0:T(8,128)(2,1)}, f32[8,768]{1,0:T(8,128)}) custom-call(bf16[192,4096]{1,0:T(8,128)(2,1)} %tok.1, bf16[192,4096]{1,0:T(8,128)(2,1)} %cot.1, bf16[768,768]{1,0:T(8,128)(2,1)} %w_in.1, bf16[768,768]{1,0:T(8,128)(2,1)} %w_out.1, ...), custom_call_target="tpu_custom_call" | custom-call | tf_op jit(solution)/shard_map/layer/pallas_call | solution.py:873
  188.0 0.0 copy-start
  188.0 7.7 %finish.1 = (f32[192,4096]{1,0:T(8,128)}, f32[768,768]{1,0:T(8,128)}, f32[768,768]{1,0:T(8,128)}, f32[1,1]{1,0:T(1,128)}, f32[768]{0:T(1024)}, /*index=5*/f32[19...) custom-call(bf16[192,4096]{1,0:T(8,128)(2,1)} %get-tuple-element.26.low_x, ...), custom_call_target="tpu_custom_call" | custom-call | tf_op jit(solution)/shard_map/finish/pallas_call | solution.py:958
  195.7 0.0 copy-done
  195.7 1.1 copy.25
Async XLA Ops:
  188.0 7.7 %copy-start = (bf16[192,4096]{1,0:T(8,128)(2,1)S(1)}, bf16[192,4096]{1,0:T(8,128)(2,1)}, u32[]{:S(2)}) copy-start(bf16[192,4096]{1,0:T(8,128)(2,1)} %get-tuple-element.50) | copy-start | bytes 4718596

commit v6 on v5

--- a/solution.py
+++ b/solution.py
@@ -147,6 +147,7 @@
     mp_recv,
     dp_send,
     dp_recv,
+    near_free,
 ):
     me = lax.axis_index("mp")
     group = lax.axis_index("dp")
@@ -497,19 +498,16 @@
             )
         return copies
 
-    out_copies = send_back(x_all, out, out_send, out_recv, 0, chunk)
+    out_copies = [
+        send_back(x_all, out, out_send.at[slot], out_recv.at[slot], slot * slot_length, slot_length)
+        for slot in range(slots)
+    ]
     out_own = pltpu.make_async_copy(x_all.at[my_rows], out.at[:, my_cols], own_sem.at[0])
 
     cot_copies = sum((exchange(cot, c_all, cot_send, cot_recv, s) for s in range(slots)), [])
     tok_copies = sum((exchange(tok, x_all, tok_send, tok_recv, s) for s in range(slots)), [])
-    for copy in cot_copies:
-        copy.wait_recv()
-    for copy in out_copies + [out_own]:
-        copy.start()
-
-    @pl.loop(0, chunk // cols)
-    def _(i):
-        col = pl.ds(pl.multiple_of(i * cols, cols), cols)
+    def norm_two_back(slot):
+        col = pl.ds(slot * slot_length, slot_length)
         upstream = c_all[:, col].astype(F32)
         normed = n_two[:, col]
         scaled = upstream * vecs[3, :, 0:1]
@@ -523,6 +521,79 @@
         acc[3] += lanes(upstream * normed)
         acc[4] += lanes(upstream)
 
+    def act_back(slot):
+        col = pl.ds(slot * slot_length, slot_length)
+
+        @pl.loop(0, shards)
+        def _(r):
+            grad_act = dot(w_all[r, pl.ds(width, units)], grad[:, col])
+            low = (grad_act * slope[r, :, col].astype(F32)).astype(BF)
+            slope[r, :, col] = low
+            if slot == 0:
+                bias[r] = lanes(low.astype(F32))
+            else:
+                bias[r] += lanes(low.astype(F32))
+
+    def hidden_back(slot):
+        col = pl.ds(slot * slot_length, slot_length)
+        total = dot(w_all[0, pl.ds(0, width)], slope[0, :, col])
+        for r in ring:
+            total += dot(w_all[r, pl.ds(0, width)], slope[r, :, col])
+        upstream = n_two[:, col] + total
+        normed = n_one[:, col]
+        scaled = upstream * vecs[1, :, 0:1]
+        first = jnp.mean(scaled, axis=0, keepdims=True)
+        both = jnp.mean(scaled * normed, axis=0, keepdims=True)
+        grad_one = inv_one[:, col] * (scaled - first - normed * both)
+        n_two[:, col] = grad_one
+        c_all[:, col] = grad_one.astype(BF)
+        acc[1] += lanes(upstream * normed)
+        acc[2] += lanes(upstream)
+
+    def transform_back(slot):
+        at = pl.ds(slot * slot_length, slot_length)
+
+        @pl.loop(0, width // rows)
+        def _(i):
+            row = pl.ds(pl.multiple_of(i * rows, rows), rows)
+            seq_c[row] = dot(cos_h[row], c_all[:, at]).astype(BF)
+            seq_s[row] = -dot(sin_h[row], c_all[:, at]).astype(BF)
+
+        @pl.loop(0, width // rows)
+        def _(i):
+            row = pl.ds(pl.multiple_of(i * rows, rows), rows)
+            back = dot(seq_c[row], cos_tab[slot]) + dot(seq_s[row], sin_tab[slot])
+            c_all[row, at] = (n_two[row, at] + back).astype(BF)
+
+        copies = send_back(
+            c_all, dx, dx_send.at[slot], dx_recv.at[slot], slot * slot_length, slot_length
+        )
+        copies.append(
+            pltpu.make_async_copy(
+                c_all.at[my_rows, at],
+                dx.at[
+                    :,
+                    pl.ds(pl.multiple_of(me * chunk + slot * slot_length, 128), slot_length),
+                ],
+                own_sem.at[1 + slot],
+            )
+        )
+        return copies
+
+    def cotangent_here(slot):
+        for copy in exchange(cot, c_all, cot_send, cot_recv, slot):
+            copy.wait_recv()
+        norm_two_back(slot)
+
+    cotangent_here(0)
+    act_back(0)
+    hidden_back(0)
+    dx_copies = [transform_back(0)]
+    for slot in range(1, slots):
+        cotangent_here(slot)
+    for copy in sum(out_copies, dx_copies[0] + [out_own]):
+        copy.start()
+
     half = width // 2
     split = 1 if half // chips % 16 == 0 else 2
     piece_rows = half * split // chips
@@ -544,7 +615,7 @@
     def near_copy(x, r):
         source = (d_in, d_out)[x]
         return remote(
-            source.at[r, give], near.at[x, r], near_send.at[x, r], near_recv.at[x, r], sibling
+            source.at[r, give], near.at[r], near_send.at[x, r], near_recv.at[x, r], sibling
         )
 
     def far_copies(x, r):
@@ -588,7 +659,7 @@
     def add_near(x, r):
         source = (d_in, d_out)[x]
         near_copy(x, r).wait_recv()
-        source[r, keep] = (source[r, keep].astype(F32) + near[x, r].astype(F32)).astype(BF)
+        source[r, keep] = (source[r, keep].astype(F32) + near[r].astype(F32)).astype(BF)
         for copy in far_copies(x, r):
             copy.start()
 
@@ -708,17 +779,13 @@
             row = pl.ds(pl.multiple_of(i * rows, rows), rows)
             d_out[r, row] = dot(act[r, row], grad[...], 1, 1).astype(BF)
 
+    second_slots = range(1, slots)
     reduce_blocks(1, second_weight)
-
-    @pl.loop(0, shards)
-    def _(r):
-        @pl.loop(0, units // some)
-        def _(i):
-            row = pl.ds(pl.multiple_of(i * some, some), some)
-            grad_act = dot(w_all[r, pl.ds(pl.multiple_of(width + i * some, some), some)], grad[...])
-            low = (grad_act * slope[r, row].astype(F32)).astype(BF)
-            slope[r, row] = low
-            bias[r, row] = lanes(low.astype(F32))
+    pl.semaphore_signal(
+        near_free, inc=1, device_id=sibling, device_id_type=pl.DeviceIdType.MESH
+    )
+    for slot in second_slots:
+        act_back(slot)
 
     for copy in wz + sum(first_plane + second_plane, ws):
         copy.wait_send()
@@ -734,60 +801,12 @@
             row = pl.ds(pl.multiple_of(i * rows, rows), rows)
             d_in[r, row] = dot(hid[row], slope[r], 1, 1).astype(BF)
 
+    pl.semaphore_wait(near_free, 1)
     reduce_blocks(0, first_weight)
     add_far(1)
-
-    @pl.loop(0, chunk // cols)
-    def _(i):
-        col = pl.ds(pl.multiple_of(i * cols, cols), cols)
-        total = dot(w_all[0, pl.ds(0, width)], slope[0, :, col])
-        for r in ring:
-            total += dot(w_all[r, pl.ds(0, width)], slope[r, :, col])
-        upstream = n_two[:, col] + total
-        normed = n_one[:, col]
-        scaled = upstream * vecs[1, :, 0:1]
-        first = jnp.mean(scaled, axis=0, keepdims=True)
-        both = jnp.mean(scaled * normed, axis=0, keepdims=True)
-        grad_one = inv_one[:, col] * (scaled - first - normed * both)
-        n_two[:, col] = grad_one
-        c_all[:, col] = grad_one.astype(BF)
-        acc[1] += lanes(upstream * normed)
-        acc[2] += lanes(upstream)
-
-    dx_copies = []
-    for slot in range(slots):
-        at = pl.ds(slot * slot_length, slot_length)
-
-        @pl.loop(0, width // rows)
-        def _(i):
-            row = pl.ds(pl.multiple_of(i * rows, rows), rows)
-            seq_c[row] = dot(cos_h[row], c_all[:, at]).astype(BF)
-            seq_s[row] = -dot(sin_h[row], c_all[:, at]).astype(BF)
-
-        @pl.loop(0, width // rows)
-        def _(i):
-            row = pl.ds(pl.multiple_of(i * rows, rows), rows)
-            back = dot(seq_c[row], cos_tab[slot]) + dot(seq_s[row], sin_tab[slot])
-            c_all[row, at] = (n_two[row, at] + back).astype(BF)
-
-        copies = send_back(
-            c_all, dx, dx_send.at[slot], dx_recv.at[slot], slot * slot_length, slot_length
-        )
-        copies.append(
-            pltpu.make_async_copy(
-                c_all.at[my_rows, at],
-                dx.at[
-                    :,
-                    pl.ds(pl.multiple_of(me * chunk + slot * slot_length, 128), slot_length),
-                ],
-                own_sem.at[1 + slot],
-            )
-        )
-        dx_copies.append(copies)
-        if slot == 0:
-            for copy in copies:
-                copy.start()
-
+    for slot in second_slots:
+        hidden_back(slot)
+        dx_copies.append(transform_back(slot))
     add_turn(1)
     add_far(0)
 
@@ -853,7 +872,7 @@
         copy.wait_send()
     for copy in done_out + done_in:
         copy.wait_send()
-    for copy in out_copies + [out_own] + sum(dx_copies, []) + [share_out, share_in]:
+    for copy in sum(out_copies + dx_copies, [out_own, share_out, share_in]):
         copy.wait()
 
 
@@ -903,7 +922,7 @@
             pltpu.VMEM((shards, units, 128), F32),
             pltpu.VMEM((5, width, 128), F32),
             pltpu.VMEM((1, cols), F32),
-            pltpu.VMEM((2, shards, width // 2, width), BF),
+            pltpu.VMEM((shards, width // 2, width), BF),
             pltpu.VMEM((2, (side - 1) * side, shards) + piece, BF),
             pltpu.VMEM((2, side - 1, shards) + piece, BF),
             pltpu.VMEM((2, shards) + piece, BF),
@@ -920,8 +939,7 @@
         + [dma((slots, shards))] * 4
         + [dma((shards,))] * 4
         + [dma((shards - 1, 2 * chips))] * 4
-        + [dma((shards,))] * 2
-        + [dma((slots, shards))] * 2
+        + [dma((slots, shards))] * 4
         + [dma((2, shards))] * 2
         + [dma((2, (side - 1) * side, shards))] * 2
         + [dma((2, side - 1, shards))] * 2
@@ -929,7 +947,8 @@
         + [dma((2, chips))] * 2
         + [dma((2,))] * 2
         + [dma((shards,))] * 2
-        + [dma((groups,))] * 2,
+        + [dma((groups,))] * 2
+        + [pltpu.SemaphoreType.REGULAR],
         compiler_params=pltpu.CompilerParams(
             collective_id=0, has_side_effects=True, vmem_limit_bytes=VMEM_LIMIT
         ),

time: 197 us -> 192 us (0.975)
  Pallas kernels: 193 us -> 187 us
    pallas_call x1, Pallas kernels: 185 us -> 180 us  [layer_call(): pl.pallas_call(functools.partial(layer_kernel, shards, groups), out_shape...]
where the time goes in v6:
time: 192 us; the launch traced here: 191 us
  Pallas kernels  187 us (97%)
  local copies, waits for them, and re-layouts  2.6 us (1%)
    pallas_call x1, Pallas kernels, layer_call(): pl.pallas_call(functools.partial(layer_kernel, shards, groups), out_shape...  180 us
    pallas_call x1, Pallas kernels, finish_call(): pl.pallas_call(functools.partial(finish_kernel, scale), grid=(steps,), ou...  7.71 us

profile of v6, /device:TPU:0, one launch (start us, length us, event | category | flops | bytes accessed | tf_op | source)
XLA Modules:
  0.0 191.4 jit_solution(17516646836710905621)
XLA Ops:
  0.6 0.7 broadcast_in_dim.3
  1.3 0.8 stack.23
  2.1 0.6 select_maximum_fusion.small
  2.7 179.8 %layer.1 = (bf16[192,4096]{1,0:T(8,128)(2,1)}, bf16[192,4096]{1,0:T(8,128)(2,1)}, bf16[2,768,768]{2,1,0:T(8,128)(2,1)}, f32[8,768]{1,0:T(8,128)}) custom-call(bf16[192,4096]{1,0:T(8,128)(2,1)} %tok.1, bf16[192,4096]{1,0:T(8,128)(2,1)} %cot.1, bf16[768,768]{1,0:T(8,128)(2,1)} %w_in.1, bf16[768,768]{1,0:T(8,128)(2,1)} %w_out.1, ...), custom_call_target="tpu_custom_call" | custom-call | tf_op jit(solution)/shard_map/layer/pallas_call | solution.py:892
  182.5 0.0 copy-start
  182.5 7.7 %finish.1 = (f32[192,4096]{1,0:T(8,128)}, f32[768,768]{1,0:T(8,128)}, f32[768,768]{1,0:T(8,128)}, f32[1,1]{1,0:T(1,128)}, f32[768]{0:T(1024)}, /*index=5*/f32[19...) custom-call(bf16[192,4096]{1,0:T(8,128)(2,1)} %get-tuple-element.26.low_x, ...), custom_call_target="tpu_custom_call" | custom-call | tf_op jit(solution)/shard_map/finish/pallas_call | solution.py:977
  190.2 0.0 copy-done
  190.2 1.1 copy.25
Async XLA Ops:
  182.5 7.7 %copy-start = (bf16[192,4096]{1,0:T(8,128)(2,1)S(1)}, bf16[192,4096]{1,0:T(8,128)(2,1)}, u32[]{:S(2)}) copy-start(bf16[192,4096]{1,0:T(8,128)(2,1)} %get-tuple-element.50) | copy-start | bytes 4718596

commit v7 on v6

--- a/solution.py
+++ b/solution.py
@@ -72,7 +72,7 @@
     cot,
     w_in,
     w_out,
-    small,
+    vectors,
     bucket,
     labels,
     mask,
@@ -190,7 +190,6 @@
         pltpu.make_async_copy(source, target, load_sem.at[i])
         for i, (source, target) in enumerate(
             [
-                (small, small_all.at[0]),
                 (tok.at[:, my_cols], x_all.at[my_rows]),
                 (cot.at[:, my_cols], c_all.at[my_rows]),
             ]
@@ -199,6 +198,10 @@
     for copy in own_w + loads:
         copy.start()
 
+    small_all[0] = jnp.zeros((8, units), F32)
+    for i, vector in enumerate(vectors):
+        length = vector.shape[0]
+        small_all[0, i : i + 1, :length] = vector[...].reshape(1, length)
     greet([{"mp": mp_peer(d)} for d in ring] + plane)
 
     def exchange(source, target, send, recv, slot, steps=(1, 2, 3)):
@@ -222,7 +225,7 @@
 
     small_copies = [
         remote(
-            small,
+            small_all.at[0],
             small_all.at[shards - d],
             small_send.at[d],
             small_recv.at[d],
@@ -876,7 +879,7 @@
         copy.wait()
 
 
-def layer_call(shards, groups, tok, cot, w_in, w_out, small, bucket, labels, mask):
+def layer_call(shards, groups, tok, cot, w_in, w_out, vectors, bucket, labels, mask):
     width_local, tokens = tok.shape
     width = width_local * shards
     units = w_in.shape[1]
@@ -897,7 +900,7 @@
             jax.ShapeDtypeStruct((2, width, units), BF),
             jax.ShapeDtypeStruct((8, units), F32),
         ],
-        in_specs=[ANY] * 5 + [SMEM, VMEM, VMEM],
+        in_specs=[ANY] * 4 + [[VMEM] * 6, SMEM, VMEM, VMEM],
         out_specs=[ANY, ANY, ANY, VMEM],
         scratch_shapes=[
             pltpu.VMEM((width, chunk), BF),
@@ -933,7 +936,7 @@
             pltpu.VMEM((shards, 8, units), F32),
             pltpu.VMEM((8, units), F32),
             pltpu.VMEM((groups, 8, units), F32),
-            dma((3,)),
+            dma((2,)),
             dma((3 + slots,)),
         ]
         + [dma((slots, shards))] * 4
@@ -953,7 +956,7 @@
             collective_id=0, has_side_effects=True, vmem_limit_bytes=VMEM_LIMIT
         ),
         name="layer",
-    )(tok, cot, w_in, w_out, small, bucket, labels, mask)
+    )(tok, cot, w_in, w_out, vectors, bucket, labels, mask)
 
 
 def finish_kernel(scale, low_x, low_w, sums, d_tokens, d_w_in, d_w_out, hits, d_b_in, *rest):
@@ -972,7 +975,7 @@
 def finish_call(scale, low_x, low_w, sums):
     width_local, tokens = low_x.shape
     _, width, units = low_w.shape
-    steps = 8
+    steps = 4
     whole = lambda length: pl.BlockSpec((length,), lambda i: (0,))
     return pl.pallas_call(
         functools.partial(finish_kernel, scale),
@@ -1020,11 +1023,7 @@
     shards = lax.axis_size("mp")
     groups = lax.axis_size("dp")
     width_local, token_count = tokens.shape
-    units = w_in.shape[1]
-    vectors = jnp.stack([b_out, gain_one, shift_one, gain_two, shift_two])
-    small = jnp.concatenate(
-        [b_in[None, :], jnp.pad(vectors, ((0, 2), (0, units - width_local)))], axis=0
-    )
+    vectors = [b_in, b_out, gain_one, shift_one, gain_two, shift_two]
     output, d_x, grads, sums = layer_call(
         shards,
         groups,
@@ -1032,7 +1031,7 @@
         cotangent,
         w_in,
         w_out,
-        small,
+        vectors,
         bucket,
         labels,
         mask,

time: 192 us -> 188 us (0.979)
  no operation moved by 1% of the time
where the time goes in v7:
time: 188 us; the launch traced here: 187 us
  Pallas kernels  186 us (99%)
    pallas_call x1, Pallas kernels, layer_call(): pl.pallas_call(functools.partial(layer_kernel, shards, groups), out_shape...  180 us
    pallas_call x1, Pallas kernels, finish_call(): pl.pallas_call(functools.partial(finish_kernel, scale), grid=(steps,), ou...  5.89 us

profile of v7, /device:TPU:0, one launch (start us, length us, event | category | flops | bytes accessed | tf_op | source)
XLA Modules:
  0.0 187.3 jit_solution(11426129332190827876)
XLA Ops:
  0.6 179.6 %layer.1 = (bf16[192,4096]{1,0:T(8,128)(2,1)}, bf16[192,4096]{1,0:T(8,128)(2,1)}, bf16[2,768,768]{2,1,0:T(8,128)(2,1)}, f32[8,768]{1,0:T(8,128)}) custom-call(bf16[192,4096]{1,0:T(8,128)(2,1)} %tok.1, bf16[192,4096]{1,0:T(8,128)(2,1)} %cot.1, bf16[768,768]{1,0:T(8,128)(2,1)} %w_in.1, bf16[768,768]{1,0:T(8,128)(2,1)} %w_out.1, f32[768]{0:T(1024)} %vectors_0_.1, ...), custom_call_target="tpu_custom_call" | custom-call | tf_op jit(solution)/shard_map/layer/pallas_call | solution.py:895
  180.3 0.0 copy-start
  180.3 5.9 %finish.1 = (f32[192,4096]{1,0:T(8,128)}, f32[768,768]{1,0:T(8,128)}, f32[768,768]{1,0:T(8,128)}, f32[1,1]{1,0:T(1,128)}, f32[768]{0:T(1024)}, /*index=5*/f32[19...) custom-call(bf16[192,4096]{1,0:T(8,128)(2,1)} %get-tuple-element.26.low_x, ...), custom_call_target="tpu_custom_call" | custom-call | tf_op jit(solution)/shard_map/finish/pallas_call | solution.py:980
  186.2 0.0 copy-done
  186.2 1.1 copy.25
Async XLA Ops:
  180.3 5.9 %copy-start = (bf16[192,4096]{1,0:T(8,128)(2,1)S(1)}, bf16[192,4096]{1,0:T(8,128)(2,1)}, u32[]{:S(2)}) copy-start(bf16[192,4096]{1,0:T(8,128)(2,1)} %get-tuple-element.50) | copy-start | bytes 4718596

commit v8 on v7

--- a/solution.py
+++ b/solution.py
@@ -809,8 +809,9 @@
     add_far(1)
     for slot in second_slots:
         hidden_back(slot)
+        if slot == 1:
+            add_turn(1)
         dx_copies.append(transform_back(slot))
-    add_turn(1)
     add_far(0)
 
     lane = lax.broadcasted_iota(jnp.int32, (width_local, 128), 1)

time: 188 us -> 188 us (level)
  no operation moved by 1% of the time
where the time goes in v8:
time: 188 us; the launch traced here: 187 us
  Pallas kernels  186 us (99%)
    pallas_call x1, Pallas kernels, layer_call(): pl.pallas_call(functools.partial(layer_kernel, shards, groups), out_shape...  180 us
    pallas_call x1, Pallas kernels, finish_call(): pl.pallas_call(functools.partial(finish_kernel, scale), grid=(steps,), ou...  5.89 us

profile of v8, /device:TPU:0, one launch (start us, length us, event | category | flops | bytes accessed | tf_op | source)
XLA Modules:
  0.0 187.3 jit_solution(11404290217084277672)
XLA Ops:
  0.6 179.6 %layer.1 = (bf16[192,4096]{1,0:T(8,128)(2,1)}, bf16[192,4096]{1,0:T(8,128)(2,1)}, bf16[2,768,768]{2,1,0:T(8,128)(2,1)}, f32[8,768]{1,0:T(8,128)}) custom-call(bf16[192,4096]{1,0:T(8,128)(2,1)} %tok.1, bf16[192,4096]{1,0:T(8,128)(2,1)} %cot.1, bf16[768,768]{1,0:T(8,128)(2,1)} %w_in.1, bf16[768,768]{1,0:T(8,128)(2,1)} %w_out.1, f32[768]{0:T(1024)} %vectors_0_.1, ...), custom_call_target="tpu_custom_call" | custom-call | tf_op jit(solution)/shard_map/layer/pallas_call | solution.py:896
  180.3 0.0 copy-start
  180.3 5.9 %finish.1 = (f32[192,4096]{1,0:T(8,128)}, f32[768,768]{1,0:T(8,128)}, f32[768,768]{1,0:T(8,128)}, f32[1,1]{1,0:T(1,128)}, f32[768]{0:T(1024)}, /*index=5*/f32[19...) custom-call(bf16[192,4096]{1,0:T(8,128)(2,1)} %get-tuple-element.26.low_x, ...), custom_call_target="tpu_custom_call" | custom-call | tf_op jit(solution)/shard_map/finish/pallas_call | solution.py:981
  186.2 0.0 copy-done
  186.2 1.1 copy.25
Async XLA Ops:
  180.3 5.9 %copy-start = (bf16[192,4096]{1,0:T(8,128)(2,1)S(1)}, bf16[192,4096]{1,0:T(8,128)(2,1)}, u32[]{:S(2)}) copy-start(bf16[192,4096]{1,0:T(8,128)(2,1)} %get-tuple-element.50) | copy-start | bytes 4718596
